TPU v7x, 32 devices: a whole 2x2x4 slice. The times are simulated.
32 devices in a mesh: dp: 4 (over z), seq: 8 (over y, x, core).
Axes of the slice: x: 2, y: 2, z: 4, core: 2. Of those that a mesh axis runs over, the one named last changes fastest.
Arguments:
- tokens: bfloat16 [8, 1024, 2048], P('dp', 'seq'), may hold values from -6 to 6
- cotangent: bfloat16 [8, 1024, 2048], P('dp', 'seq'), may hold values from -6 to 6
- lengths: int32 [8], replicated, may hold values from 1 to 1024, 6656 in all
- owner_order: int32 [8], replicated, may hold values from 0 to 7, each once
- first_gain: bfloat16 [2048], P(('dp', 'seq')), may hold values from 0.5 to 1.5
- first_bias: bfloat16 [2048], P(('dp', 'seq')), may hold values from -3 to 3
- w_query: bfloat16 [2048, 2048], P(('dp', 'seq')), may hold values from -0.125 to 0.125
- b_query: bfloat16 [2048], P(('dp', 'seq')), may hold values from -3 to 3
- w_keyval: bfloat16 [2048, 256], P(('dp', 'seq')), may hold values from -0.25 to 0.25
- b_value: bfloat16 [128], P(('dp', 'seq')), may hold values from -3 to 3
- w_out: bfloat16 [2048, 2048], P(('dp', 'seq')), may hold values from -1 to 1
- b_out: bfloat16 [2048], P(('dp', 'seq')), may hold values from -3 to 3
- second_gain: bfloat16 [2048], P(('dp', 'seq')), may hold values from 0.5 to 1.5
- second_bias: bfloat16 [2048], P(('dp', 'seq')), may hold values from -3 to 3
- w_expand: bfloat16 [2048, 8192], P(('dp', 'seq')), may hold values from -0.125 to 0.125
- b_expand: bfloat16 [8192], P(('dp', 'seq')), may hold values from -3 to 3
- w_contract: bfloat16 [8192, 2048], P(('dp', 'seq')), may hold values from -0.0625 to 0.0625
- b_contract: bfloat16 [2048], P(('dp', 'seq')), may hold values from -3 to 3
Outputs:
- result: bfloat16 [8, 1024, 2048], P('dp', 'seq')
- grad_tokens: float32 [8, 1024, 2048], P('dp', 'seq')
- grad_first_gain: float32 [2048], P(('dp', 'seq'))
- grad_first_bias: float32 [2048], P(('dp', 'seq'))
- grad_w_query: float32 [2048, 2048], P(('dp', 'seq'))
- grad_b_query: float32 [2048], P(('dp', 'seq'))
- grad_w_keyval: float32 [2048, 256], P(('dp', 'seq'))
- grad_b_value: float32 [128], P(('dp', 'seq'))
- grad_w_out: float32 [2048, 2048], P(('dp', 'seq'))
- grad_b_out: float32 [2048], P(('dp', 'seq'))
- grad_second_gain: float32 [2048], P(('dp', 'seq'))
- grad_second_bias: float32 [2048], P(('dp', 'seq'))
- grad_w_expand: float32 [2048, 8192], P(('dp', 'seq'))
- grad_b_expand: float32 [8192], P(('dp', 'seq'))
- grad_w_contract: float32 [8192, 2048], P(('dp', 'seq'))
- grad_b_contract: float32 [2048], P(('dp', 'seq'))
Inputs may be any that keep to these rules, and one draw needn't show every extreme that they name: `lengths`: each sequence has 1 to 1024 valid tokens, 6656 in all; at least one has 1024. `owner_order`: each sequence number appears exactly once.
All inputs are finite; a program needn't handle non-finite values.
Results may differ from a plain program's by a relative error of at most 0.011.
The roundings to bfloat16 on the way count: a program that leaves them out, or rounds other values in their place, can miss the bound.
Values may be sent and summed in bfloat16 or wider, within the bound.
No kernel may reach another device: no remote copies, remote signals or barrier semaphores. Data moves between devices by JAX's collectives and lax.ppermute only.
A program may use at most 384 MiB of HBM per device.

v0:
```python
import math

import jax
import jax.numpy as jnp
from jax import lax
from jax.sharding import PartitionSpec as P

norm_eps = 1e-05


def norm_rows(hidden):
    mean = jnp.mean(hidden, axis=1, keepdims=True)
    centered = hidden - mean
    inv_std = lax.rsqrt(jnp.mean(centered * centered, axis=1, keepdims=True) + norm_eps)
    return (centered * inv_std, inv_std)


def norm_back(grad_normed, normed, inv_std):
    mean_grad = jnp.mean(grad_normed, axis=1, keepdims=True)
    mean_proj = jnp.mean(grad_normed * normed, axis=1, keepdims=True)
    return inv_std * (grad_normed - mean_grad - normed * mean_proj)


def valid_rows(length, first, block):
    place = first + jnp.arange(block, dtype=jnp.int32)
    return (place < length).astype(jnp.float32)[:, None]


def causal_mask(length, first, block, heads, span):
    row_place = first + jnp.arange(block * heads, dtype=jnp.int32) // heads
    key_place = jnp.arange(span, dtype=jnp.int32)
    return (key_place[None, :] <= row_place[:, None]) & (key_place[None, :] < length)


def masked_scores(query_rows, keyval_all, mask):
    head_size = query_rows.shape[1]
    raw = jnp.einsum(
        "rd,kd->rk", query_rows, keyval_all[:, :head_size], preferred_element_type=jnp.float32
    )
    return jnp.where(mask, raw * (1.0 / math.sqrt(head_size)), -1e30)


def column_sum(values):
    return jnp.sum(values.astype(jnp.float32), axis=0)


def outer_sum(left, right):
    return jnp.einsum("rd,re->de", left, right, preferred_element_type=jnp.float32)


def first_half(hidden, attention_set):
    (
        gain_one,
        bias_one,
        query_weight,
        query_bias,
        keyval_weight,
        value_bias,
        out_weight,
        out_bias,
    ) = attention_set
    normed, inv_std = norm_rows(hidden)
    normed_in = (normed * gain_one.astype(jnp.float32) + bias_one.astype(jnp.float32)).astype(
        jnp.bfloat16
    )
    query = (
        jnp.dot(normed_in, query_weight, preferred_element_type=jnp.float32)
        + query_bias.astype(jnp.float32)
    ).astype(jnp.bfloat16)
    value_part = value_bias.astype(jnp.float32)
    keyval_bias = jnp.concatenate([jnp.zeros_like(value_part), value_part])
    keyval = (
        jnp.dot(normed_in, keyval_weight, preferred_element_type=jnp.float32) + keyval_bias
    ).astype(jnp.bfloat16)
    return (normed, inv_std, normed_in, query, keyval)


def second_half(hidden, front, keyval_all, attention_set, feedforward_set, length, first):
    normed, inv_std, normed_in, query, keyval = front
    out_weight = attention_set[6]
    out_bias = attention_set[7]
    gain_two, bias_two, expand_weight, expand_bias, contract_weight, contract_bias = feedforward_set
    head_size = attention_set[5].shape[0]
    block = query.shape[0]
    query_rows = query.reshape(-1, head_size)
    heads = query_rows.shape[0] // block
    mask = causal_mask(length, first, block, heads, keyval_all.shape[0])
    masked = masked_scores(query_rows, keyval_all, mask)
    top = jnp.max(masked, axis=1, keepdims=True)
    unnormed = jnp.exp(masked - top)
    total = jnp.sum(unnormed, axis=1, keepdims=True)
    probs = unnormed / total
    log_total = top + jnp.log(total)
    mixed = jnp.dot(
        probs.astype(jnp.bfloat16), keyval_all[:, head_size:], preferred_element_type=jnp.float32
    )
    mixed = mixed.reshape(query.shape).astype(jnp.bfloat16)
    resid = (
        hidden
        + jnp.dot(mixed, out_weight, preferred_element_type=jnp.float32)
        + out_bias.astype(jnp.float32)
    )
    normed2, inv_std2 = norm_rows(resid)
    normed2_in = (normed2 * gain_two.astype(jnp.float32) + bias_two.astype(jnp.float32)).astype(
        jnp.bfloat16
    )
    preact = jnp.dot(
        normed2_in, expand_weight, preferred_element_type=jnp.float32
    ) + expand_bias.astype(jnp.float32)
    active = jax.nn.gelu(preact, approximate=True).astype(jnp.bfloat16)
    output = jnp.dot(
        active, contract_weight, preferred_element_type=jnp.float32
    ) + contract_bias.astype(jnp.float32)
    valid = valid_rows(length, first, block)
    result = (valid * (resid + output)).astype(jnp.bfloat16)
    stash = (
        normed,
        inv_std,
        normed_in,
        query,
        keyval_all,
        log_total,
        mixed,
        normed2,
        inv_std2,
        normed2_in,
        preact,
        active,
    )
    return (result, stash)


def run_backward(grad_out, stash, attention_set, feedforward_set, length, first):
    (
        normed,
        inv_std,
        normed_in,
        query,
        keyval_all,
        log_total,
        mixed,
        normed2,
        inv_std2,
        normed2_in,
        preact,
        active,
    ) = stash
    (
        gain_one,
        bias_one,
        query_weight,
        query_bias,
        keyval_weight,
        value_bias,
        out_weight,
        out_bias,
    ) = attention_set
    gain_two, bias_two, expand_weight, expand_bias, contract_weight, contract_bias = feedforward_set
    head_size = value_bias.shape[0]
    block = query.shape[0]
    valid = valid_rows(length, first, block)
    grad_y = grad_out.astype(jnp.float32) * valid
    grad_m = grad_y.astype(jnp.bfloat16)
    grad_active = jnp.einsum(
        "rd,fd->rf", grad_m, contract_weight, preferred_element_type=jnp.float32
    )
    unused_value, gelu_back = jax.vjp(lambda v: jax.nn.gelu(v, approximate=True), preact)
    grad_pre = gelu_back(grad_active)[0].astype(jnp.bfloat16)
    grad_c = jnp.einsum("rf,df->rd", grad_pre, expand_weight, preferred_element_type=jnp.float32)
    grad_resid = grad_y + norm_back(grad_c * gain_two.astype(jnp.float32), normed2, inv_std2)
    grad_branch = grad_resid.astype(jnp.bfloat16)
    grad_mixed = jnp.einsum(
        "rd,ed->re", grad_branch, out_weight, preferred_element_type=jnp.float32
    ).astype(jnp.bfloat16)
    query_rows = query.reshape(-1, head_size)
    grad_rows = grad_mixed.reshape(-1, head_size)
    heads = query_rows.shape[0] // block
    mask = causal_mask(length, first, block, heads, keyval_all.shape[0])
    probs = jnp.exp(masked_scores(query_rows, keyval_all, mask) - log_total)
    grad_probs = jnp.einsum(
        "rd,kd->rk", grad_rows, keyval_all[:, head_size:], preferred_element_type=jnp.float32
    )
    grad_values = jnp.einsum(
        "rk,rd->kd", probs.astype(jnp.bfloat16), grad_rows, preferred_element_type=jnp.float32
    )
    inner = jnp.sum(probs * grad_probs, axis=1, keepdims=True)
    grad_scores = (probs * (grad_probs - inner)).astype(jnp.bfloat16)
    scale = 1.0 / math.sqrt(head_size)
    grad_query = (
        jnp.dot(grad_scores, keyval_all[:, :head_size], preferred_element_type=jnp.float32) * scale
    )
    grad_query = grad_query.reshape(query.shape).astype(jnp.bfloat16)
    grad_keys = (
        jnp.einsum("rk,rd->kd", grad_scores, query_rows, preferred_element_type=jnp.float32) * scale
    )
    grad_keyval = lax.psum_scatter(
        jnp.concatenate([grad_keys, grad_values], axis=1), "seq", scatter_dimension=0, tiled=True
    ).astype(jnp.bfloat16)
    grad_in = jnp.einsum("rd,ed->re", grad_query, query_weight, preferred_element_type=jnp.float32)
    grad_in = grad_in + jnp.einsum(
        "rc,ec->re", grad_keyval, keyval_weight, preferred_element_type=jnp.float32
    )
    grad_hidden = grad_resid + norm_back(grad_in * gain_one.astype(jnp.float32), normed, inv_std)
    factors = (
        normed_in,
        grad_query,
        grad_keyval,
        mixed,
        grad_branch,
        normed2_in,
        grad_pre,
        active,
        grad_m,
    )
    smalls = (
        jnp.sum(grad_in * normed, axis=0),
        jnp.sum(grad_in, axis=0),
        jnp.sum(grad_c * normed2, axis=0),
        jnp.sum(grad_c, axis=0),
    )
    return (grad_hidden, factors, smalls)


def shards(
    tokens,
    cotangent,
    lengths,
    owner_order,
    first_gain,
    first_bias,
    w_query,
    b_query,
    w_keyval,
    b_value,
    w_out,
    b_out,
    second_gain,
    second_bias,
    w_expand,
    b_expand,
    w_contract,
    b_contract,
):
    micro = tokens.shape[0]
    block = tokens.shape[1]
    owner = lax.axis_index("dp")
    first = lax.axis_index("seq") * block
    seq_ids = jnp.arange(lengths.shape[0], dtype=jnp.int32)
    wanted = lax.dynamic_slice_in_dim(owner_order, owner * micro, micro)
    own_length = jnp.sum(
        jnp.where(seq_ids[None, :] == wanted[:, None], lengths[None, :], 0), axis=1
    )
    piece = lax.all_gather(tokens, "dp", axis=0, tiled=True)
    piece_ids = jnp.arange(piece.shape[0], dtype=jnp.int32)
    select = (piece_ids[None, :] == wanted[:, None]).astype(jnp.bfloat16)
    picked = jnp.einsum("mn,nbd->mbd", select, piece, preferred_element_type=jnp.float32)
    dealt = picked.astype(jnp.bfloat16)
    attention_parts = (first_gain, first_bias, w_query, b_query, w_keyval, b_value, w_out, b_out)
    feedforward_parts = (second_gain, second_bias, w_expand, b_expand, w_contract, b_contract)
    results = []
    backs = []
    for index in range(micro):
        attention_set = (
            lax.all_gather(attention_parts[0], ("dp", "seq"), axis=0, tiled=True),
            lax.all_gather(attention_parts[1], ("dp", "seq"), axis=0, tiled=True),
            lax.all_gather(attention_parts[2], ("dp", "seq"), axis=0, tiled=True),
            lax.all_gather(attention_parts[3], ("dp", "seq"), axis=0, tiled=True),
            lax.all_gather(attention_parts[4], ("dp", "seq"), axis=0, tiled=True),
            lax.all_gather(attention_parts[5], ("dp", "seq"), axis=0, tiled=True),
            lax.all_gather(attention_parts[6], ("dp", "seq"), axis=0, tiled=True),
            lax.all_gather(attention_parts[7], ("dp", "seq"), axis=0, tiled=True),
        )
        feedforward_set = (
            lax.all_gather(feedforward_parts[0], ("dp", "seq"), axis=0, tiled=True),
            lax.all_gather(feedforward_parts[1], ("dp", "seq"), axis=0, tiled=True),
            lax.all_gather(feedforward_parts[2], ("dp", "seq"), axis=0, tiled=True),
            lax.all_gather(feedforward_parts[3], ("dp", "seq"), axis=0, tiled=True),
            lax.all_gather(feedforward_parts[4], ("dp", "seq"), axis=0, tiled=True),
            lax.all_gather(feedforward_parts[5], ("dp", "seq"), axis=0, tiled=True),
        )
        forward_hidden = dealt[index].astype(jnp.float32)
        forward_front = first_half(forward_hidden, attention_set)
        forward_keyval_all = lax.all_gather(forward_front[4], "seq", axis=0, tiled=True)
        result, stash = second_half(
            forward_hidden,
            forward_front,
            forward_keyval_all,
            attention_set,
            feedforward_set,
            own_length[index],
            first,
        )
        results.append(result)
    for index in range(micro):
        attention_set = (
            lax.all_gather(attention_parts[0], ("dp", "seq"), axis=0, tiled=True),
            lax.all_gather(attention_parts[1], ("dp", "seq"), axis=0, tiled=True),
            lax.all_gather(attention_parts[2], ("dp", "seq"), axis=0, tiled=True),
            lax.all_gather(attention_parts[3], ("dp", "seq"), axis=0, tiled=True),
            lax.all_gather(attention_parts[4], ("dp", "seq"), axis=0, tiled=True),
            lax.all_gather(attention_parts[5], ("dp", "seq"), axis=0, tiled=True),
            lax.all_gather(attention_parts[6], ("dp", "seq"), axis=0, tiled=True),
            lax.all_gather(attention_parts[7], ("dp", "seq"), axis=0, tiled=True),
        )
        feedforward_set = (
            lax.all_gather(feedforward_parts[0], ("dp", "seq"), axis=0, tiled=True),
            lax.all_gather(feedforward_parts[1], ("dp", "seq"), axis=0, tiled=True),
            lax.all_gather(feedforward_parts[2], ("dp", "seq"), axis=0, tiled=True),
            lax.all_gather(feedforward_parts[3], ("dp", "seq"), axis=0, tiled=True),
            lax.all_gather(feedforward_parts[4], ("dp", "seq"), axis=0, tiled=True),
            lax.all_gather(feedforward_parts[5], ("dp", "seq"), axis=0, tiled=True),
        )
        hidden = dealt[index].astype(jnp.float32)
        front = first_half(hidden, attention_set)
        keyval_all = lax.all_gather(front[4], "seq", axis=0, tiled=True)
        recomputed, stash = second_half(
            hidden, front, keyval_all, attention_set, feedforward_set, own_length[index], first
        )
        backs.append(
            run_backward(
                cotangent[index], stash, attention_set, feedforward_set, own_length[index], first
            )
        )
    grad_rows = jnp.stack([entry[0] for entry in backs])
    mine = owner * micro + jnp.arange(micro, dtype=jnp.int32)
    slots = jnp.sum(jnp.where(owner_order[None, :] == mine[:, None], seq_ids[None, :], 0), axis=1)
    piece = lax.all_gather(grad_rows, "dp", axis=0, tiled=True)
    piece_ids = jnp.arange(piece.shape[0], dtype=jnp.int32)
    select = (piece_ids[None, :] == slots[:, None]).astype(jnp.float32)
    picked = jnp.einsum(
        "mn,nbd->mbd",
        select,
        piece,
        precision=lax.Precision.HIGHEST,
        preferred_element_type=jnp.float32,
    )
    factors = [jnp.concatenate([entry[1][place] for entry in backs], axis=0) for place in range(9)]
    smalls = [sum((entry[2][place] for entry in backs)) for place in range(4)]
    (
        normed_all,
        grad_query_all,
        grad_keyval_all,
        mixed_all,
        grad_branch_all,
        normed2_all,
        grad_pre_all,
        active_all,
        grad_m_all,
    ) = factors
    head_size = grad_keyval_all.shape[1] // 2
    feedforward_terms = (
        smalls[2],
        smalls[3],
        outer_sum(normed2_all, grad_pre_all),
        column_sum(grad_pre_all),
        outer_sum(active_all, grad_m_all),
        column_sum(grad_m_all),
    )
    feedforward_grads = (
        lax.psum_scatter(feedforward_terms[0], ("dp", "seq"), scatter_dimension=0, tiled=True),
        lax.psum_scatter(feedforward_terms[1], ("dp", "seq"), scatter_dimension=0, tiled=True),
        lax.psum_scatter(feedforward_terms[2], ("dp", "seq"), scatter_dimension=0, tiled=True),
        lax.psum_scatter(feedforward_terms[3], ("dp", "seq"), scatter_dimension=0, tiled=True),
        lax.psum_scatter(feedforward_terms[4], ("dp", "seq"), scatter_dimension=0, tiled=True),
        lax.psum_scatter(feedforward_terms[5], ("dp", "seq"), scatter_dimension=0, tiled=True),
    )
    attention_terms = (
        smalls[0],
        smalls[1],
        outer_sum(normed_all, grad_query_all),
        column_sum(grad_query_all),
        outer_sum(normed_all, grad_keyval_all),
        column_sum(grad_keyval_all)[head_size:],
        outer_sum(mixed_all, grad_branch_all),
        column_sum(grad_branch_all),
    )
    attention_grads = (
        lax.psum_scatter(attention_terms[0], ("dp", "seq"), scatter_dimension=0, tiled=True),
        lax.psum_scatter(attention_terms[1], ("dp", "seq"), scatter_dimension=0, tiled=True),
        lax.psum_scatter(attention_terms[2], ("dp", "seq"), scatter_dimension=0, tiled=True),
        lax.psum_scatter(attention_terms[3], ("dp", "seq"), scatter_dimension=0, tiled=True),
        lax.psum_scatter(attention_terms[4], ("dp", "seq"), scatter_dimension=0, tiled=True),
        lax.psum_scatter(attention_terms[5], ("dp", "seq"), scatter_dimension=0, tiled=True),
        lax.psum_scatter(attention_terms[6], ("dp", "seq"), scatter_dimension=0, tiled=True),
        lax.psum_scatter(attention_terms[7], ("dp", "seq"), scatter_dimension=0, tiled=True),
    )
    return (
        jnp.stack(results),
        picked,
        attention_grads[0],
        attention_grads[1],
        attention_grads[2],
        attention_grads[3],
        attention_grads[4],
        attention_grads[5],
        attention_grads[6],
        attention_grads[7],
        feedforward_grads[0],
        feedforward_grads[1],
        feedforward_grads[2],
        feedforward_grads[3],
        feedforward_grads[4],
        feedforward_grads[5],
    )


def solution(mesh):
    return jax.shard_map(
        shards,
        mesh=mesh,
        in_specs=(
            P("dp", "seq", None),
            P("dp", "seq", None),
            P(),
            P(),
            P(("dp", "seq")),
            P(("dp", "seq")),
            P(("dp", "seq"), None),
            P(("dp", "seq")),
            P(("dp", "seq"), None),
            P(("dp", "seq")),
            P(("dp", "seq"), None),
            P(("dp", "seq")),
            P(("dp", "seq")),
            P(("dp", "seq")),
            P(("dp", "seq"), None),
            P(("dp", "seq")),
            P(("dp", "seq"), None),
            P(("dp", "seq")),
        ),
        out_specs=(
            P("dp", "seq", None),
            P("dp", "seq", None),
            P(("dp", "seq")),
            P(("dp", "seq")),
            P(("dp", "seq"), None),
            P(("dp", "seq")),
            P(("dp", "seq"), None),
            P(("dp", "seq")),
            P(("dp", "seq"), None),
            P(("dp", "seq")),
            P(("dp", "seq")),
            P(("dp", "seq")),
            P(("dp", "seq"), None),
            P(("dp", "seq")),
            P(("dp", "seq"), None),
            P(("dp", "seq")),
        ),
        check_vma=False,
    )
```

profile of v0, /device:TPU:1, one launch (start us, length us, event | category | flops | bytes accessed | tf_op | source)
XLA Modules:
  0.0 3130.0 jit_solution(7982215472824809684)
XLA Ops:
  18.6 46.9 %all-reduce.19 = (bf16[2048]{0:T(1024)(128)(2,1)S(1)}, bf16[2048]{0:T(1024)(128)(2,1)S(1)}, bf16[2048]{0:T(1024)(128)(2,1)S(1)}, bf16[128]{0:T(256)(128)(2,1)S(1...) all-reduce(bf16[2048]{0:T(1024)(128)(2,1)S(1)} %dynamic-update-slic, ...), channel_id=1, replica_groups=mesh['dp'=4,'seq'=8] {'dp','seq'}, use_global_device_ids=true, to_apply=%add.2 | all-reduce | flops 14464 | bytes 57856
  65.6 41.2 %all-gather = bf16[32,1,256]{2,1,0:T(2,128)(2,1)S(1)} all-gather(bf16[1,1,256]{2,1,0:T(2,128)(2,1)S(1)} %reshape.239), channel_id=1, replica_groups=mesh['dp'=4,'seq'=8] {'dp','seq'}, dimensions={0}, use_global_device_ids=true | all-gather | bytes 16896 | tf_op jit(solution)/shard_map/all_gather | solution.py:277
  123.9 25.0 all-gather.13.cloned.1.call-done
  173.2 54.6 %all-gather.11.cloned.1.call-done = bf16[2048,2048]{1,0:T(8,128)(2,1)} async-done(((bf16[64,2048]{1,0:T(8,128)(2,1)}), bf16[2048,2048]{1,0:T(8,128)(2,1)}) %all-gather.11.cloned.1.call-update) | async-done | bytes 8388624 | tf_op jit(solution)/shard_map/all_gather | solution.py:266
  257.3 49.0 %all-gather.15.cloned.1.call-done = bf16[2048,2048]{1,0:T(8,128)(2,1)} async-done(((bf16[64,2048]{1,0:T(8,128)(2,1)}), bf16[2048,2048]{1,0:T(8,128)(2,1)}) %all-gather.15.cloned.1.call-update) | async-done | bytes 8388624 | tf_op jit(solution)/shard_map/all_gather | solution.py:270
  315.6 186.1 %all-gather.19.cloned.1.call-done = bf16[8192,2048]{1,0:T(8,128)(2,1)} async-done(((bf16[256,2048]{1,0:T(8,128)(2,1)}), bf16[8192,2048]{1,0:T(8,128)(2,1)}) %all-gather.19.cloned.1.call-update) | async-done | bytes 33554448 | tf_op jit(solution)/shard_map/all_gather | solution.py:278
  501.8 19.0 fusion.125
  520.8 17.4 fusion.127
  538.2 158.6 %all-gather.17.cloned.1.call-done = bf16[2048,8192]{1,0:T(8,128)(2,1)} async-done(((bf16[64,8192]{1,0:T(8,128)(2,1)}), bf16[2048,8192]{1,0:T(8,128)(2,1)}) %all-gather.17.cloned.1.call-update) | async-done | bytes 33554448 | tf_op jit(solution)/shard_map/all_gather | solution.py:276
  696.8 17.3 fusion.21
  714.1 17.7 fusion.128
  731.8 18.1 fusion.14
  749.9 19.7 multiply_reduce_fusion.3
  865.4 31.6 %reduce-scatter.10.cloned.1.call-done = f32[128,256]{0,1:T(8,128)} async-done(((f32[1024,256]{0,1:T(8,128)}), f32[128,256]{0,1:T(8,128)}) %reduce-scatter.10.cloned.1.call-update) | async-done | bytes 131088 | tf_op jit(solution)/shard_map/reduce_scatter | solution.py:196
  935.3 24.8 fusion.36
  961.9 24.9 fusion.26
  988.0 15.9 fusion.55
  1018.4 17.7 all-reduce.22.cloned.1.call-done
  1047.5 141.5 %all-gather.21.cloned.1.call-done = f32[8,128,2048]{2,1,0:T(8,128)} async-done(((f32[2,128,2048]{2,1,0:T(8,128)}), f32[8,128,2048]{2,1,0:T(8,128)}) %all-gather.21.cloned.1.call-update) | async-done | bytes 8388624 | tf_op jit(solution)/shard_map/all_gather | solution.py:327
  1203.4 119.2 %reduce-scatter.14.cloned.1.call-done = f32[64,256]{1,0:T(8,128)} async-done(((f32[2048,256]{1,0:T(8,128)}), f32[64,256]{1,0:T(8,128)}) %reduce-scatter.14.cloned.1.call-update) | async-done | bytes 65552 | tf_op jit(solution)/shard_map/reduce_scatter | solution.py:382
  1322.7 187.2 %reduce-scatter.12.cloned.1.call-done = f32[64,2048]{1,0:T(8,128)} async-done(((f32[2048,2048]{1,0:T(8,128)}), f32[64,2048]{1,0:T(8,128)}) %reduce-scatter.12.cloned.1.call-update) | async-done | bytes 524304 | tf_op jit(solution)/shard_map/reduce_scatter | solution.py:380
  1509.8 187.5 %reduce-scatter.16.cloned.1.call-done = f32[64,2048]{1,0:T(8,128)} async-done(((f32[2048,2048]{1,0:T(8,128)}), f32[64,2048]{1,0:T(8,128)}) %reduce-scatter.16.cloned.1.call-update) | async-done | bytes 524304 | tf_op jit(solution)/shard_map/reduce_scatter | solution.py:384
  1697.4 712.4 %reduce-scatter.18.cloned.1.call-done = f32[64,8192]{1,0:T(8,128)} async-done(((f32[2048,8192]{1,0:T(8,128)}), f32[64,8192]{1,0:T(8,128)}) %reduce-scatter.18.cloned.1.call-update) | async-done | bytes 2097168 | tf_op jit(solution)/shard_map/reduce_scatter | solution.py:362
  2409.8 713.2 %reduce-scatter.20.cloned.1.call-done = f32[256,2048]{1,0:T(8,128)} async-done(((f32[8192,2048]{1,0:T(8,128)}), f32[256,2048]{1,0:T(8,128)}) %reduce-scatter.20.cloned.1.call-update) | async-done | bytes 2097168 | tf_op jit(solution)/shard_map/reduce_scatter | solution.py:364
  (313 shorter events, 268.1 us)
Async XLA Ops:
  7.2 103.1 %copy-start.36 = (bf16[2,128,2048]{2,1,0:T(8,128)(2,1)S(1)}, bf16[2,128,2048]{2,1,0:T(8,128)(2,1)}, u32[]{:S(2)}) copy-start(bf16[2,128,2048]{2,1,0:T(8,128)(2,1)} %param.19) | copy-start | bytes 3145732
  7.2 106.3 %all-gather.9.cloned.1.call-start = ((), (), s32[]{:S(2)}) async-start(), calls=%async_computation.7 | async-start | bytes 5242880 | tf_op jit(solution)/shard_map/all_gather | solution.py:253
  7.9 141.0 %all-gather.13.cloned.1.call-start = ((), (), s32[]{:S(2)}) async-start(), calls=%async_computation.9 | async-start | bytes 1081344 | tf_op jit(solution)/shard_map/all_gather | solution.py:268
  8.7 219.2 %all-gather.11.cloned.1.call-start = ((), (), s32[]{:S(2)}) async-start(), calls=%async_computation.8 | async-start | bytes 8650752 | tf_op jit(solution)/shard_map/all_gather | solution.py:266
  9.4 296.8 %all-gather.15.cloned.1.call-start = ((), (), s32[]{:S(2)}) async-start(), calls=%async_computation.10 | async-start | bytes 8650752 | tf_op jit(solution)/shard_map/all_gather | solution.py:270
  10.0 491.8 %all-gather.19.cloned.1.call-start = ((), (), s32[]{:S(2)}) async-start(), calls=%async_computation.12 | async-start | bytes 34603008 | tf_op jit(solution)/shard_map/all_gather | solution.py:278
  10.6 686.3 %all-gather.17.cloned.1.call-start = ((), (), s32[]{:S(2)}) async-start(), calls=%async_computation.11 | async-start | bytes 34603008 | tf_op jit(solution)/shard_map/all_gather | solution.py:276
  11.1 849.9 %reduce-scatter.8.cloned.1.call-start = ((), (), s32[]{:S(2)}) async-start(), calls=%async_computation.13 | async-start | bytes 1179648 | tf_op jit(solution)/shard_map/reduce_scatter | solution.py:196
  65.5 57.7 %copy-start.49 = (f32[2048]{0:T(1024)}, f32[2048]{0:T(1024)S(1)}, u32[]{:S(2)}) copy-start(f32[2048]{0:T(1024)S(1)} %convert_element_type.242) | copy-start | bytes 24580
  122.8 109.7 %copy-start.61 = (f32[128]{0:T(128)}, f32[128]{0:T(128)S(1)}, u32[]{:S(2)}) copy-start(f32[128]{0:T(128)S(1)} %broadcast_multiply_fusion.9) | copy-start | bytes 1540
  123.2 109.3 %copy-start.63 = (f32[128]{0:T(128)}, f32[128]{0:T(128)S(1)}, u32[]{:S(2)}) copy-start(f32[128]{0:T(128)S(1)} %get-tuple-element.122) | copy-start | bytes 1540
  123.9 108.6 %copy-start.12 = (bf16[128,2048]{1,0:T(8,128)(2,1)}, bf16[128,2048]{1,0:T(8,128)(2,1)S(1)}, u32[]{:S(2)}) copy-start(bf16[128,2048]{1,0:T(8,128)(2,1)S(1)} %get-tuple-element.99) | copy-start | bytes 1572868
  123.9 108.9 %copy-start.14 = (bf16[128,2048]{1,0:T(8,128)(2,1)}, bf16[128,2048]{1,0:T(8,128)(2,1)S(1)}, u32[]{:S(2)}) copy-start(bf16[128,2048]{1,0:T(8,128)(2,1)S(1)} %get-tuple-element.100) | copy-start | bytes 1572868
  248.8 57.4 %copy-start.29 = (bf16[128,2048]{1,0:T(8,128)(2,1)}, bf16[128,2048]{1,0:T(8,128)(2,1)S(1)}, u32[]{:S(2)}) copy-start(bf16[128,2048]{1,0:T(8,128)(2,1)S(1)} %convert_element_type.267) | copy-start | bytes 1572868
  311.5 458.1 %copy-start.3 = (f32[128,2048]{1,0:T(8,128)}, f32[128,2048]{1,0:T(8,128)S(1)}, u32[]{:S(2)}) copy-start(f32[128,2048]{1,0:T(8,128)S(1)} %get-tuple-element.115) | copy-start | bytes 3145732
  313.7 456.0 %copy-start.5 = (f32[128,2048]{1,0:T(8,128)}, f32[128,2048]{1,0:T(8,128)S(1)}, u32[]{:S(2)}) copy-start(f32[128,2048]{1,0:T(8,128)S(1)} %get-tuple-element.113) | copy-start | bytes 3145732
  824.2 72.8 %reduce-scatter.10.cloned.1.call-start = ((), (), s32[]{:S(2)}) async-start(), calls=%async_computation.14 | async-start | bytes 1179648 | tf_op jit(solution)/shard_map/reduce_scatter | solution.py:196
  840.8 195.3 %all-reduce.22.cloned.1.call-start = ((), (), s32[]{:S(2)}) async-start(), calls=%async_computation.21 | async-start | bytes 181248
  909.0 280.0 %all-gather.21.cloned.1.call-start = ((), (), s32[]{:S(2)}) async-start(), calls=%async_computation.15 | async-start | bytes 10485760 | tf_op jit(solution)/shard_map/all_gather | solution.py:327
  912.3 410.4 %reduce-scatter.14.cloned.1.call-start = ((), (), s32[]{:S(2)}) async-start(), calls=%async_computation.17 | async-start | bytes 2162688 | tf_op jit(solution)/shard_map/reduce_scatter | solution.py:382
  914.2 595.6 %reduce-scatter.12.cloned.1.call-start = ((), (), s32[]{:S(2)}) async-start(), calls=%async_computation.16 | async-start | bytes 17301504 | tf_op jit(solution)/shard_map/reduce_scatter | solution.py:380
  923.6 773.7 %reduce-scatter.16.cloned.1.call-start = ((), (), s32[]{:S(2)}) async-start(), calls=%async_computation.18 | async-start | bytes 17301504 | tf_op jit(solution)/shard_map/reduce_scatter | solution.py:384
  934.1 1475.7 %reduce-scatter.18.cloned.1.call-start = ((), (), s32[]{:S(2)}) async-start(), calls=%async_computation.19 | async-start | bytes 69206016 | tf_op jit(solution)/shard_map/reduce_scatter | solution.py:362
  960.1 2162.9 %reduce-scatter.20.cloned.1.call-start = ((), (), s32[]{:S(2)}) async-start(), calls=%async_computation.20 | async-start | bytes 69206016 | tf_op jit(solution)/shard_map/reduce_scatter | solution.py:364
  (62 other events, 556.1 us)
Sparse Core Ops, SparseCore 0:
  9.6 83.7 all-gather.8
  96.2 52.5 all-gather.12
  151.8 76.0 all-gather.10
  230.6 75.6 all-gather.14
  308.9 192.7 all-gather.18
  504.5 192.3 all-gather.16
  824.3 33.4 reduce-scatter.7
  860.9 35.9 reduce-scatter.9
  909.2 126.8 all-reduce.21
  1037.5 151.4 all-gather.20
  1191.8 130.7 reduce-scatter.13
  1325.4 184.4 reduce-scatter.11
  1512.7 184.6 reduce-scatter.15
  1700.2 709.6 reduce-scatter.17
  2412.6 710.3 reduce-scatter.19
where the time goes:
time: 3140 us; the launch traced here: 3130 us
  waiting for transfers between devices  2590 us (82%)
  matrix products  318 us (10%)
  blocking collectives  109 us (3%)
  other arithmetic  53.2 us (2%)
  local copies, waits for them, and re-layouts  45.6 us (1%)
    reduce_scatter x1, waiting for transfers between devices, shards(): lax.psum_scatter(feedforward_terms[4], ('dp', 'seq'), scatter_dimension=0...  713 us
    reduce_scatter x1, waiting for transfers between devices, shards(): lax.psum_scatter(feedforward_terms[2], ('dp', 'seq'), scatter_dimension=0...  712 us
    reduce_scatter x1, waiting for transfers between devices, shards(): lax.psum_scatter(attention_terms[6], ('dp', 'seq'), scatter_dimension=0,...  188 us
    reduce_scatter x1, waiting for transfers between devices, shards(): lax.psum_scatter(attention_terms[2], ('dp', 'seq'), scatter_dimension=0,...  187 us
    all_gather x1, waiting for transfers between devices, shards(): lax.all_gather(feedforward_parts[4], ('dp', 'seq'), axis=0, tiled=True)  186 us
    all_gather x1, waiting for transfers between devices, shards(): lax.all_gather(feedforward_parts[2], ('dp', 'seq'), axis=0, tiled=True)  159 us
    all_gather x1, waiting for transfers between devices, shards(): piece = lax.all_gather(grad_rows, 'dp', axis=0, tiled=True)  142 us
    reduce_scatter x1, waiting for transfers between devices, shards(): lax.psum_scatter(attention_terms[4], ('dp', 'seq'), scatter_dimension=0,...  119 us
  transfers between devices with their start and end apart: 15, of which 13 were waited for; matrix products, arithmetic and copies ran while one was open for 9% of the time, Pallas kernels for 0%

commit v1 on v0

v1 whole, which is shorter than its diff:
```python
import functools
import math

import jax
import jax.numpy as jnp
from jax import lax
from jax.experimental import pallas as pl
from jax.experimental.pallas import tpu as pltpu
from jax.sharding import PartitionSpec as P

norm_eps = 1e-05
f32 = jnp.float32
bf16 = jnp.bfloat16
BOTH = ("dp", "seq")


def norm_rows(hidden):
    mean = jnp.mean(hidden, axis=1, keepdims=True)
    centered = hidden - mean
    inv_std = lax.rsqrt(jnp.mean(centered * centered, axis=1, keepdims=True) + norm_eps)
    return (centered * inv_std, inv_std)


def norm_back(grad_normed, normed, inv_std):
    mean_grad = jnp.mean(grad_normed, axis=1, keepdims=True)
    mean_proj = jnp.mean(grad_normed * normed, axis=1, keepdims=True)
    return inv_std * (grad_normed - mean_grad - normed * mean_proj)


def dot(left, right):
    return jnp.dot(left, right, preferred_element_type=f32)


def dot_general(left, right, left_dims, right_dims):
    return lax.dot_general(
        left, right, ((left_dims, right_dims), ((), ())), preferred_element_type=f32
    )


def ring(count):
    return [(i, (i + 1) % count) for i in range(count)]


def ring_gather(piece, count):
    me = lax.axis_index("dp")
    whole = jnp.zeros((count,) + piece.shape, piece.dtype)
    whole = lax.dynamic_update_index_in_dim(whole, piece, me, 0)
    moving = piece
    for step in range(1, count):
        moving = lax.ppermute(moving, "dp", ring(count))
        whole = lax.dynamic_update_index_in_dim(whole, moving, (me - step) % count, 0)
    return whole


def ring_scatter(parts, count):
    me = lax.axis_index("dp")
    moving = None
    for step in range(count):
        mine = lax.dynamic_index_in_dim(parts, (me - 1 - step) % count, 0, keepdims=False)
        mine = mine.astype(f32)
        total = mine if moving is None else mine + moving.astype(f32)
        if step < count - 1:
            moving = lax.ppermute(total.astype(bf16), "dp", ring(count))
    return total


def block_probs(query, key, limit, scale):
    raw = dot_general(query, key, (1,), (1,)) * scale
    place = lax.broadcasted_iota(jnp.int32, raw.shape, 1)
    masked = jnp.where(place <= limit, raw, -1e30)
    top = jnp.max(masked, axis=1, keepdims=True)
    unnormed = jnp.exp(masked - top)
    return unnormed / jnp.sum(unnormed, axis=1, keepdims=True)


def row_limit(first, rows, length):
    place = first + lax.broadcasted_iota(jnp.int32, (rows, 1), 0)
    return jnp.minimum(place, length - 1)


def attend_kernel(rows, scale, lengths_ref, query_ref, keyval_ref, mixed_ref):
    length = lengths_ref[pl.program_id(0)]
    blocks, one, block, size = query_ref.shape
    total = blocks * block
    step = rows // block
    for at in range(total // rows):
        span = (at + 1) * rows
        query = query_ref[at * step : (at + 1) * step].reshape(rows, size)
        keyval = keyval_ref[: (at + 1) * step].reshape(span, 2 * size)
        probs = block_probs(query, keyval[:, :size], row_limit(at * rows, rows, length), scale)
        mixed = dot(probs.astype(bf16), keyval[:, size:])
        mixed_ref[at * step : (at + 1) * step] = mixed.astype(bf16).reshape(step, 1, block, size)


def attend_back_kernel(
    rows, scale, lengths_ref, query_ref, keyval_ref, grad_ref, grad_query_ref, grad_keyval_ref, sums
):
    length = lengths_ref[pl.program_id(0)]
    head = pl.program_id(1)
    blocks, one, block, size = query_ref.shape
    total = blocks * block
    step = rows // block

    @pl.when(head == 0)
    def _():
        sums[...] = jnp.zeros_like(sums)

    for at in range(total // rows):
        span = (at + 1) * rows
        query = query_ref[at * step : (at + 1) * step].reshape(rows, size)
        grad = grad_ref[at * step : (at + 1) * step].reshape(rows, size)
        keyval = keyval_ref[: (at + 1) * step].reshape(span, 2 * size)
        probs = block_probs(query, keyval[:, :size], row_limit(at * rows, rows, length), scale)
        grad_probs = dot_general(grad, keyval[:, size:], (1,), (1,))
        inner = jnp.sum(probs * grad_probs, axis=1, keepdims=True)
        grad_scores = (probs * (grad_probs - inner)).astype(bf16)
        grad_query = (dot(grad_scores, keyval[:, :size]) * scale).astype(bf16)
        grad_query_ref[at * step : (at + 1) * step] = grad_query.reshape(step, 1, block, size)
        sums[:span, :size] += dot_general(grad_scores, query, (0,), (0,)) * scale
        sums[:span, size:] += dot_general(probs.astype(bf16), grad, (0,), (0,))

    @pl.when(head == pl.num_programs(1) - 1)
    def _():
        grad_keyval_ref[...] = sums[...].astype(bf16).reshape(grad_keyval_ref.shape)


def attention_calls(shape, head_size, rows):
    blocks, micro, block, width = shape
    heads = width // head_size
    scale = 1.0 / math.sqrt(head_size)
    head_spec = pl.BlockSpec((blocks, 1, block, head_size), lambda m, h, n: (0, m, 0, h))
    keyval_spec = pl.BlockSpec((blocks, 1, block, 2 * head_size), lambda m, h, n: (0, m, 0, 0))
    area = micro * heads * (blocks * block) ** 2 * head_size
    size = blocks * micro * block * (width + 2 * head_size) * 2
    head_out = jax.ShapeDtypeStruct(shape, bf16)
    keyval_out = jax.ShapeDtypeStruct((blocks, micro, block, 2 * head_size), bf16)
    params = pltpu.CompilerParams(vmem_limit_bytes=56 * 2**20)
    forward = pl.pallas_call(
        functools.partial(attend_kernel, rows, scale),
        out_shape=head_out,
        grid_spec=pltpu.PrefetchScalarGridSpec(
            num_scalar_prefetch=1,
            grid=(micro, heads),
            in_specs=[head_spec, keyval_spec],
            out_specs=head_spec,
        ),
        compiler_params=params,
        cost_estimate=pl.CostEstimate(
            flops=4 * area, bytes_accessed=2 * size, transcendentals=area // head_size
        ),
        name="attend",
    )
    backward = pl.pallas_call(
        functools.partial(attend_back_kernel, rows, scale),
        out_shape=(head_out, keyval_out),
        grid_spec=pltpu.PrefetchScalarGridSpec(
            num_scalar_prefetch=1,
            grid=(micro, heads),
            in_specs=[head_spec, keyval_spec, head_spec],
            out_specs=[head_spec, keyval_spec],
            scratch_shapes=[pltpu.VMEM((blocks * block, 2 * head_size), f32)],
        ),
        compiler_params=params,
        cost_estimate=pl.CostEstimate(
            flops=10 * area, bytes_accessed=4 * size, transcendentals=area // head_size
        ),
        name="attend_back",
    )
    return forward, backward


def gelu_parts(value):
    root = math.sqrt(2.0 / math.pi)
    square = value * value
    bent = jnp.tanh(root * value * (1.0 + 0.044715 * square))
    active = 0.5 * value * (1.0 + bent)
    slope = 0.5 * (1.0 + bent) + 0.5 * value * (1.0 - bent * bent) * root * (
        1.0 + 3.0 * 0.044715 * square
    )
    return active, slope


def shards(
    parts,
    ranks,
    tokens,
    cotangent,
    lengths,
    owner_order,
    first_gain,
    first_bias,
    w_query,
    b_query,
    w_keyval,
    b_value,
    w_out,
    b_out,
    second_gain,
    second_bias,
    w_expand,
    b_expand,
    w_contract,
    b_contract,
):
    micro, block, width = tokens.shape
    head_size = w_keyval.shape[1] // 2
    every = parts * ranks
    rows = micro * block
    all_rows = ranks * rows
    head_cols = width // ranks
    strip = w_query.shape[0]
    hidden_strip = w_contract.shape[0]
    hidden_cols = parts * hidden_strip
    owner = lax.axis_index("dp")
    rank = lax.axis_index("seq")
    seq_ids = jnp.arange(lengths.shape[0], dtype=jnp.int32)
    own_length = lax.dynamic_slice_in_dim(lengths, owner * micro, micro)
    place = rank * block + jnp.arange(block, dtype=jnp.int32)
    valid = (place[None, :] < own_length[:, None]).astype(f32).reshape(rows, 1)

    tokens_all = lax.all_gather(tokens.reshape(rows, width), "seq", axis=0, tiled=True)
    smalls = [
        first_gain,
        first_bias,
        b_query,
        b_out,
        second_gain,
        second_bias,
        b_contract,
        b_expand,
        b_value,
    ]
    lengths_of = [item.shape[0] for item in smalls]
    pad = -sum(lengths_of) % (2 * head_size)
    packed = jnp.concatenate(smalls + [jnp.zeros((pad,), bf16)]).reshape(-1, 2 * head_size)
    packed = jnp.concatenate([w_keyval, packed], axis=0)
    packed = lax.all_gather(packed, BOTH, axis=0, tiled=False)
    keyval_weight = packed[:, :strip].reshape(width, 2 * head_size)
    packed = packed[:, strip:].reshape(every, -1)
    whole = []
    at = 0
    for count in lengths_of:
        whole.append(packed[:, at : at + count].astype(f32))
        at += count
    gain_one, bias_one, query_bias, out_bias, gain_two, bias_two, contract_bias = [
        item.reshape(1, width) for item in whole[:7]
    ]
    expand_bias = lax.dynamic_index_in_dim(
        whole[7].reshape(parts, ranks, hidden_strip), rank, 1, keepdims=False
    ).reshape(1, hidden_cols)
    value_bias = whole[8].reshape(1, head_size)
    query_bias = lax.dynamic_slice_in_dim(query_bias, rank * head_cols, head_cols, axis=1)
    keyval_bias = jnp.concatenate([jnp.zeros_like(value_bias), value_bias], axis=1)

    sent = jnp.concatenate(
        [
            w_query.reshape(strip, ranks, head_cols).transpose(1, 0, 2),
            w_expand.reshape(strip, parts, ranks, hidden_strip)
            .transpose(2, 0, 1, 3)
            .reshape(ranks, strip, hidden_cols),
        ],
        axis=2,
    )
    sent = lax.all_to_all(sent, "seq", 0, 0).reshape(ranks * strip, head_cols + hidden_cols)
    query_weight = ring_gather(sent[:, :head_cols], parts).reshape(width, head_cols)
    moved = [(f, (f % parts) * ranks + f // parts) for f in range(every)]
    out_weight = ring_gather(lax.ppermute(w_out, BOTH, moved), parts)
    out_weight = lax.all_gather(out_weight.reshape(head_cols, width), "seq", axis=0, tiled=True)
    cotangent_all = ring_gather(cotangent, parts).reshape(-1, block, width)
    expand_weight = ring_gather(sent[:, head_cols:], parts).reshape(width, hidden_cols)
    contract_weight = ring_gather(w_contract, parts).reshape(hidden_cols, width)

    mine = owner * micro + jnp.arange(micro, dtype=jnp.int32)
    slots = jnp.sum(jnp.where(owner_order[None, :] == mine[:, None], seq_ids[None, :], 0), axis=1)
    grad_y = jnp.stack(
        [lax.dynamic_index_in_dim(cotangent_all, slots[i], 0, keepdims=False) for i in range(micro)]
    )
    grad_y = grad_y.reshape(rows, width).astype(f32) * valid
    grad_m = grad_y.astype(bf16)
    grad_m_all = lax.all_gather(grad_m, "seq", axis=0, tiled=True)

    head_shape = (ranks, micro, block, head_cols)
    attend, attend_back = attention_calls(head_shape, head_size, 2 * block)
    normed_all, unused_std = norm_rows(tokens_all.astype(f32))
    normed_in_all = (normed_all * gain_one + bias_one).astype(bf16)
    query = (dot(normed_in_all, query_weight) + query_bias).astype(bf16)
    keyval = (dot(normed_in_all, keyval_weight) + keyval_bias).astype(bf16)
    query = query.reshape(head_shape)
    keyval = keyval.reshape(ranks, micro, block, 2 * head_size)
    mixed = attend(own_length, query, keyval)
    mixed_rows = lax.all_to_all(mixed, "seq", 0, 0).reshape(ranks, rows, head_cols)
    mixed_rows = mixed_rows.transpose(1, 0, 2).reshape(rows, width)

    hidden = tokens.reshape(rows, width).astype(f32)
    resid = hidden + dot(mixed_rows, out_weight) + out_bias
    normed2, inv_std2 = norm_rows(resid)
    normed2_in = (normed2 * gain_two + bias_two).astype(bf16)
    normed2_all = lax.all_gather(normed2_in, "seq", axis=0, tiled=True)

    preact = dot(normed2_all, expand_weight) + expand_bias
    active, slope = gelu_parts(preact)
    active = active.astype(bf16)
    grad_active = dot_general(grad_m_all, contract_weight, (1,), (1,))
    grad_pre = (grad_active * slope).astype(bf16)
    grad_c = dot_general(grad_pre, expand_weight, (1,), (1,)).astype(bf16)
    grad_c = lax.psum_scatter(grad_c, "seq", scatter_dimension=0, tiled=True).astype(f32)
    output = dot(active, contract_weight).astype(bf16)
    output = lax.psum_scatter(output, "seq", scatter_dimension=0, tiled=True).astype(f32)
    result = (valid * (resid + output + contract_bias)).astype(bf16)
    result_all = ring_gather(result.reshape(micro, block, width), parts).reshape(-1, block, width)
    wanted = lax.dynamic_slice_in_dim(owner_order, owner * micro, micro)
    result = jnp.stack(
        [lax.dynamic_index_in_dim(result_all, wanted[i], 0, keepdims=False) for i in range(micro)]
    )
    grad_contract = dot_general(active, grad_m_all, (0,), (0,))
    grad_contract = ring_scatter(grad_contract.reshape(parts, hidden_strip, width), parts)
    grad_expand = dot_general(normed2_all, grad_pre, (0,), (0,))
    grad_expand = ring_scatter(
        grad_expand.reshape(parts, ranks * strip, hidden_cols), parts
    ).astype(bf16)
    grad_expand = lax.all_to_all(grad_expand.reshape(ranks, strip, hidden_cols), "seq", 0, 0)
    grad_expand = (
        grad_expand.reshape(ranks, strip, parts, hidden_strip)
        .transpose(1, 2, 0, 3)
        .reshape(strip, every * hidden_strip)
        .astype(f32)
    )

    grad_resid = grad_y + norm_back(grad_c * gain_two, normed2, inv_std2)
    grad_branch = grad_resid.astype(bf16)
    grad_mixed = dot_general(grad_branch, out_weight, (1,), (1,)).astype(bf16)
    grad_mixed = grad_mixed.reshape(rows, ranks, head_cols).transpose(1, 0, 2)
    grad_mixed = lax.all_to_all(grad_mixed, "seq", 0, 0).reshape(head_shape)
    grad_query, grad_keyval = attend_back(own_length, query, keyval, grad_mixed)
    grad_branch_all = lax.all_gather(grad_branch, "seq", axis=0, tiled=True)
    grad_out = dot_general(mixed.reshape(all_rows, head_cols), grad_branch_all, (0,), (0,))
    grad_out = ring_scatter(grad_out.reshape(parts, head_cols // parts, width), parts)
    back = [(d * ranks + s, s * parts + d) for d in range(parts) for s in range(ranks)]
    grad_out = lax.ppermute(grad_out.astype(bf16), BOTH, back).astype(f32)

    both = jnp.concatenate([grad_query, grad_keyval], axis=3).reshape(all_rows, -1)
    grad_in_weight = dot_general(normed_in_all, both, (0,), (0,))
    grad_in_weight = ring_scatter(
        grad_in_weight.reshape(parts, ranks * strip, both.shape[1]), parts
    ).astype(bf16)
    grad_in_weight = lax.all_to_all(
        grad_in_weight.reshape(ranks, strip, both.shape[1]), "seq", 0, 0
    )
    grad_query_weight = (
        grad_in_weight[:, :, :head_cols].transpose(1, 0, 2).reshape(strip, width).astype(f32)
    )
    grad_keyval_weight = jnp.sum(grad_in_weight[:, :, head_cols:].astype(f32), axis=0)

    query_weight_all = lax.all_gather(query_weight, "seq", axis=0, tiled=False)
    both = lax.all_to_all(both.reshape(ranks, rows, -1), "seq", 0, 0)
    grad_query_rows = both[:, :, :head_cols]
    grad_keyval_rows = jnp.sum(both[:, :, head_cols:].astype(f32), axis=0).astype(bf16)
    grad_in = dot_general(grad_query_rows, query_weight_all, (0, 2), (0, 2))
    grad_in = grad_in + dot_general(grad_keyval_rows, keyval_weight, (1,), (1,))
    normed, inv_std = norm_rows(hidden)
    grad_tokens = grad_resid + norm_back(grad_in * gain_one, normed, inv_std)

    def spread(values):
        return values.reshape(every, -1)

    def column_sum(values):
        return jnp.sum(values.astype(f32), axis=0)

    expand_sum = column_sum(grad_pre).reshape(parts, 1, hidden_strip)
    here = jnp.arange(ranks, dtype=jnp.int32)[None, :, None] == rank
    expand_sum = jnp.where(here, expand_sum, 0.0).reshape(every, hidden_strip)
    sums = jnp.concatenate(
        [
            spread(column_sum(grad_in * normed)),
            spread(column_sum(grad_in)),
            spread(column_sum(grad_query_rows.transpose(1, 0, 2).reshape(rows, width))),
            spread(column_sum(grad_branch)),
            spread(column_sum(grad_c * normed2)),
            spread(column_sum(grad_c)),
            spread(column_sum(grad_m)),
            expand_sum,
            spread(column_sum(grad_keyval_rows)[head_size:]),
        ],
        axis=1,
    )
    sums = lax.psum_scatter(sums, BOTH, scatter_dimension=0, tiled=True).reshape(-1)
    small_grads = []
    at = 0
    for count in lengths_of:
        small_grads.append(sums[at : at + count])
        at += count
    return (
        result,
        grad_tokens.reshape(micro, block, width),
        small_grads[0],
        small_grads[1],
        grad_query_weight,
        small_grads[2],
        grad_keyval_weight,
        small_grads[8],
        grad_out,
        small_grads[3],
        small_grads[4],
        small_grads[5],
        grad_expand,
        small_grads[7],
        grad_contract,
        small_grads[6],
    )


def solution(mesh):
    split = P(BOTH)
    rows = P(BOTH, None)
    moved = P("dp", "seq", None)
    return jax.shard_map(
        functools.partial(shards, mesh.shape["dp"], mesh.shape["seq"]),
        mesh=mesh,
        in_specs=(
            moved,
            moved,
            P(),
            P(),
            split,
            split,
            rows,
            split,
            rows,
            split,
            rows,
            split,
            split,
            split,
            rows,
            split,
            rows,
            split,
        ),
        out_specs=(
            moved,
            moved,
            split,
            split,
            rows,
            split,
            rows,
            split,
            rows,
            split,
            split,
            split,
            rows,
            split,
            rows,
            split,
        ),
        check_vma=False,
    )
```

time: 3140 us -> 1050 us (0.33)
  waiting for transfers between devices: 2590 us -> 596 us
  matrix products: 318 us -> 137 us
  blocking collectives: 109 us -> 43.8 us
  local copies, waits for them, and re-layouts: 45.6 us -> 102 us
  starting transfers between devices: 0.98 us -> 53.1 us
    reduce_scatter x7 -> x2, waiting for transfers between devices: 1950 us -> 110 us  [the longest x1 72.8 us: shards(): lax.psum_scatter(output, 'seq', scatter_dimension=0, tiled=True).astype(f32)]
    all_gather x7, waiting for transfers between devices: 615 us -> 15.7 us  [the longest x1 8.32 us: shards(): lax.all_gather(out_weight.reshape(head_cols, width), 'seq', axis=0, tiled...]
    ppermute x0 -> x32, waiting for transfers between devices: none -> 332 us  [the longest x18 235 us: ring_gather(): moving = lax.ppermute(moving, 'dp', ring(count))]
    dot_general x39 -> x14, matrix products: 318 us -> 137 us  [the longest x9 93.5 us: dot_general(): lax.dot_general(left, right, ((left_dims, right_dims), ((), ())), preferr...]
    unnamed x16 -> x11, waiting for transfers between devices: 21.5 us -> 115 us
    all_gather x3 -> x0, blocking collectives: 62.4 us -> none  [the longest x1 41.2 us: shards(): lax.all_gather(feedforward_parts[3], ('dp', 'seq'), axis=0, tiled=True)]
    unnamed x1 -> x0, blocking collectives: 46.9 us -> none
    all_to_all x0 -> x1, blocking collectives: none -> 43.8 us  [shards(): lax.all_to_all(sent, 'seq', 0, 0)]
  transfers between devices with their start and end apart: 15 -> 47, of which waited for: 13 -> 32; matrix products, arithmetic and copies ran while one was open for 9% -> 23% of each run, Pallas kernels for 0% -> 3%
where the time goes in v1:
time: 1050 us
  waiting for transfers between devices  596 us (57%)
  matrix products  137 us (13%)
  local copies, waits for them, and re-layouts  102 us (10%)
  other arithmetic  62.4 us (6%)
  starting transfers between devices  53.1 us (5%)
  blocking collectives  43.8 us (4%)
  Pallas kernels  28.7 us (3%)
  between operations  23.2 us (2%)
    ppermute x18, waiting for transfers between devices, ring_gather(): moving = lax.ppermute(moving, 'dp', ring(count))  235 us
    unnamed x11, waiting for transfers between devices  115 us
    dot_general x9, matrix products, dot_general(): lax.dot_general(left, right, ((left_dims, right_dims), ((), ())), preferr...  93.5 us
    ppermute x12, waiting for transfers between devices, ring_scatter(): moving = lax.ppermute(total.astype(bf16), 'dp', ring(count))  80.9 us
    reduce_scatter x1, waiting for transfers between devices, shards(): lax.psum_scatter(output, 'seq', scatter_dimension=0, tiled=True).astype(f32)  72.8 us
    all_to_all x1, blocking collectives, shards(): lax.all_to_all(sent, 'seq', 0, 0)  43.8 us
    dot_general x5, matrix products, dot(): return jnp.dot(left, right, preferred_element_type=f32)  43.2 us
    reduce_scatter x1, waiting for transfers between devices, shards(): lax.psum_scatter(grad_c, 'seq', scatter_dimension=0, tiled=True).astype(f32)  37.3 us
  transfers between devices with their start and end apart: 47, of which 32 were waited for; matrix products, arithmetic and copies ran while one was open for 23% of the time, Pallas kernels for 3%

profile of v1, /device:TPU:1, one launch (start us, length us, event | category | flops | bytes accessed | tf_op | source)
XLA Modules:
  0.0 1046.2 jit_solution(1468550178073485551)
XLA Ops:
  26.1 14.0 %collective-permute-done.4 = bf16[64,2048]{1,0:T(8,128)(2,1)S(1)} collective-permute-done((bf16[64,2048]{1,0:T(8,128)(2,1)S(1)}, bf16[64,2048]{1,0:T(8,128)(2,1)S(1)}, u32[]{:S(2)}, u32[]{:S(2)}) %collective-permute-start.4) | collective-permute-done | bytes 262176 | tf_op jit(solution)/shard_map/ppermute | solution.py:50
  60.4 43.8 %all_to_all.30 = bf16[8,64,1280]{2,1,0:T(8,128)(2,1)S(1)} all-to-all(bf16[8,64,1280]{2,1,0:T(8,128)(2,1)S(1)} %pad_maximum_fusion), channel_id=1, replica_groups=mesh['dp'=4,'seq'=8] {'seq'}, dimensions={0} | all-to-all | bytes 2621440 | tf_op jit(solution)/shard_map/all_to_all | solution.py:264
  170.9 22.8 %all-to-all-done.1 = bf16[8,2,128,256]{3,2,1,0:T(8,128)(2,1)S(1)} async-done(((bf16[8,2,128,256]{3,2,1,0:T(8,128)(2,1)}), bf16[8,2,128,256]{3,2,1,0:T(8,128)(2,1)S(1)}, u32[]{:S(2)}, u32[]{:S(2)}) %all-to-all-start.1) | async-done | bytes 1048608 | tf_op jit(solution)/shard_map/all_to_all | solution.py:291
  212.6 25.4 %collective-permute-done.16 = bf16[2,128,2048]{2,1,0:T(8,128)(2,1)} collective-permute-done((bf16[2,128,2048]{2,1,0:T(8,128)(2,1)}, bf16[2,128,2048]{2,1,0:T(8,128)(2,1)}, u32[]{:S(2)}, u32[]{:S(2)}) %collective-permute-start.16) | collective-permute-done | bytes 1048608 | tf_op jit(solution)/shard_map/ppermute | solution.py:50
  242.4 21.3 %collective-permute-done.17 = bf16[2,128,2048]{2,1,0:T(8,128)(2,1)} collective-permute-done((bf16[2,128,2048]{2,1,0:T(8,128)(2,1)}, bf16[2,128,2048]{2,1,0:T(8,128)(2,1)}, u32[]{:S(2)}, u32[]{:S(2)}) %collective-permute-start.17) | collective-permute-done | bytes 1048608 | tf_op jit(solution)/shard_map/ppermute | solution.py:50
  272.8 15.8 %collective-permute-done.18 = bf16[2,128,2048]{2,1,0:T(8,128)(2,1)} collective-permute-done((bf16[2,128,2048]{2,1,0:T(8,128)(2,1)}, bf16[2,128,2048]{2,1,0:T(8,128)(2,1)}, u32[]{:S(2)}, u32[]{:S(2)}) %collective-permute-start.18) | collective-permute-done | bytes 1048608 | tf_op jit(solution)/shard_map/ppermute | solution.py:50
  296.9 21.6 %collective-permute-done.10 = bf16[256,2048]{1,0:T(8,128)(2,1)} collective-permute-done((bf16[256,2048]{1,0:T(8,128)(2,1)}, bf16[256,2048]{1,0:T(8,128)(2,1)}, u32[]{:S(2)}, u32[]{:S(2)}) %collective-permute-start.10) | collective-permute-done | bytes 1048608 | tf_op jit(solution)/shard_map/ppermute | solution.py:50
  324.7 16.3 %collective-permute-done.7 = bf16[512,1024]{1,0:T(8,128)(2,1)} collective-permute-done((bf16[512,1024]{1,0:T(8,128)(2,1)}, bf16[512,1024]{1,0:T(8,128)(2,1)}, u32[]{:S(2)}, u32[]{:S(2)}) %collective-permute-start.7) | collective-permute-done | bytes 1048608 | tf_op jit(solution)/shard_map/ppermute | solution.py:50
  344.7 18.7 %collective-permute-done.11 = bf16[256,2048]{1,0:T(8,128)(2,1)S(1)} collective-permute-done((bf16[256,2048]{1,0:T(8,128)(2,1)}, bf16[256,2048]{1,0:T(8,128)(2,1)S(1)}, u32[]{:S(2)}, u32[]{:S(2)}) %collective-permute-start.11) | collective-permute-done | bytes 1048608 | tf_op jit(solution)/shard_map/ppermute | solution.py:50
  364.5 21.3 %collective-permute-done.8 = bf16[512,1024]{1,0:T(8,128)(2,1)S(1)} collective-permute-done((bf16[512,1024]{1,0:T(8,128)(2,1)}, bf16[512,1024]{1,0:T(8,128)(2,1)S(1)}, u32[]{:S(2)}, u32[]{:S(2)}) %collective-permute-start.8) | collective-permute-done | bytes 1048608 | tf_op jit(solution)/shard_map/ppermute | solution.py:50
  388.1 20.2 %collective-permute-done.12 = bf16[256,2048]{1,0:T(8,128)(2,1)S(1)} collective-permute-done((bf16[256,2048]{1,0:T(8,128)(2,1)S(1)}, bf16[256,2048]{1,0:T(8,128)(2,1)S(1)}, u32[]{:S(2)}, u32[]{:S(2)}) %collective-permute-start.12) | collective-permute-done | bytes 1048608 | tf_op jit(solution)/shard_map/ppermute | solution.py:50
  410.5 20.3 %collective-permute-done.9 = bf16[512,1024]{1,0:T(8,128)(2,1)S(1)} collective-permute-done((bf16[512,1024]{1,0:T(8,128)(2,1)S(1)}, bf16[512,1024]{1,0:T(8,128)(2,1)S(1)}, u32[]{:S(2)}, u32[]{:S(2)}) %collective-permute-start.9) | collective-permute-done | bytes 1048608 | tf_op jit(solution)/shard_map/ppermute | solution.py:50
  431.8 14.5 %fusion.57 = f32[2048,1024]{1,0:T(8,128)} fusion(bf16[2048,2048]{1,0:T(8,128)(2,1)} %all-gather.14.cloned.1.call-done, bf16[2048,1024]{1,0:T(8,128)(2,1)} %bitcast.28), kind=kOutput, calls=%fused_computation.176 | convolution fusion | flops 8589934592 | bytes 20971520 | tf_op jit(solution)/shard_map/dot_general | solution.py:31
  446.3 19.4 %convert_reduce_fusion.1 = (f32[1024]{0:T(1024)S(1)}, bf16[2048,1024]{1,0:T(8,128)(2,1)S(1)}) fusion(f32[2048,1024]{1,0:T(8,128)} %fusion.57, f32[1024]{0:T(1024)S(1)} %bitcast.283, bf16[2048,2048]{1,0:T(8,128)(2,1)} %all-gather.16.cloned.1.call-done, bf16[1024,2048]{1,0:T(8,128)(2,1)} %bitcast.35), kind=kOutput, calls=%fused_computation.10 | convolution fusion | flops 8633973760 | bytes 25174016 | tf_op jit(solution)/shard_map/dot_general | solution.py:35
  467.7 13.2 %convolution_convert_fusion = bf16[2048,2048]{1,0:T(8,128)(2,1)} fusion(bf16[2048,1024]{1,0:T(8,128)(2,1)S(1)} %get-tuple-element.62, bf16[2048,1024]{1,0:T(8,128)(2,1)} %bitcast.28), kind=kOutput, calls=%fused_computation.14 | convolution fusion | flops 8594128896 | bytes 16777216 | tf_op jit(solution)/shard_map/dot_general | solution.py:35
  481.0 15.6 %convolution_convert_fusion.1 = bf16[2048,2048]{1,0:T(8,128)(2,1)} fusion(bf16[1024,2048]{1,0:T(8,128)(2,1)} %bitcast.35, f32[2048,1024]{1,0:T(8,128)} %fusion.57, f32[1024]{0:T(1024)S(1)} %bitcast.284), kind=kOutput, calls=%fused_computation.15 | convolution fusion | flops 8615100416 | bytes 20975616 | tf_op jit(solution)/shard_map/dot_general | solution.py:31
  497.6 13.2 %fusion.60 = f32[2048,1024]{1,0:T(8,128)S(1)} fusion(bf16[2048,2048]{1,0:T(8,128)(2,1)} %all-gather.14.cloned.1.call-done, bf16[2048,1024]{1,0:T(8,128)(2,1)} %copy-done.35), kind=kOutput, calls=%fused_computation.179 | convolution fusion | flops 8589934592 | bytes 20971520 | tf_op jit(solution)/shard_map/dot_general | solution.py:35
  515.4 37.3 %reduce-scatter.5.cloned.1.call-done = bf16[256,2048]{1,0:T(8,128)(2,1)} async-done(((bf16[2048,2048]{1,0:T(8,128)(2,1)}), bf16[256,2048]{1,0:T(8,128)(2,1)}) %reduce-scatter.5.cloned.1.call-update) | async-done | bytes 1048592 | tf_op jit(solution)/shard_map/reduce_scatter | solution.py:306
  554.9 72.8 %reduce-scatter.3.cloned.1.call-done = bf16[256,2048]{1,0:T(8,128)(2,1)} async-done(((bf16[2048,2048]{1,0:T(8,128)(2,1)}), bf16[256,2048]{1,0:T(8,128)(2,1)}) %reduce-scatter.3.cloned.1.call-update) | async-done | bytes 1048592 | tf_op jit(solution)/shard_map/reduce_scatter | solution.py:308
  632.9 17.0 %fusion.52 = f32[1024,2048]{1,0:T(8,128)S(1)} fusion(bf16[2048,2048]{1,0:T(8,128)(2,1)} %all-gather.16.cloned.1.call-done, f32[2048,1024]{1,0:T(8,128)} %fusion.57, f32[1024]{0:T(1024)S(1)} %bitcast.285), kind=kOutput, calls=%fused_computation.172 | convolution fusion | flops 8610906112 | bytes 25169920 | tf_op jit(solution)/shard_map/dot_general | solution.py:35
  663.3 15.4 %collective-permute-done.29 = bf16[256,2048]{1,0:T(8,128)(2,1)S(1)} collective-permute-done((bf16[256,2048]{1,0:T(8,128)(2,1)S(1)}, bf16[256,2048]{1,0:T(8,128)(2,1)S(1)}, u32[]{:S(2)}, u32[]{:S(2)}) %collective-permute-start.29) | collective-permute-done | bytes 1048608 | tf_op jit(solution)/shard_map/ppermute | solution.py:63
  680.7 20.5 %collective-permute-done.27 = bf16[512,1024]{1,0:T(8,128)(2,1)S(1)} collective-permute-done((bf16[512,1024]{1,0:T(8,128)(2,1)S(1)}, bf16[512,1024]{1,0:T(8,128)(2,1)S(1)}, u32[]{:S(2)}, u32[]{:S(2)}) %collective-permute-start.27) | collective-permute-done | bytes 1048608 | tf_op jit(solution)/shard_map/ppermute | solution.py:63
  755.2 16.8 %attend_back.1 = (bf16[8,2,128,256]{3,2,1,0:T(8,128)(2,1)}, bf16[8,2,128,256]{3,2,1,0:T(8,128)(2,1)}) custom-call(s32[2]{0:T(128)} %dynamic_slice.78.lengths_ref, bf16[8,2,128,256]{3,2,1,0:T(8,128)(2,1)} %bitcast.289, bf16[8,2,128,256]{3,2,1,0:T(8,128)(2,1)} %bitcast.291, bf16[8,2,128,256]{3,2,1,0:T(8,128)(2,1)} %bitcast.54.grad_ref), custom_call_target="tpu_custom_call" | custom-call | flops 5368709120 | bytes 8388608 | tf_op jit(solution)/shard_map/attend_back/pallas_call | solution.py:334
  882.6 113.6 %all-reduce.4.cloned.1.call-done = f32[32,708]{1,0:T(8,128)} async-done(((f32[32,708]{1,0:T(8,128)}), f32[32,708]{1,0:T(8,128)}) %all-reduce.4.cloned.1.call-update) | async-done | bytes 90640
  (311 shorter events, 392.2 us)
Async XLA Ops:
  7.2 118.4 %all-gather.22.cloned.1.call-start = ((), (), s32[]{:S(2)}) async-start(), calls=%async_computation.16 | async-start | bytes 1216512 | tf_op jit(solution)/shard_map/all_gather | solution.py:237
  14.8 121.0 %all-gather.10.cloned.1.call-start = ((), (), s32[]{:S(2)}) async-start(), calls=%async_computation.8 | async-start | bytes 9437184 | tf_op jit(solution)/shard_map/all_gather | solution.py:221
  15.6 187.7 %all-gather.12.cloned.1.call-start = ((), (), s32[]{:S(2)}) async-start(), calls=%async_computation.9 | async-start | bytes 9437184 | tf_op jit(solution)/shard_map/all_gather | solution.py:268
  170.3 261.5 %all-gather.14.cloned.1.call-start = ((), (), s32[]{:S(2)}) async-start(), calls=%async_computation.10 | async-start | bytes 9437184 | tf_op jit(solution)/shard_map/all_gather | solution.py:298
  211.3 235.0 %all-gather.16.cloned.1.call-start = ((), (), s32[]{:S(2)}) async-start(), calls=%async_computation.12 | async-start | bytes 9437184 | tf_op jit(solution)/shard_map/all_gather | solution.py:280
  294.4 258.2 %reduce-scatter.5.cloned.1.call-start = ((), (), s32[]{:S(2)}) async-start(), calls=%async_computation.13 | async-start | bytes 9437184 | tf_op jit(solution)/shard_map/reduce_scatter | solution.py:306
  296.9 44.1 %collective-permute-start.7 = (bf16[512,1024]{1,0:T(8,128)(2,1)}, bf16[512,1024]{1,0:T(8,128)(2,1)}, u32[]{:S(2)}, u32[]{:S(2)}) collective-permute-start(bf16[512,1024]{1,0:T(8,128)(2,1)} %slice.178), channel_id=1, source_target_pairs={{0,8},{8,16},{16,24},{24,0},{1,9},{9,17},{17,25},{25,1},{2,10},{10... | collective-permute-start | bytes 3145736 | tf_op jit(solution)/shard_map/ppermute | solution.py:50
  318.5 44.8 %collective-permute-start.11 = (bf16[256,2048]{1,0:T(8,128)(2,1)}, bf16[256,2048]{1,0:T(8,128)(2,1)S(1)}, u32[]{:S(2)}, u32[]{:S(2)}) collective-permute-start(bf16[256,2048]{1,0:T(8,128)(2,1)} %collective-permute-done.10), channel_id=1, source_target_pairs={{0,8},{8,16},{16,24},{24,0},{1,9},{9,17},{17,25},{25,1},{2,10},{10... | collective-permute-start | bytes 3145736 | tf_op jit(solution)/shard_map/ppermute | solution.py:50
  341.0 44.8 %collective-permute-start.8 = (bf16[512,1024]{1,0:T(8,128)(2,1)}, bf16[512,1024]{1,0:T(8,128)(2,1)S(1)}, u32[]{:S(2)}, u32[]{:S(2)}) collective-permute-start(bf16[512,1024]{1,0:T(8,128)(2,1)} %collective-permute-done.7), channel_id=1, source_target_pairs={{0,8},{8,16},{16,24},{24,0},{1,9},{9,17},{17,25},{25,1},{2,10},{10... | collective-permute-start | bytes 3145736 | tf_op jit(solution)/shard_map/ppermute | solution.py:50
  363.4 44.9 %collective-permute-start.12 = (bf16[256,2048]{1,0:T(8,128)(2,1)S(1)}, bf16[256,2048]{1,0:T(8,128)(2,1)S(1)}, u32[]{:S(2)}, u32[]{:S(2)}) collective-permute-start(bf16[256,2048]{1,0:T(8,128)(2,1)S(1)} %collective-permute-done.11), channel_id=1, source_target_pairs={{0,8},{8,16},{16,24},{24,0},{1,9},{9,17},{17,25},{25,1},{2,10},{10... | collective-permute-start | bytes 3145736 | tf_op jit(solution)/shard_map/ppermute | solution.py:50
  385.9 44.9 %collective-permute-start.9 = (bf16[512,1024]{1,0:T(8,128)(2,1)S(1)}, bf16[512,1024]{1,0:T(8,128)(2,1)S(1)}, u32[]{:S(2)}, u32[]{:S(2)}) collective-permute-start(bf16[512,1024]{1,0:T(8,128)(2,1)S(1)} %collective-permute-done.8), channel_id=1, source_target_pairs={{0,8},{8,16},{16,24},{24,0},{1,9},{9,17},{17,25},{25,1},{2,10},{10... | collective-permute-start | bytes 3145736 | tf_op jit(solution)/shard_map/ppermute | solution.py:50
  480.9 146.8 %reduce-scatter.3.cloned.1.call-start = ((), (), s32[]{:S(2)}) async-start(), calls=%async_computation.11 | async-start | bytes 9437184 | tf_op jit(solution)/shard_map/reduce_scatter | solution.py:308
  496.6 368.1 %all-gather.18.cloned.1.call-start = ((), (), s32[]{:S(2)}) async-start(), calls=%async_computation.14 | async-start | bytes 9437184 | tf_op jit(solution)/shard_map/all_gather | solution.py:354
  497.4 376.7 %all-gather.20.cloned.1.call-start = ((), (), s32[]{:S(2)}) async-start(), calls=%async_computation.15 | async-start | bytes 9437184 | tf_op jit(solution)/shard_map/all_gather | solution.py:335
  515.2 144.0 %collective-permute-start.26 = (bf16[512,1024]{1,0:T(8,128)(2,1)}, bf16[512,1024]{1,0:T(8,128)(2,1)}, u32[]{:S(2)}, u32[]{:S(2)}) collective-permute-start(bf16[512,1024]{1,0:T(8,128)(2,1)} %fusion.37), channel_id=1, source_target_pairs={{0,8},{8,16},{16,24},{24,0},{1,9},{9,17},{17,25},{25,1},{2,10},{10... | collective-permute-start | bytes 3145736 | tf_op jit(solution)/shard_map/ppermute | solution.py:63
  680.6 59.4 %collective-permute-start.30 = (bf16[256,2048]{1,0:T(8,128)(2,1)S(1)}, bf16[256,2048]{1,0:T(8,128)(2,1)}, u32[]{:S(2)}, u32[]{:S(2)}) collective-permute-start(bf16[256,2048]{1,0:T(8,128)(2,1)S(1)} %fusion.31), channel_id=1, source_target_pairs={{0,8},{8,16},{16,24},{24,0},{1,9},{9,17},{17,25},{25,1},{2,10},{10... | collective-permute-start | bytes 3145736 | tf_op jit(solution)/shard_map/ppermute | solution.py:63
  743.3 68.4 %collective-permute-start.31 = (bf16[256,2048]{1,0:T(8,128)(2,1)}, bf16[256,2048]{1,0:T(8,128)(2,1)}, u32[]{:S(2)}, u32[]{:S(2)}) collective-permute-start(bf16[256,2048]{1,0:T(8,128)(2,1)} %fusion.32), channel_id=1, source_target_pairs={{0,8},{8,16},{16,24},{24,0},{1,9},{9,17},{17,25},{25,1},{2,10},{10... | collective-permute-start | bytes 3145736 | tf_op jit(solution)/shard_map/ppermute | solution.py:63
  749.1 57.2 %all-to-all-start.5 = ((bf16[8,64,1024]{2,1,0:T(8,128)(2,1)}), bf16[8,64,1024]{2,1,0:T(8,128)(2,1)}, u32[]{:S(2)}, u32[]{:S(2)}) async-start(bf16[8,64,1024]{2,1,0:T(8,128)(2,1)} %bitcast.91), calls=%async_computation.7 | async-start | bytes 2097152 | tf_op jit(solution)/shard_map/all_to_all | solution.py:321
  793.0 47.6 %collective-permute-start.14 = (bf16[2,128,2048]{2,1,0:T(8,128)(2,1)}, bf16[2,128,2048]{2,1,0:T(8,128)(2,1)}, u32[]{:S(2)}, u32[]{:S(2)}) collective-permute-start(bf16[2,128,2048]{2,1,0:T(8,128)(2,1)} %collective-permute-done.13), channel_id=1, source_target_pairs={{0,8},{8,16},{16,24},{24,0},{1,9},{9,17},{17,25},{25,1},{2,10},{10... | collective-permute-start | bytes 3145736 | tf_op jit(solution)/shard_map/ppermute | solution.py:50
  806.3 48.3 %all-to-all-start.3 = ((bf16[8,256,512]{2,1,0:T(8,128)(2,1)}), bf16[8,256,512]{2,1,0:T(8,128)(2,1)S(1)}, u32[]{:S(2)}, u32[]{:S(2)}) async-start(bf16[8,256,512]{2,1,0:T(8,128)(2,1)} %bitcast.260), calls=%async_computation.5 | async-start | bytes 4194304 | tf_op jit(solution)/shard_map/all_to_all | solution.py:355
  840.6 169.0 %collective-permute-start.15 = (bf16[2,128,2048]{2,1,0:T(8,128)(2,1)}, bf16[2,128,2048]{2,1,0:T(8,128)(2,1)}, u32[]{:S(2)}, u32[]{:S(2)}) collective-permute-start(bf16[2,128,2048]{2,1,0:T(8,128)(2,1)} %collective-permute-done.14), channel_id=1, source_target_pairs={{0,8},{8,16},{16,24},{24,0},{1,9},{9,17},{17,25},{25,1},{2,10},{10... | collective-permute-start | bytes 3145736 | tf_op jit(solution)/shard_map/ppermute | solution.py:50
  854.6 148.2 %all-to-all-start.4 = ((bf16[8,64,512]{2,1,0:T(8,128)(2,1)}), bf16[8,64,512]{2,1,0:T(8,128)(2,1)}, u32[]{:S(2)}, u32[]{:S(2)}) async-start(bf16[8,64,512]{2,1,0:T(8,128)(2,1)} %bitcast.270), calls=%async_computation.6 | async-start | bytes 1048576 | tf_op jit(solution)/shard_map/all_to_all | solution.py:346
  861.5 134.6 %all-reduce.4.cloned.1.call-start = ((), (), s32[]{:S(2)}) async-start(), calls=%async_computation.17 | async-start | bytes 196608
  880.4 119.8 %collective-permute-start.22 = (bf16[64,2048]{1,0:T(8,128)(2,1)S(1)}, bf16[64,2048]{1,0:T(8,128)(2,1)}, u32[]{:S(2)}, u32[]{:S(2)}) collective-permute-start(bf16[64,2048]{1,0:T(8,128)(2,1)S(1)} %fusion.47), channel_id=1, source_target_pairs={{0,8},{8,16},{16,24},{24,0},{1,9},{9,17},{17,25},{25,1},{2,10},{10... | collective-permute-start | bytes 786440 | tf_op jit(solution)/shard_map/ppermute | solution.py:63
  (59 other events, 1063.7 us)
Sparse Core Ops, SparseCore 0:
  15.0 59.0 all-gather.21
  75.9 59.9 all-gather.9
  137.8 65.4 all-gather.11
  211.4 54.2 all-gather.13
  294.6 54.0 all-gather.15
  481.1 71.5 reduce-scatter.4
  556.2 71.5 reduce-scatter.2
  629.6 54.8 all-gather.17
  686.4 65.4 all-gather.19
  874.2 121.8 all-reduce.3

commit v2 on v1

--- a/solution.py
+++ b/solution.py
@@ -37,31 +37,84 @@
     )
 
 
-def ring(count):
-    return [(i, (i + 1) % count) for i in range(count)]
-
-
-def ring_gather(piece, count):
+def shift(count, by):
+    return [(i, (i + by) % count) for i in range(count)]
+
+
+def gather_parts(piece, count):
     me = lax.axis_index("dp")
     whole = jnp.zeros((count,) + piece.shape, piece.dtype)
     whole = lax.dynamic_update_index_in_dim(whole, piece, me, 0)
-    moving = piece
+    for by in range(1, count):
+        moved = lax.ppermute(piece, "dp", shift(count, by))
+        whole = lax.dynamic_update_index_in_dim(whole, moved, (me - by) % count, 0)
+    return whole
+
+
+def ring_pieces(piece, count):
+    pieces = [piece]
     for step in range(1, count):
-        moving = lax.ppermute(moving, "dp", ring(count))
-        whole = lax.dynamic_update_index_in_dim(whole, moving, (me - step) % count, 0)
+        pieces.append(lax.ppermute(pieces[-1], "dp", shift(count, 1)))
+    return pieces
+
+
+def exchange_parts(pieces, count):
+    me = lax.axis_index("dp")
+    own = lax.dynamic_index_in_dim(pieces, me, 0, keepdims=False)
+    whole = lax.dynamic_update_index_in_dim(jnp.zeros_like(pieces), own, me, 0)
+    for by in range(1, count):
+        piece = lax.dynamic_index_in_dim(pieces, (me + by) % count, 0, keepdims=False)
+        moved = lax.ppermute(piece, "dp", shift(count, by))
+        whole = lax.dynamic_update_index_in_dim(whole, moved, (me - by) % count, 0)
     return whole
+
+
+def ring_sum(part_for, count):
+    moving = None
+    for step in range(count):
+        total = part_for((1 + step) % count)
+        if moving is not None:
+            total = total + moving.astype(f32)
+        if step < count - 1:
+            moving = lax.ppermute(total.astype(bf16), "dp", shift(count, 1))
+    return total
 
 
 def ring_scatter(parts, count):
     me = lax.axis_index("dp")
-    moving = None
-    for step in range(count):
-        mine = lax.dynamic_index_in_dim(parts, (me - 1 - step) % count, 0, keepdims=False)
-        mine = mine.astype(f32)
-        total = mine if moving is None else mine + moving.astype(f32)
-        if step < count - 1:
-            moving = lax.ppermute(total.astype(bf16), "dp", ring(count))
-    return total
+
+    def part_for(by):
+        return lax.dynamic_index_in_dim(parts, (me - by) % count, 0, keepdims=False).astype(f32)
+
+    return ring_sum(part_for, count)
+
+
+def halve(values, axis, bit, rank, count):
+    mine = (rank >> bit) & 1
+    keep = lax.dynamic_index_in_dim(values, mine, axis, keepdims=False)
+    give = lax.dynamic_index_in_dim(values, 1 - mine, axis, keepdims=False)
+    moved = lax.ppermute(give.astype(bf16), "seq", [(i, i ^ (1 << bit)) for i in range(count)])
+    return keep.astype(f32) + moved.astype(f32)
+
+
+def rank_scatter(values, count):
+    rank = lax.axis_index("seq")
+    bits = count.bit_length() - 1
+    outer, unused, length, width = values.shape
+    halves = values.reshape((outer,) + (2,) * bits + (2, length // 2, width))
+    halves = halve(halves, bits, 0, rank, count).astype(bf16)
+    done = []
+    for at in range(2):
+        half = lax.index_in_dim(halves, at, bits, keepdims=False)
+        left = list(range(bits - 1, 0, -1))
+        order = left[::-1] if at == 0 else left[:]
+        for bit in order:
+            half = halve(half, 1 + left.index(bit), bit, rank, count)
+            left.remove(bit)
+            if left:
+                half = half.astype(bf16)
+        done.append(half)
+    return jnp.concatenate(done, axis=1)
 
 
 def block_probs(query, key, limit, scale):
@@ -210,13 +263,12 @@
     head_cols = width // ranks
     strip = w_query.shape[0]
     hidden_strip = w_contract.shape[0]
-    hidden_cols = parts * hidden_strip
+    hidden_cols = ranks * hidden_strip
     owner = lax.axis_index("dp")
     rank = lax.axis_index("seq")
     seq_ids = jnp.arange(lengths.shape[0], dtype=jnp.int32)
     own_length = lax.dynamic_slice_in_dim(lengths, owner * micro, micro)
     place = rank * block + jnp.arange(block, dtype=jnp.int32)
-    valid = (place[None, :] < own_length[:, None]).astype(f32).reshape(rows, 1)
 
     tokens_all = lax.all_gather(tokens.reshape(rows, width), "seq", axis=0, tiled=True)
     smalls = [
@@ -231,10 +283,11 @@
         b_value,
     ]
     lengths_of = [item.shape[0] for item in smalls]
-    pad = -sum(lengths_of) % (2 * head_size)
+    pad = -sum(lengths_of) % (16 * head_size)
     packed = jnp.concatenate(smalls + [jnp.zeros((pad,), bf16)]).reshape(-1, 2 * head_size)
     packed = jnp.concatenate([w_keyval, packed], axis=0)
-    packed = lax.all_gather(packed, BOTH, axis=0, tiled=False)
+    packed = jnp.broadcast_to(packed[None], (every,) + packed.shape)
+    packed = lax.all_to_all(packed, BOTH, 0, 0)
     keyval_weight = packed[:, :strip].reshape(width, 2 * head_size)
     packed = packed[:, strip:].reshape(every, -1)
     whole = []
@@ -245,39 +298,46 @@
     gain_one, bias_one, query_bias, out_bias, gain_two, bias_two, contract_bias = [
         item.reshape(1, width) for item in whole[:7]
     ]
-    expand_bias = lax.dynamic_index_in_dim(
-        whole[7].reshape(parts, ranks, hidden_strip), rank, 1, keepdims=False
-    ).reshape(1, hidden_cols)
+    expand_bias = lax.dynamic_slice_in_dim(whole[7], owner * ranks, ranks)
+    expand_bias = expand_bias.reshape(1, hidden_cols)
     value_bias = whole[8].reshape(1, head_size)
     query_bias = lax.dynamic_slice_in_dim(query_bias, rank * head_cols, head_cols, axis=1)
     keyval_bias = jnp.concatenate([jnp.zeros_like(value_bias), value_bias], axis=1)
 
-    sent = jnp.concatenate(
-        [
-            w_query.reshape(strip, ranks, head_cols).transpose(1, 0, 2),
-            w_expand.reshape(strip, parts, ranks, hidden_strip)
-            .transpose(2, 0, 1, 3)
-            .reshape(ranks, strip, hidden_cols),
-        ],
-        axis=2,
-    )
-    sent = lax.all_to_all(sent, "seq", 0, 0).reshape(ranks * strip, head_cols + hidden_cols)
-    query_weight = ring_gather(sent[:, :head_cols], parts).reshape(width, head_cols)
+    sent = w_query.reshape(strip, ranks, head_cols).transpose(1, 0, 2)
+    sent = lax.all_to_all(sent, "seq", 0, 0).reshape(ranks * strip, head_cols)
+    query_weight = gather_parts(sent, parts).reshape(width, head_cols)
     moved = [(f, (f % parts) * ranks + f // parts) for f in range(every)]
-    out_weight = ring_gather(lax.ppermute(w_out, BOTH, moved), parts)
+    out_weight = gather_parts(lax.ppermute(w_out, BOTH, moved), parts)
     out_weight = lax.all_gather(out_weight.reshape(head_cols, width), "seq", axis=0, tiled=True)
-    cotangent_all = ring_gather(cotangent, parts).reshape(-1, block, width)
-    expand_weight = ring_gather(sent[:, head_cols:], parts).reshape(width, hidden_cols)
-    contract_weight = ring_gather(w_contract, parts).reshape(hidden_cols, width)
-
-    mine = owner * micro + jnp.arange(micro, dtype=jnp.int32)
-    slots = jnp.sum(jnp.where(owner_order[None, :] == mine[:, None], seq_ids[None, :], 0), axis=1)
-    grad_y = jnp.stack(
-        [lax.dynamic_index_in_dim(cotangent_all, slots[i], 0, keepdims=False) for i in range(micro)]
-    )
-    grad_y = grad_y.reshape(rows, width).astype(f32) * valid
-    grad_m = grad_y.astype(bf16)
-    grad_m_all = lax.all_gather(grad_m, "seq", axis=0, tiled=True)
+    sent = w_expand.reshape(strip, parts, hidden_cols).transpose(1, 0, 2)
+    sent = exchange_parts(sent, parts).reshape(parts * strip, hidden_cols)
+    expand_weight = lax.all_gather(sent, "seq", axis=0, tiled=False)
+    expand_weight = (
+        expand_weight.reshape(ranks, parts, strip, hidden_cols)
+        .transpose(1, 0, 2, 3)
+        .reshape(width, hidden_cols)
+    )
+    contract_weight = lax.all_gather(w_contract, "seq", axis=0, tiled=True)
+
+    cotangents = jnp.stack(ring_pieces(cotangent, parts)).reshape(-1, block, width)
+    slot_of = jnp.sum(
+        jnp.where(owner_order[None, :] == seq_ids[:, None], seq_ids[None, :], 0), axis=1
+    )
+
+    def grad_of(behind):
+        taken = []
+        for i in range(micro):
+            seq = ((owner - behind) % parts) * micro + i
+            slot = slot_of[seq]
+            at = ((owner - slot // micro) % parts) * micro + slot % micro
+            piece = lax.dynamic_index_in_dim(cotangents, at, 0, keepdims=False)
+            inside = (place < lengths[seq])[:, None]
+            taken.append(jnp.where(inside, piece, jnp.zeros_like(piece)))
+        return jnp.concatenate(taken, axis=0)
+
+    grad_ms = [grad_of(behind) for behind in range(parts)]
+    grad_y = grad_ms[0].astype(f32)
 
     head_shape = (ranks, micro, block, head_cols)
     attend, attend_back = attention_calls(head_shape, head_size, 2 * block)
@@ -295,36 +355,53 @@
     resid = hidden + dot(mixed_rows, out_weight) + out_bias
     normed2, inv_std2 = norm_rows(resid)
     normed2_in = (normed2 * gain_two + bias_two).astype(bf16)
-    normed2_all = lax.all_gather(normed2_in, "seq", axis=0, tiled=True)
-
-    preact = dot(normed2_all, expand_weight) + expand_bias
-    active, slope = gelu_parts(preact)
-    active = active.astype(bf16)
-    grad_active = dot_general(grad_m_all, contract_weight, (1,), (1,))
-    grad_pre = (grad_active * slope).astype(bf16)
-    grad_c = dot_general(grad_pre, expand_weight, (1,), (1,)).astype(bf16)
-    grad_c = lax.psum_scatter(grad_c, "seq", scatter_dimension=0, tiled=True).astype(f32)
-    output = dot(active, contract_weight).astype(bf16)
-    output = lax.psum_scatter(output, "seq", scatter_dimension=0, tiled=True).astype(f32)
-    result = (valid * (resid + output + contract_bias)).astype(bf16)
-    result_all = ring_gather(result.reshape(micro, block, width), parts).reshape(-1, block, width)
-    wanted = lax.dynamic_slice_in_dim(owner_order, owner * micro, micro)
-    result = jnp.stack(
-        [lax.dynamic_index_in_dim(result_all, wanted[i], 0, keepdims=False) for i in range(micro)]
-    )
-    grad_contract = dot_general(active, grad_m_all, (0,), (0,))
-    grad_contract = ring_scatter(grad_contract.reshape(parts, hidden_strip, width), parts)
-    grad_expand = dot_general(normed2_all, grad_pre, (0,), (0,))
-    grad_expand = ring_scatter(
-        grad_expand.reshape(parts, ranks * strip, hidden_cols), parts
-    ).astype(bf16)
-    grad_expand = lax.all_to_all(grad_expand.reshape(ranks, strip, hidden_cols), "seq", 0, 0)
-    grad_expand = (
-        grad_expand.reshape(ranks, strip, parts, hidden_strip)
-        .transpose(1, 2, 0, 3)
-        .reshape(strip, every * hidden_strip)
-        .astype(f32)
-    )
+
+    normed2_ins = ring_pieces(normed2_in, parts)
+    actives = [None] * parts
+    grad_pres = [None] * parts
+
+    def grad_c_for(behind):
+        preact = dot(normed2_ins[behind], expand_weight) + expand_bias
+        active, slope = gelu_parts(preact)
+        actives[behind] = active.astype(bf16)
+        grad_active = dot_general(grad_ms[behind], contract_weight, (1,), (1,))
+        grad_pres[behind] = (grad_active * slope).astype(bf16)
+        return dot_general(grad_pres[behind], expand_weight, (1,), (1,))
+
+    grad_c = ring_sum(grad_c_for, parts)
+    outputs = jnp.stack([dot(active, contract_weight).astype(bf16) for active in actives])
+    outputs = outputs.reshape(parts * micro, block, width)
+    resid_rows = resid.reshape(micro, block, width)
+
+    def output_for(behind):
+        taken = []
+        for i in range(micro):
+            seq = owner_order[((owner - behind) % parts) * micro + i]
+            source = (owner - seq // micro) % parts
+            piece = lax.dynamic_index_in_dim(
+                outputs, source * micro + seq % micro, 0, keepdims=False
+            )
+            own = lax.dynamic_index_in_dim(resid_rows, seq % micro, 0, keepdims=False)
+            taken.append(piece.astype(f32) + jnp.where(source == 0, own, 0.0))
+        return jnp.stack(taken)
+
+    result = ring_sum(output_for, parts)
+    held = lax.dynamic_slice_in_dim(owner_order, owner * micro, micro)
+    held_length = jnp.sum(jnp.where(held[:, None] == seq_ids[None, :], lengths[None, :], 0), axis=1)
+    held_valid = (place[None, :] < held_length[:, None])[:, :, None]
+    result = jnp.where(held_valid, result + contract_bias, 0.0).astype(bf16)
+
+    active_all = jnp.concatenate(actives, axis=0)
+    grad_pre_all = jnp.concatenate(grad_pres, axis=0)
+    grad_m_all = jnp.concatenate(grad_ms, axis=0)
+    normed2_all = jnp.concatenate(normed2_ins, axis=0)
+    grad_contract = dot_general(active_all, grad_m_all, (0,), (0,)).astype(bf16)
+    grad_contract = rank_scatter(grad_contract.reshape(1, ranks, hidden_strip, width), ranks)
+    grad_contract = grad_contract.reshape(hidden_strip, width)
+    grad_expand = dot_general(normed2_all, grad_pre_all, (0,), (0,)).astype(bf16)
+    grad_expand = rank_scatter(grad_expand.reshape(parts, ranks, strip, hidden_cols), ranks)
+    grad_expand = exchange_parts(grad_expand.astype(bf16), parts)
+    grad_expand = grad_expand.transpose(1, 0, 2).reshape(strip, -1).astype(f32)
 
     grad_resid = grad_y + norm_back(grad_c * gain_two, normed2, inv_std2)
     grad_branch = grad_resid.astype(bf16)
@@ -351,11 +428,11 @@
     )
     grad_keyval_weight = jnp.sum(grad_in_weight[:, :, head_cols:].astype(f32), axis=0)
 
-    query_weight_all = lax.all_gather(query_weight, "seq", axis=0, tiled=False)
+    query_weight_all = lax.all_gather(query_weight.T, "seq", axis=0, tiled=True)
     both = lax.all_to_all(both.reshape(ranks, rows, -1), "seq", 0, 0)
-    grad_query_rows = both[:, :, :head_cols]
+    grad_query_rows = both[:, :, :head_cols].transpose(1, 0, 2).reshape(rows, width)
     grad_keyval_rows = jnp.sum(both[:, :, head_cols:].astype(f32), axis=0).astype(bf16)
-    grad_in = dot_general(grad_query_rows, query_weight_all, (0, 2), (0, 2))
+    grad_in = dot(grad_query_rows, query_weight_all)
     grad_in = grad_in + dot_general(grad_keyval_rows, keyval_weight, (1,), (1,))
     normed, inv_std = norm_rows(hidden)
     grad_tokens = grad_resid + norm_back(grad_in * gain_one, normed, inv_std)
@@ -366,24 +443,24 @@
     def column_sum(values):
         return jnp.sum(values.astype(f32), axis=0)
 
-    expand_sum = column_sum(grad_pre).reshape(parts, 1, hidden_strip)
-    here = jnp.arange(ranks, dtype=jnp.int32)[None, :, None] == rank
+    expand_sum = column_sum(grad_pre_all).reshape(1, ranks, hidden_strip)
+    here = jnp.arange(parts, dtype=jnp.int32)[:, None, None] == owner
     expand_sum = jnp.where(here, expand_sum, 0.0).reshape(every, hidden_strip)
     sums = jnp.concatenate(
         [
             spread(column_sum(grad_in * normed)),
             spread(column_sum(grad_in)),
-            spread(column_sum(grad_query_rows.transpose(1, 0, 2).reshape(rows, width))),
+            spread(column_sum(grad_query_rows)),
             spread(column_sum(grad_branch)),
             spread(column_sum(grad_c * normed2)),
             spread(column_sum(grad_c)),
-            spread(column_sum(grad_m)),
+            spread(column_sum(grad_y)),
             expand_sum,
             spread(column_sum(grad_keyval_rows)[head_size:]),
         ],
         axis=1,
     )
-    sums = lax.psum_scatter(sums, BOTH, scatter_dimension=0, tiled=True).reshape(-1)
+    sums = jnp.sum(lax.all_to_all(sums, BOTH, 0, 0), axis=0)
     small_grads = []
     at = 0
     for count in lengths_of:

time: 1050 us -> 796 us (0.76)
  waiting for transfers between devices: 596 us -> 258 us
  starting transfers between devices: 53.1 us -> 123 us
  blocking collectives: 43.8 us -> 0 us
  between operations: 23.2 us -> 57.8 us
  other arithmetic: 62.4 us -> 90.6 us
  local copies, waits for them, and re-layouts: 102 us -> 79.1 us
  matrix products: 137 us -> 150 us
    unnamed x11 -> x6, waiting for transfers between devices: 115 us -> 1.27 us
    reduce_scatter x2 -> x0, waiting for transfers between devices: 110 us -> none  [the longest x1 72.8 us: shards(): lax.psum_scatter(output, 'seq', scatter_dimension=0, tiled=True).astype(f32)]
    ppermute x31 -> x41, waiting for transfers between devices: 320 us -> 234 us  [the longest x12 80.6 us: ring_sum(): moving = lax.ppermute(total.astype(bf16), 'dp', shift(count, 1))]
    ppermute x31 -> x41, starting transfers between devices: 15.5 us -> 75.9 us  [the longest x6 17.8 us: ring_pieces(): pieces.append(lax.ppermute(pieces[-1], 'dp', shift(count, 1)))]
    all_to_all x1 -> x0, blocking collectives: 43.8 us -> none  [shards(): lax.all_to_all(sent, 'seq', 0, 0)]
    dynamic_update_slice x24 -> x15, local copies, waits for them, and re-layouts: 26.2 us -> 2.38 us  [the longest x6 1.08 us: gather_parts(): whole = lax.dynamic_update_index_in_dim(whole, moved, (me - by) % count, 0)]
    all_to_all x1, waiting for transfers between devices: 22.8 us -> 0.01 us  [shards(): lax.all_to_all(mixed, 'seq', 0, 0).reshape(ranks, rows, head_cols)]
    dot_general x5 -> x12, matrix products: 43.2 us -> 64.9 us  [dot(): return jnp.dot(left, right, preferred_element_type=f32)]
  transfers between devices with their start and end apart: 47 -> 55, of which waited for: 32 -> 27; matrix products, arithmetic and copies ran while one was open for 23% -> 39% of each run, Pallas kernels for 3% -> 4%
where the time goes in v2:
time: 796 us; the launch traced here: 787 us
  waiting for transfers between devices  258 us (32%)
  matrix products  150 us (19%)
  starting transfers between devices  123 us (15%)
  other arithmetic  90.6 us (11%)
  local copies, waits for them, and re-layouts  79.1 us (10%)
  between operations  57.8 us (7%)
  Pallas kernels  28.9 us (4%)
    dot_general x14, matrix products, dot_general(): lax.dot_general(left, right, ((left_dims, right_dims), ((), ())), preferr...  84.9 us
    ppermute x12, waiting for transfers between devices, ring_sum(): moving = lax.ppermute(total.astype(bf16), 'dp', shift(count, 1))  80.6 us
    dot_general x12, matrix products, dot(): return jnp.dot(left, right, preferred_element_type=f32)  64.9 us
    ppermute x10, waiting for transfers between devices, halve(): lax.ppermute(give.astype(bf16), 'seq', [(i, i ^ 1 << bit) for i in range(...  57.5 us
    ppermute x6, waiting for transfers between devices, gather_parts(): moved = lax.ppermute(piece, 'dp', shift(count, by))  47.9 us
    ppermute x6, waiting for transfers between devices, ring_pieces(): pieces.append(lax.ppermute(pieces[-1], 'dp', shift(count, 1)))  28.4 us
    ppermute x6, starting transfers between devices, ring_pieces(): pieces.append(lax.ppermute(pieces[-1], 'dp', shift(count, 1)))  17.8 us
    pallas_call x1, Pallas kernels, shards(): grad_query, grad_keyval = attend_back(own_length, query, keyval, grad_mixed)  16.8 us
  transfers between devices with their start and end apart: 55, of which 27 were waited for; matrix products, arithmetic and copies ran while one was open for 39% of the time, Pallas kernels for 4%

profile of v2, /device:TPU:1, one launch (start us, length us, event | category | flops | bytes accessed | tf_op | source)
XLA Modules:
  0.0 786.9 jit_solution(11141817866008376381)
XLA Ops:
  22.5 11.9 %collective-permute-done.8 = bf16[64,2048]{1,0:T(8,128)(2,1)S(1)} collective-permute-done((bf16[64,2048]{1,0:T(8,128)(2,1)S(1)}, bf16[64,2048]{1,0:T(8,128)(2,1)S(1)}, u32[]{:S(2)}, u32[]{:S(2)}) %collective-permute-start.8) | collective-permute-done | bytes 262176 | tf_op jit(solution)/shard_map/ppermute | solution.py:67
  35.6 8.1 %collective-permute-start.3 = (bf16[64,2048]{1,0:T(8,128)(2,1)S(1)}, bf16[64,2048]{1,0:T(8,128)(2,1)S(1)}, u32[]{:S(2)}, u32[]{:S(2)}) collective-permute-start(bf16[64,2048]{1,0:T(8,128)(2,1)S(1)} %copy-done.68), channel_id=1, source_target_pairs={{0,0},{1,8},{2,16},{3,24},{4,1},{5,9},{6,17},{7,25},{8,2},{9,10},{... | collective-permute-start | bytes 786440 | tf_op jit(solution)/shard_map/ppermute | solution.py:311
  47.1 9.8 %collective-permute-start.4 = (bf16[64,2048]{1,0:T(8,128)(2,1)S(1)}, bf16[64,2048]{1,0:T(8,128)(2,1)S(1)}, u32[]{:S(2)}, u32[]{:S(2)}) collective-permute-start(bf16[64,2048]{1,0:T(8,128)(2,1)S(1)} %collective-permute-done.3), channel_id=1, source_target_pairs={{0,8},{8,16},{16,24},{24,0},{1,9},{9,17},{17,25},{25,1},{2,10},{10... | collective-permute-start | bytes 786440 | tf_op jit(solution)/shard_map/ppermute | solution.py:49
  63.0 9.7 %collective-permute-done.5 = bf16[64,2048]{1,0:T(8,128)(2,1)S(1)} collective-permute-done((bf16[64,2048]{1,0:T(8,128)(2,1)S(1)}, bf16[64,2048]{1,0:T(8,128)(2,1)S(1)}, u32[]{:S(2)}, u32[]{:S(2)}) %collective-permute-start.5) | collective-permute-done | bytes 262176 | tf_op jit(solution)/shard_map/ppermute | solution.py:49
  158.1 34.3 %collective-permute-done.1 = bf16[512,256]{1,0:T(8,128)(2,1)S(1)} collective-permute-done((bf16[512,256]{1,0:T(8,128)(2,1)S(1)}, bf16[512,256]{1,0:T(8,128)(2,1)S(1)}, u32[]{:S(2)}, u32[]{:S(2)}) %collective-permute-start.1) | collective-permute-done | bytes 262176 | tf_op jit(solution)/shard_map/ppermute | solution.py:49
  227.4 12.1 %attend.1 = bf16[8,2,128,256]{3,2,1,0:T(8,128)(2,1)} custom-call(s32[2]{0:T(128)} %dynamic_slice.272.lengths_ref, bf16[8,2,128,256]{3,2,1,0:T(8,128)(2,1)} %bitcast.382, bf16[8,2,128,256]{3,2,1,0:T(8,128)(2,1)} %bitcast.384), custom_call_target="tpu_custom_call" | custom-call | flops 2147483648 | bytes 4194304 | tf_op jit(solution)/shard_map/attend/pallas_call | solution.py:350
  248.2 8.6 %fusion.146 = bf16[2048,2048]{0,1:T(8,128)(2,1)} fusion(f32[2048]{0:T(1024)S(1)} %reshape.468, f32[2048]{0:T(1024)S(1)} %reshape.467, f32[2048]{0:T(1024)S(1)} %add_rsqrt_fusion, f32[2048]{0:T(1024)S(1)} %broadcast_multiply_fusion, bf16[2048,2048]{1,0:T(8,128)(2,1)} %all-gather.7.cloned.1.call-done), kind=kLoop, calls=%fused_computation.292 | loop fusion | flops 25165824 | bytes 16809984 | tf_op jit(solution)/shard_map/dot_general | solution.py:35
  256.7 12.3 %copy.123 = bf16[2048,2048]{1,0:T(8,128)(2,1)} copy(bf16[2048,2048]{0,1:T(8,128)(2,1)} %fusion.146) | data formatting | bytes 16777216 | tf_op jit(solution)/shard_map/dot_general | solution.py:35
  269.0 8.6 %copy.112 = bf16[4,8,64,2048]{3,2,1,0:T(8,128)(2,1)} copy(bf16[4,8,64,2048]{3,2,0,1:T(8,128)(2,1)} %bitcast.329) | data formatting | bytes 16777216 | tf_op jit(solution)/shard_map/transpose | solution.py:318
  339.8 8.5 %collective-permute-done.11 = bf16[256,2048]{1,0:T(8,128)(2,1)S(1)} collective-permute-done((bf16[256,2048]{1,0:T(8,128)(2,1)}, bf16[256,2048]{1,0:T(8,128)(2,1)S(1)}, u32[]{:S(2)}, u32[]{:S(2)}) %collective-permute-start.11) | collective-permute-done | bytes 1048608 | tf_op jit(solution)/shard_map/ppermute | solution.py:57
  359.7 11.0 %collective-permute-done.19 = bf16[256,2048]{1,0:T(8,128)(2,1)S(1)} collective-permute-done((bf16[256,2048]{1,0:T(8,128)(2,1)S(1)}, bf16[256,2048]{1,0:T(8,128)(2,1)S(1)}, u32[]{:S(2)}, u32[]{:S(2)}) %collective-permute-start.19) | collective-permute-done | bytes 1048608 | tf_op jit(solution)/shard_map/ppermute | solution.py:79
  380.5 12.7 %collective-permute-done.12 = bf16[256,2048]{1,0:T(8,128)(2,1)S(1)} collective-permute-done((bf16[256,2048]{1,0:T(8,128)(2,1)S(1)}, bf16[256,2048]{1,0:T(8,128)(2,1)S(1)}, u32[]{:S(2)}, u32[]{:S(2)}) %collective-permute-start.12) | collective-permute-done | bytes 1048608 | tf_op jit(solution)/shard_map/ppermute | solution.py:57
  397.4 13.7 %convolution_convert_fusion = bf16[2048,2048]{1,0:T(8,128)(2,1)} fusion(bf16[1024,2048]{1,0:T(8,128)(2,1)} %get-tuple-element.28, bf16[256,2048]{1,0:T(8,128)(2,1)S(1)} %get-tuple-element.116, bf16[256,2048]{1,0:T(8,128)(2,1)S(1)} %copy-done.76, bf16[256,2048]{1,0:T(8,128)(2,1)S(1)} %copy-done.73, bf16[256,2048]{1,0:T(8,128)(2,1)S(1)} %copy-done.71), kind=kOutput, calls=%fused_computation.15 | convolution fusion | flops 8610906112 | bytes 16777216 | tf_op jit(solution)/shard_map/dot_general | solution.py:35
  445.1 14.4 %collective-permute-done.21 = bf16[256,2048]{1,0:T(8,128)(2,1)S(1)} collective-permute-done((bf16[256,2048]{1,0:T(8,128)(2,1)S(1)}, bf16[256,2048]{1,0:T(8,128)(2,1)S(1)}, u32[]{:S(2)}, u32[]{:S(2)}) %collective-permute-start.21) | collective-permute-done | bytes 1048608 | tf_op jit(solution)/shard_map/ppermute | solution.py:79
  479.6 14.1 %convolution_convert_fusion.1 = bf16[2048,2048]{1,0:T(8,128)(2,1)} fusion(bf16[256,2048]{1,0:T(8,128)(2,1)} %copy-done.67, bf16[256,2048]{1,0:T(8,128)(2,1)} %copy-done.66, bf16[256,2048]{1,0:T(8,128)(2,1)} %collective-permute-done.10, bf16[256,2048]{1,0:T(8,128)(2,1)} %copy-done.30, bf16[256,2048]{1,0:T(8,128)(2,1)} %copy-done.28, ...), kind=kOutput, calls=%fused_computation.16 | convolution fusion | flops 8627683328 | bytes 16777216 | tf_op jit(solution)/shard_map/dot_general | solution.py:35
  496.3 16.8 %attend_back.1 = (bf16[8,2,128,256]{3,2,1,0:T(8,128)(2,1)}, bf16[8,2,128,256]{3,2,1,0:T(8,128)(2,1)}) custom-call(s32[2]{0:T(128)} %dynamic_slice.272.lengths_ref, bf16[8,2,128,256]{3,2,1,0:T(8,128)(2,1)} %bitcast.383, bf16[8,2,128,256]{3,2,1,0:T(8,128)(2,1)} %bitcast.385, bf16[8,2,128,256]{3,2,1,0:T(8,128)(2,1)} %bitcast.73.grad_ref), custom_call_target="tpu_custom_call" | custom-call | flops 5368709120 | bytes 8388608 | tf_op jit(solution)/shard_map/attend_back/pallas_call | solution.py:411
  557.1 20.8 %collective-permute-done.23 = bf16[512,512]{1,0:T(8,128)(2,1)} collective-permute-done((bf16[512,512]{1,0:T(8,128)(2,1)}, bf16[512,512]{1,0:T(8,128)(2,1)}, u32[]{:S(2)}, u32[]{:S(2)}) %collective-permute-start.23) | collective-permute-done | bytes 524320 | tf_op jit(solution)/shard_map/ppermute | solution.py:79
  583.6 11.5 %collective-permute-done.24 = bf16[512,512]{1,0:T(8,128)(2,1)} collective-permute-done((bf16[512,512]{1,0:T(8,128)(2,1)}, bf16[512,512]{1,0:T(8,128)(2,1)}, u32[]{:S(2)}, u32[]{:S(2)}) %collective-permute-start.24) | collective-permute-done | bytes 524320 | tf_op jit(solution)/shard_map/ppermute | solution.py:79
  600.9 8.6 %fusion.43 = (f32[2048]{0:T(1024)S(1)}, f32[256]{0:T(256)S(1)}, f32[256]{0:T(256)S(1)}, f32[2048]{0:T(1024)S(1)}, f32[256,2048]{1,0:T(8,128)}) fusion(f32[256]{0:T(256)S(1)} %copy-done.46, f32[256]{0:T(256)S(1)} %copy-done.47, bf16[2,128,2048]{2,1,0:T(8,128)(2,1)S(1)} %copy-done.2, f32[2048]{0:T(1024)S(1)} %copy-done.41, f32[256,2048]{1,0:T(8,128)} %fusion.100, ...), kind=kOutput, calls=%fused_computation.80 | convolution fusion | flops 2153246208 | bytes 14708736 | tf_op jit(solution)/shard_map/dot_general | solution.py:31
  651.9 14.3 %collective-permute-done.38 = bf16[1,2,128,2048]{3,2,1,0:T(8,128)(2,1)S(1)} collective-permute-done((bf16[1,2,128,2048]{3,2,1,0:T(8,128)(2,1)S(1)}, bf16[1,2,128,2048]{3,2,1,0:T(8,128)(2,1)S(1)}, u32[]{:S(2)}, u32[]{:S(2)}) %collective-permute-start.38) | collective-permute-done | bytes 1048608 | tf_op jit(solution)/shard_map/ppermute | solution.py:96
  674.9 13.8 %collective-permute-done.30 = bf16[4,2,32,2048]{3,2,0,1:T(8,128)(2,1)S(1)} collective-permute-done((bf16[4,2,32,2048]{3,2,0,1:T(8,128)(2,1)S(1)}, bf16[4,2,32,2048]{3,2,0,1:T(8,128)(2,1)S(1)}, u32[]{:S(2)}, u32[]{:S(2)}) %collective-permute-start.30) | collective-permute-done | bytes 1048608 | tf_op jit(solution)/shard_map/ppermute | solution.py:96
  700.0 16.7 %collective-permute-done.31 = bf16[4,32,2048]{2,1,0:T(8,128)(2,1)S(1)} collective-permute-done((bf16[4,32,2048]{2,1,0:T(8,128)(2,1)S(1)}, bf16[4,32,2048]{2,1,0:T(8,128)(2,1)S(1)}, u32[]{:S(2)}, u32[]{:S(2)}) %collective-permute-start.31) | collective-permute-done | bytes 524320 | tf_op jit(solution)/shard_map/ppermute | solution.py:96
  729.4 11.7 %collective-permute-done.25 = bf16[64,2048]{1,0:T(8,128)(2,1)S(1)} collective-permute-done((bf16[64,2048]{1,0:T(8,128)(2,1)S(1)}, bf16[64,2048]{1,0:T(8,128)(2,1)S(1)}, u32[]{:S(2)}, u32[]{:S(2)}) %collective-permute-start.25) | collective-permute-done | bytes 262176 | tf_op jit(solution)/shard_map/ppermute | solution.py:79
  765.0 14.0 %collective-permute-done.28 = bf16[64,2048]{1,0:T(8,128)(2,1)S(1)} collective-permute-done((bf16[64,2048]{1,0:T(8,128)(2,1)S(1)}, bf16[64,2048]{1,0:T(8,128)(2,1)S(1)}, u32[]{:S(2)}, u32[]{:S(2)}) %collective-permute-start.28) | collective-permute-done | bytes 262176 | tf_op jit(solution)/shard_map/ppermute | solution.py:416
  (454 shorter events, 411.0 us)
Async XLA Ops:
  7.2 201.0 %all-gather.7.cloned.1.call-start = ((), (), s32[]{:S(2)}) async-start(), calls=%async_computation.7 | async-start | bytes 9437184 | tf_op jit(solution)/shard_map/all_gather | solution.py:273
  7.9 261.1 %all-gather.11.cloned.1.call-start = ((), (), s32[]{:S(2)}) async-start(), calls=%async_computation.9 | async-start | bytes 9437184 | tf_op jit(solution)/shard_map/all_gather | solution.py:315
  35.6 243.3 %all-gather.9.cloned.1.call-start = ((), (), s32[]{:S(2)}) async-start(), calls=%async_computation.8 | async-start | bytes 9437184 | tf_op jit(solution)/shard_map/all_gather | solution.py:312
  73.9 223.3 %all-gather.13.cloned.1.call-start = ((), (), s32[]{:S(2)}) async-start(), calls=%async_computation.10 | async-start | bytes 9437184 | tf_op jit(solution)/shard_map/all_gather | solution.py:321
  96.8 96.7 %all-to-all-start = ((bf16[32,72,256]{2,1,0:T(8,128)(2,1)}), bf16[32,72,256]{2,1,0:T(8,128)(2,1)S(1)}, u32[]{:S(2)}, u32[]{:S(2)}) async-start(bf16[32,72,256]{2,1,0:T(8,128)(2,1)} %broadcast_in_dim.209), calls=%async_computation | async-start | bytes 2359296 | tf_op jit(solution)/shard_map/all_to_all | solution.py:290
  102.3 498.6 %all-gather.15.cloned.1.call-start = ((), (), s32[]{:S(2)}) async-start(), calls=%async_computation.11 | async-start | bytes 9437184 | tf_op jit(solution)/shard_map/all_gather | solution.py:431
  103.7 52.8 %collective-permute-start.17 = (bf16[2,128,2048]{2,1,0:T(8,128)(2,1)}, bf16[2,128,2048]{2,1,0:T(8,128)(2,1)}, u32[]{:S(2)}, u32[]{:S(2)}) collective-permute-start(bf16[2,128,2048]{2,1,0:T(8,128)(2,1)} %collective-permute-done.16), channel_id=1, source_target_pairs={{0,8},{8,16},{16,24},{24,0},{1,9},{9,17},{17,25},{25,1},{2,10},{10... | collective-permute-start | bytes 3145736 | tf_op jit(solution)/shard_map/ppermute | solution.py:57
  112.8 44.3 %collective-permute-start = (bf16[512,256]{1,0:T(8,128)(2,1)S(1)}, bf16[512,256]{1,0:T(8,128)(2,1)}, u32[]{:S(2)}, u32[]{:S(2)}) collective-permute-start(bf16[512,256]{1,0:T(8,128)(2,1)S(1)} %bitcast.360), channel_id=1, source_target_pairs={{0,8},{8,16},{16,24},{24,0},{1,9},{9,17},{17,25},{25,1},{2,10},{10... | collective-permute-start | bytes 786440 | tf_op jit(solution)/shard_map/ppermute | solution.py:49
  153.1 39.3 %collective-permute-start.1 = (bf16[512,256]{1,0:T(8,128)(2,1)S(1)}, bf16[512,256]{1,0:T(8,128)(2,1)S(1)}, u32[]{:S(2)}, u32[]{:S(2)}) collective-permute-start(bf16[512,256]{1,0:T(8,128)(2,1)S(1)} %bitcast.361), channel_id=1, source_target_pairs={{0,16},{8,24},{16,0},{24,8},{1,17},{9,25},{17,1},{25,9},{2,18},{10... | collective-permute-start | bytes 786440 | tf_op jit(solution)/shard_map/ppermute | solution.py:49
  154.2 38.3 %collective-permute-start.2 = (bf16[512,256]{1,0:T(8,128)(2,1)S(1)}, bf16[512,256]{1,0:T(8,128)(2,1)S(1)}, u32[]{:S(2)}, u32[]{:S(2)}) collective-permute-start(bf16[512,256]{1,0:T(8,128)(2,1)S(1)} %bitcast.362), channel_id=1, source_target_pairs={{0,24},{8,0},{16,8},{24,16},{1,25},{9,1},{17,9},{25,17},{2,26},{10... | collective-permute-start | bytes 786440 | tf_op jit(solution)/shard_map/ppermute | solution.py:49
  156.6 38.7 %collective-permute-start.18 = (bf16[2,128,2048]{2,1,0:T(8,128)(2,1)}, bf16[2,128,2048]{2,1,0:T(8,128)(2,1)}, u32[]{:S(2)}, u32[]{:S(2)}) collective-permute-start(bf16[2,128,2048]{2,1,0:T(8,128)(2,1)} %collective-permute-done.17), channel_id=1, source_target_pairs={{0,8},{8,16},{16,24},{24,0},{1,9},{9,17},{17,25},{25,1},{2,10},{10... | collective-permute-start | bytes 3145736 | tf_op jit(solution)/shard_map/ppermute | solution.py:57
  239.6 38.0 %all-to-all-start.2 = ((bf16[8,2,128,256]{3,2,1,0:T(8,128)(2,1)}), bf16[8,2,128,256]{3,2,1,0:T(8,128)(2,1)S(1)}, u32[]{:S(2)}, u32[]{:S(2)}) async-start(bf16[8,2,128,256]{3,2,1,0:T(8,128)(2,1)} %attend.1), calls=%async_computation.2 | async-start | bytes 2097152 | tf_op jit(solution)/shard_map/all_to_all | solution.py:351
  352.1 41.1 %collective-permute-start.12 = (bf16[256,2048]{1,0:T(8,128)(2,1)S(1)}, bf16[256,2048]{1,0:T(8,128)(2,1)S(1)}, u32[]{:S(2)}, u32[]{:S(2)}) collective-permute-start(bf16[256,2048]{1,0:T(8,128)(2,1)S(1)} %collective-permute-done.11), channel_id=1, source_target_pairs={{0,8},{8,16},{16,24},{24,0},{1,9},{9,17},{17,25},{25,1},{2,10},{10... | collective-permute-start | bytes 3145736 | tf_op jit(solution)/shard_map/ppermute | solution.py:57
  374.2 58.6 %collective-permute-start.20 = (bf16[256,2048]{1,0:T(8,128)(2,1)}, bf16[256,2048]{1,0:T(8,128)(2,1)S(1)}, u32[]{:S(2)}, u32[]{:S(2)}) collective-permute-start(bf16[256,2048]{1,0:T(8,128)(2,1)} %add_convert_fusion.1), channel_id=1, source_target_pairs={{0,8},{8,16},{16,24},{24,0},{1,9},{9,17},{17,25},{25,1},{2,10},{10... | collective-permute-start | bytes 3145736 | tf_op jit(solution)/shard_map/ppermute | solution.py:79
  420.3 214.9 %collective-permute-start.37 = (bf16[1,2,2,2,128,2048]{5,4,2,3,1,0:T(8,128)(2,1)}, bf16[1,2,2,2,128,2048]{5,4,2,3,1,0:T(8,128)(2,1)}, u32[]{:S(2)}, u32[]{:S(2)}) collective-permute-start(bf16[1,2,2,2,128,2048]{5,4,2,3,1,0:T(8,128)(2,1)} %bitcast.307), channel_id=1, source_target_pairs={{0,1},{1,0},{2,3},{3,2},{4,5},{5,4},{6,7},{7,6},{8,9},{9,8},{10,11... | collective-permute-start | bytes 12582920 | tf_op jit(solution)/shard_map/ppermute | solution.py:96
  444.6 49.1 %collective-permute-start.13 = (bf16[2,128,2048]{2,1,0:T(8,128)(2,1)}, bf16[2,128,2048]{2,1,0:T(8,128)(2,1)}, u32[]{:S(2)}, u32[]{:S(2)}) collective-permute-start(bf16[2,128,2048]{2,1,0:T(8,128)(2,1)} %pad_maximum_fusion.3), channel_id=1, source_target_pairs={{0,8},{8,16},{16,24},{24,0},{1,9},{9,17},{17,25},{25,1},{2,10},{10... | collective-permute-start | bytes 3145736 | tf_op jit(solution)/shard_map/ppermute | solution.py:79
  479.1 243.1 %all-gather.17.cloned.1.call-start = ((), (), s32[]{:S(2)}) async-start(), calls=%async_computation.12 | async-start | bytes 9437184 | tf_op jit(solution)/shard_map/all_gather | solution.py:412
  496.3 39.5 %collective-permute-start.14 = (bf16[2,128,2048]{2,1,0:T(8,128)(2,1)}, bf16[2,128,2048]{2,1,0:T(8,128)(2,1)}, u32[]{:S(2)}, u32[]{:S(2)}) collective-permute-start(bf16[2,128,2048]{2,1,0:T(8,128)(2,1)} %fusion.50), channel_id=1, source_target_pairs={{0,8},{8,16},{16,24},{24,0},{1,9},{9,17},{17,25},{25,1},{2,10},{10... | collective-permute-start | bytes 3145736 | tf_op jit(solution)/shard_map/ppermute | solution.py:79
  531.6 65.9 %all-to-all-start.4 = ((bf16[8,256,512]{1,2,0:T(8,128)(2,1)}), bf16[8,256,512]{1,2,0:T(8,128)(2,1)S(1)}, u32[]{:S(2)}, u32[]{:S(2)}) async-start(bf16[8,256,512]{1,2,0:T(8,128)(2,1)} %copy.114), calls=%async_computation.4 | async-start | bytes 4194304 | tf_op jit(solution)/shard_map/all_to_all | solution.py:432
  539.3 41.5 %collective-permute-start.15 = (bf16[2,128,2048]{2,1,0:T(8,128)(2,1)}, bf16[2,128,2048]{2,1,0:T(8,128)(2,1)}, u32[]{:S(2)}, u32[]{:S(2)}) collective-permute-start(bf16[2,128,2048]{2,1,0:T(8,128)(2,1)} %fusion.49), channel_id=1, source_target_pairs={{0,8},{8,16},{16,24},{24,0},{1,9},{9,17},{17,25},{25,1},{2,10},{10... | collective-permute-start | bytes 3145736 | tf_op jit(solution)/shard_map/ppermute | solution.py:79
  555.1 88.9 %collective-permute-start.29 = (bf16[4,2,2,2,32,2048]{5,4,0,2,3,1:T(8,128)(2,1)}, bf16[4,2,2,2,32,2048]{5,4,0,2,3,1:T(8,128)(2,1)}, u32[]{:S(2)}, u32[]{:S(2)}) collective-permute-start(bf16[4,2,2,2,32,2048]{5,4,0,2,3,1:T(8,128)(2,1)} %bitcast.308), channel_id=1, source_target_pairs={{0,1},{1,0},{2,3},{3,2},{4,5},{5,4},{6,7},{7,6},{8,9},{9,8},{10,11... | collective-permute-start | bytes 12582920 | tf_op jit(solution)/shard_map/ppermute | solution.py:96
  648.9 45.4 %collective-permute-start.40 = (bf16[1,2,128,2048]{3,2,1,0:T(8,128)(2,1)S(1)}, bf16[1,2,128,2048]{3,2,1,0:T(8,128)(2,1)S(1)}, u32[]{:S(2)}, u32[]{:S(2)}) collective-permute-start(bf16[1,2,128,2048]{3,2,1,0:T(8,128)(2,1)S(1)} %dynamic-slice_bitcast_fusion), channel_id=1, source_target_pairs={{0,4},{1,5},{2,6},{3,7},{4,0},{5,1},{6,2},{7,3},{8,12},{9,13},{10,... | collective-permute-start | bytes 3145736 | tf_op jit(solution)/shard_map/ppermute | solution.py:96
  650.4 38.2 %collective-permute-start.30 = (bf16[4,2,32,2048]{3,2,0,1:T(8,128)(2,1)S(1)}, bf16[4,2,32,2048]{3,2,0,1:T(8,128)(2,1)S(1)}, u32[]{:S(2)}, u32[]{:S(2)}) collective-permute-start(bf16[4,2,32,2048]{3,2,0,1:T(8,128)(2,1)S(1)} %dynamic-slice_bitcast_fusion.3), channel_id=1, source_target_pairs={{0,2},{1,3},{2,0},{3,1},{4,6},{5,7},{6,4},{7,5},{8,10},{9,11},{10,... | collective-permute-start | bytes 3145736 | tf_op jit(solution)/shard_map/ppermute | solution.py:96
  666.6 53.8 %collective-permute-start.39 = (bf16[1,128,2048]{2,1,0:T(8,128)(2,1)S(1)}, bf16[1,128,2048]{2,1,0:T(8,128)(2,1)S(1)}, u32[]{:S(2)}, u32[]{:S(2)}) collective-permute-start(bf16[1,128,2048]{2,1,0:T(8,128)(2,1)S(1)} %dynamic-slice_bitcast_fusion.5), channel_id=1, source_target_pairs={{0,4},{1,5},{2,6},{3,7},{4,0},{5,1},{6,2},{7,3},{8,12},{9,13},{10,... | collective-permute-start | bytes 1572872 | tf_op jit(solution)/shard_map/ppermute | solution.py:96
  (112 other events, 1730.5 us)
Sparse Core Ops, SparseCore 0:
  9.9 58.2 all-gather.6
  70.1 70.8 all-gather.10
  143.5 55.4 all-gather.8
  200.7 57.6 all-gather.12
  260.2 63.7 all-gather.14
  527.8 77.6 all-gather.16

commit v3 on v1

--- a/solution.py
+++ b/solution.py
@@ -37,31 +37,98 @@
     )
 
 
-def ring(count):
-    return [(i, (i + 1) % count) for i in range(count)]
-
-
-def ring_gather(piece, count):
-    me = lax.axis_index("dp")
-    whole = jnp.zeros((count,) + piece.shape, piece.dtype)
-    whole = lax.dynamic_update_index_in_dim(whole, piece, me, 0)
-    moving = piece
-    for step in range(1, count):
-        moving = lax.ppermute(moving, "dp", ring(count))
-        whole = lax.dynamic_update_index_in_dim(whole, moving, (me - step) % count, 0)
+def shift(count, by):
+    return [(i, (i + by) % count) for i in range(count)]
+
+
+def count_of(values):
+    return lax.convert_element_type(values, jnp.uint32)
+
+
+def turned(me, count):
+    turns = lax.rem(me + jnp.asarray([count - by for by in range(count)], jnp.uint32), count_of(count))
+    return [turns[by] for by in range(count)]
+
+
+def pick(values, at, axis=0):
+    return lax.dynamic_index_in_dim(values, at, axis, keepdims=False)
+
+
+def after(value, *gates):
+    return lax.optimization_barrier((value,) + gates)[0]
+
+
+def gather_parts(piece, behind):
+    count = len(behind)
+    whole = [piece]
+    for by in range(1, count):
+        whole.append(lax.ppermute(piece, "dp", shift(count, by)))
+    return in_order(whole, behind)
+
+
+def in_order(pieces, behind):
+    whole = jnp.zeros((len(pieces),) + pieces[0].shape, pieces[0].dtype)
+    for piece, at in zip(pieces, behind):
+        whole = lax.dynamic_update_index_in_dim(whole, piece, at, 0)
     return whole
 
 
-def ring_scatter(parts, count):
-    me = lax.axis_index("dp")
+def ring_pieces(piece, steps, count):
+    pieces = [piece]
+    for step in range(1, steps):
+        pieces.append(lax.ppermute(pieces[-1], "dp", shift(count, 1)))
+    return pieces
+
+
+def strip_routes(parts, ranks, by):
+    return [(r, (r % parts + by) % parts * ranks + r // parts) for r in range(parts * ranks)]
+
+
+def deal_strips(piece_for, ranks, behind, gates=()):
+    parts = len(behind)
+    moved = []
+    for by in range(parts):
+        routes = strip_routes(parts, ranks, by)
+        moved.append(after(lax.ppermute(piece_for(by), BOTH, routes), *gates))
+    moved = in_order(moved, behind)
+    return moved.reshape((-1,) + moved.shape[2:])
+
+
+def exchange_parts(pieces, ahead, behind, gates):
+    count = len(behind)
+    size = pieces.shape[2]
+    moved = [pick(pieces, ahead[0])]
+    for by in range(1, count):
+        moved.append(after(lax.ppermute(pick(pieces, ahead[by]), "dp", shift(count, by)), *gates))
+    whole = jnp.zeros((pieces.shape[1], count * size), pieces.dtype)
+    for piece, at in zip(moved, behind):
+        whole = lax.dynamic_update_slice_in_dim(whole, piece, at * count_of(size), 1)
+    return whole
+
+
+def ring_sum(part_for, count, gates=()):
     moving = None
+    sent = ()
     for step in range(count):
-        mine = lax.dynamic_index_in_dim(parts, (me - 1 - step) % count, 0, keepdims=False)
-        mine = mine.astype(f32)
-        total = mine if moving is None else mine + moving.astype(f32)
+        total = part_for((1 + step) % count, sent)
+        if moving is not None:
+            gate = gates[step - 1]() if step <= len(gates) else ()
+            if gate:
+                moving = after(moving, *gate)
+            total = total + moving.astype(f32)
         if step < count - 1:
-            moving = lax.ppermute(total.astype(bf16), "dp", ring(count))
+            sent = (total.astype(bf16),)
+            moving = lax.ppermute(sent[0], "dp", shift(count, 1))
     return total
+
+
+def ring_scatter(parts, behind, gates=(), all_sent=None):
+    def part_for(by, sent):
+        if all_sent is not None:
+            all_sent.extend(sent)
+        return pick(parts, behind[by]).astype(f32)
+
+    return ring_sum(part_for, len(behind), gates)
 
 
 def block_probs(query, key, limit, scale):
@@ -210,13 +277,38 @@
     head_cols = width // ranks
     strip = w_query.shape[0]
     hidden_strip = w_contract.shape[0]
-    hidden_cols = parts * hidden_strip
-    owner = lax.axis_index("dp")
-    rank = lax.axis_index("seq")
-    seq_ids = jnp.arange(lengths.shape[0], dtype=jnp.int32)
-    own_length = lax.dynamic_slice_in_dim(lengths, owner * micro, micro)
-    place = rank * block + jnp.arange(block, dtype=jnp.int32)
-    valid = (place[None, :] < own_length[:, None]).astype(f32).reshape(rows, 1)
+    hidden_cols = ranks * hidden_strip
+    owner = count_of(lax.axis_index("dp"))
+    rank = count_of(lax.axis_index("seq"))
+    behind = turned(owner, parts)
+    ahead = behind[:1] + behind[:0:-1]
+    strip_at = lax.rem(owner * count_of(ranks) + rank, count_of(parts))
+    strip_steps = lax.rem(strip_at + jnp.arange(parts, dtype=jnp.uint32), count_of(parts))
+    own_length = lax.dynamic_slice_in_dim(lengths, owner * count_of(micro), micro)
+    place = lax.axis_index("seq") * block + jnp.arange(block, dtype=jnp.int32)
+
+    seqs = jnp.arange(parts * micro, dtype=jnp.uint32)
+    steps = jnp.asarray([k // micro for k in range(parts * micro)], jnp.uint32)
+    inner = jnp.asarray([k % micro for k in range(parts * micro)], jnp.uint32)
+
+    def member(back):
+        return lax.rem(owner + count_of(parts) - back, count_of(parts))
+
+    def look_up(table, at):
+        return jnp.sum(jnp.where(at[:, None] == seqs[None, :], table[None, :], 0), axis=1)
+
+    order = count_of(owner_order)
+    held = member(steps) * count_of(micro) + inner
+    slots = jnp.sum(jnp.where(held[:, None] == order[None, :], seqs[None, :], 0), axis=1)
+    slot_step = member(lax.div(count_of(slots), count_of(micro)))
+    slot_at = slot_step * count_of(micro) + lax.rem(count_of(slots), count_of(micro))
+    held_lengths = look_up(lengths, held)
+    wanted = count_of(look_up(order, held))
+    wanted_step = member(lax.div(wanted, count_of(micro)))
+    wanted_inner = lax.rem(wanted, count_of(micro))
+    wanted_at = wanted_step * count_of(micro) + wanted_inner
+    wanted_steps = lax.optimization_barrier([wanted_step[k] for k in range(parts * micro)])
+    wanted_lengths = look_up(lengths, wanted)[:micro]
 
     tokens_all = lax.all_gather(tokens.reshape(rows, width), "seq", axis=0, tiled=True)
     smalls = [
@@ -231,10 +323,13 @@
         b_value,
     ]
     lengths_of = [item.shape[0] for item in smalls]
-    pad = -sum(lengths_of) % (2 * head_size)
+    pad = -sum(lengths_of) % (16 * head_size)
     packed = jnp.concatenate(smalls + [jnp.zeros((pad,), bf16)]).reshape(-1, 2 * head_size)
     packed = jnp.concatenate([w_keyval, packed], axis=0)
-    packed = lax.all_gather(packed, BOTH, axis=0, tiled=False)
+    packed = gather_parts(packed, behind)
+    packed = jnp.broadcast_to(packed[None], (ranks,) + packed.shape)
+    packed = lax.all_to_all(packed, "seq", 0, 0).transpose(1, 0, 2, 3)
+    packed = packed.reshape((every,) + packed.shape[2:])
     keyval_weight = packed[:, :strip].reshape(width, 2 * head_size)
     packed = packed[:, strip:].reshape(every, -1)
     whole = []
@@ -245,118 +340,176 @@
     gain_one, bias_one, query_bias, out_bias, gain_two, bias_two, contract_bias = [
         item.reshape(1, width) for item in whole[:7]
     ]
-    expand_bias = lax.dynamic_index_in_dim(
-        whole[7].reshape(parts, ranks, hidden_strip), rank, 1, keepdims=False
-    ).reshape(1, hidden_cols)
+    expand_bias = pick(whole[7].reshape(parts, ranks, -1), owner)
+    expand_bias = expand_bias.reshape(1, hidden_cols)
     value_bias = whole[8].reshape(1, head_size)
-    query_bias = lax.dynamic_slice_in_dim(query_bias, rank * head_cols, head_cols, axis=1)
+    query_bias = pick(query_bias.reshape(ranks, 1, head_cols), rank)
     keyval_bias = jnp.concatenate([jnp.zeros_like(value_bias), value_bias], axis=1)
 
-    sent = jnp.concatenate(
-        [
-            w_query.reshape(strip, ranks, head_cols).transpose(1, 0, 2),
-            w_expand.reshape(strip, parts, ranks, hidden_strip)
-            .transpose(2, 0, 1, 3)
-            .reshape(ranks, strip, hidden_cols),
-        ],
-        axis=2,
-    )
-    sent = lax.all_to_all(sent, "seq", 0, 0).reshape(ranks * strip, head_cols + hidden_cols)
-    query_weight = ring_gather(sent[:, :head_cols], parts).reshape(width, head_cols)
-    moved = [(f, (f % parts) * ranks + f // parts) for f in range(every)]
-    out_weight = ring_gather(lax.ppermute(w_out, BOTH, moved), parts)
-    out_weight = lax.all_gather(out_weight.reshape(head_cols, width), "seq", axis=0, tiled=True)
-    cotangent_all = ring_gather(cotangent, parts).reshape(-1, block, width)
-    expand_weight = ring_gather(sent[:, head_cols:], parts).reshape(width, hidden_cols)
-    contract_weight = ring_gather(w_contract, parts).reshape(hidden_cols, width)
-
-    mine = owner * micro + jnp.arange(micro, dtype=jnp.int32)
-    slots = jnp.sum(jnp.where(owner_order[None, :] == mine[:, None], seq_ids[None, :], 0), axis=1)
-    grad_y = jnp.stack(
-        [lax.dynamic_index_in_dim(cotangent_all, slots[i], 0, keepdims=False) for i in range(micro)]
-    )
-    grad_y = grad_y.reshape(rows, width).astype(f32) * valid
-    grad_m = grad_y.astype(bf16)
-    grad_m_all = lax.all_gather(grad_m, "seq", axis=0, tiled=True)
+    sent = w_query.reshape(strip, ranks, head_cols).transpose(1, 0, 2)
+    sent = lax.all_to_all(sent, "seq", 0, 0).reshape(ranks * strip, head_cols)
+    query_weight = gather_parts(sent, behind).reshape(width, head_cols)
+    cotangents = ring_pieces(after(cotangent, query_weight, keyval_weight), parts, parts)
+    out_strip = after(w_out, query_weight, keyval_weight)
+    out_rows = deal_strips(lambda by: out_strip, ranks, behind)
+    out_weight = lax.all_gather(after(out_rows, tokens_all), "seq", axis=0, tiled=True)
 
     head_shape = (ranks, micro, block, head_cols)
     attend, attend_back = attention_calls(head_shape, head_size, 2 * block)
-    normed_all, unused_std = norm_rows(tokens_all.astype(f32))
-    normed_in_all = (normed_all * gain_one + bias_one).astype(bf16)
+    normed_all, unused_std = norm_rows(after(tokens_all, out_rows).astype(f32))
+    normed_in_all = after((normed_all * gain_one + bias_one).astype(bf16))
     query = (dot(normed_in_all, query_weight) + query_bias).astype(bf16)
     keyval = (dot(normed_in_all, keyval_weight) + keyval_bias).astype(bf16)
-    query = query.reshape(head_shape)
+    query = after(query, cotangents[1]).reshape(head_shape)
     keyval = keyval.reshape(ranks, micro, block, 2 * head_size)
     mixed = attend(own_length, query, keyval)
-    mixed_rows = lax.all_to_all(mixed, "seq", 0, 0).reshape(ranks, rows, head_cols)
+    expand_strip = after(w_expand, query, keyval, out_rows)
+
+    def expand_piece(by):
+        at = strip_steps[by] * count_of(hidden_cols)
+        return lax.dynamic_slice_in_dim(expand_strip, at, hidden_cols, axis=1)
+
+    expand_rows = deal_strips(expand_piece, ranks, behind, (mixed,))
+    mixed_rows = lax.all_to_all(after(mixed, cotangents[2]), "seq", 0, 0)
+    mixed_rows = after(mixed_rows, *cotangents[3:])
+    mixed_rows = mixed_rows.reshape(ranks, rows, head_cols)
     mixed_rows = mixed_rows.transpose(1, 0, 2).reshape(rows, width)
-
+    expand_weight = lax.all_gather(after(expand_rows, mixed_rows), "seq", axis=0, tiled=True)
     hidden = tokens.reshape(rows, width).astype(f32)
     resid = hidden + dot(mixed_rows, out_weight) + out_bias
     normed2, inv_std2 = norm_rows(resid)
     normed2_in = (normed2 * gain_two + bias_two).astype(bf16)
-    normed2_all = lax.all_gather(normed2_in, "seq", axis=0, tiled=True)
-
-    preact = dot(normed2_all, expand_weight) + expand_bias
-    active, slope = gelu_parts(preact)
-    active = active.astype(bf16)
-    grad_active = dot_general(grad_m_all, contract_weight, (1,), (1,))
-    grad_pre = (grad_active * slope).astype(bf16)
-    grad_c = dot_general(grad_pre, expand_weight, (1,), (1,)).astype(bf16)
-    grad_c = lax.psum_scatter(grad_c, "seq", scatter_dimension=0, tiled=True).astype(f32)
-    output = dot(active, contract_weight).astype(bf16)
-    output = lax.psum_scatter(output, "seq", scatter_dimension=0, tiled=True).astype(f32)
-    result = (valid * (resid + output + contract_bias)).astype(bf16)
-    result_all = ring_gather(result.reshape(micro, block, width), parts).reshape(-1, block, width)
-    wanted = lax.dynamic_slice_in_dim(owner_order, owner * micro, micro)
-    result = jnp.stack(
-        [lax.dynamic_index_in_dim(result_all, wanted[i], 0, keepdims=False) for i in range(micro)]
-    )
-    grad_contract = dot_general(active, grad_m_all, (0,), (0,))
-    grad_contract = ring_scatter(grad_contract.reshape(parts, hidden_strip, width), parts)
-    grad_expand = dot_general(normed2_all, grad_pre, (0,), (0,))
-    grad_expand = ring_scatter(
-        grad_expand.reshape(parts, ranks * strip, hidden_cols), parts
-    ).astype(bf16)
-    grad_expand = lax.all_to_all(grad_expand.reshape(ranks, strip, hidden_cols), "seq", 0, 0)
-    grad_expand = (
-        grad_expand.reshape(ranks, strip, parts, hidden_strip)
-        .transpose(1, 2, 0, 3)
-        .reshape(strip, every * hidden_strip)
-        .astype(f32)
-    )
+    cotangents = jnp.stack(cotangents).reshape(-1, block, width)
+    inside = place[None, :, None] < held_lengths[:, None, None]
+
+    def grad_of(by):
+        taken = []
+        for at in range(by * micro, (by + 1) * micro):
+            piece = pick(cotangents, slot_at[at])
+            taken.append(jnp.where(inside[at], piece, jnp.zeros_like(piece)))
+        return jnp.concatenate(taken, axis=0)
+
+    grad_ms = [grad_of(by) for by in range(parts)]
+    grad_y = grad_ms[0].astype(f32)
+
+    normed2_ins = ring_pieces(normed2_in, parts, parts)
+    expand_weight = after(expand_weight, *normed2_ins[1:3])
+    actives = [None] * parts
+    slopes = [None] * parts
+    grad_pres = [None] * parts
+
+    for by in range(parts):
+        preact = dot(normed2_ins[by], expand_weight) + expand_bias
+        active, slopes[by] = gelu_parts(preact)
+        actives[by] = active.astype(bf16)
+    contract_weight = lax.all_gather(after(w_contract, expand_weight), "seq", axis=0, tiled=True)
+    active_all = jnp.concatenate(actives, axis=0)
+    grad_m_all = jnp.concatenate(grad_ms, axis=0)
+    grad_contract = dot_general(active_all, grad_m_all, (0,), (0,)).astype(bf16)
+    grad_contract_all = grad_contract
+
+    def grad_c_for(by, sent):
+        sums_c.extend(sent)
+        grad_active = dot_general(grad_ms[by], contract_weight, (1,), (1,))
+        grad_pres[by] = (grad_active * slopes[by]).astype(bf16)
+        return dot_general(grad_pres[by], expand_weight, (1,), (1,))
+
+    outputs = [None] * parts
+
+    def output_of(by):
+        outputs[by] = dot(actives[by], contract_weight).astype(bf16)
+        return outputs[by]
+
+    gates = (
+        lambda: [grad_contract_all],
+        lambda: [output_of(1)],
+        lambda: [output_of(2)],
+    )
+    sums_c = []
+    grad_c = ring_sum(grad_c_for, parts, gates)
+    query_weight_all = after(query_weight.T, grad_pres[1])
+    query_weight_all = lax.all_gather(query_weight_all, "seq", axis=0, tiled=True)
+    grad_contract = after(grad_contract_all, sums_c[-1], query_weight_all)
+    grad_contract = lax.psum_scatter(grad_contract, "seq", scatter_dimension=0, tiled=True)
+    for by in range(parts):
+        if outputs[by] is None:
+            output_of(by)
+    outputs = jnp.stack(outputs).reshape(parts * micro, block, width)
+    resid_rows = resid.reshape(micro, block, width)
+
+    def output_for(by, sent):
+        taken = []
+        for at in range(by * micro, (by + 1) * micro):
+            own = jnp.where(wanted_steps[at] == 0, pick(resid_rows, wanted_inner[at]), 0.0)
+            taken.append(pick(outputs, wanted_at[at]).astype(f32) + own)
+        return jnp.stack(taken)
+
+
+    grad_pre_all = jnp.concatenate(grad_pres, axis=0)
+    normed2_all = jnp.concatenate(normed2_ins, axis=0)
+
+    def grad_expand(grads):
+        grads = dot_general(normed2_all, grads, (0,), (0,)).astype(bf16)
+        grads = grads.reshape(parts, ranks, strip, hidden_cols).transpose(1, 0, 2, 3)
+        return grads.reshape(width, hidden_cols)
 
     grad_resid = grad_y + norm_back(grad_c * gain_two, normed2, inv_std2)
     grad_branch = grad_resid.astype(bf16)
     grad_mixed = dot_general(grad_branch, out_weight, (1,), (1,)).astype(bf16)
     grad_mixed = grad_mixed.reshape(rows, ranks, head_cols).transpose(1, 0, 2)
     grad_mixed = lax.all_to_all(grad_mixed, "seq", 0, 0).reshape(head_shape)
+    first_output = output_for(1, ()).astype(bf16)
+    grad_mixed = after(grad_mixed, first_output)
     grad_query, grad_keyval = attend_back(own_length, query, keyval, grad_mixed)
-    grad_branch_all = lax.all_gather(grad_branch, "seq", axis=0, tiled=True)
+    grad_branch_all = after(grad_branch, grad_mixed, grad_contract)
+    grad_branch_all = lax.all_gather(grad_branch_all, "seq", axis=0, tiled=True)
+
+    both = jnp.concatenate([grad_query, grad_keyval], axis=3)
+    both_rows = lax.all_to_all(both.reshape(ranks, rows, -1), "seq", 0, 0)
+    moved = after(lax.ppermute(first_output, "dp", shift(parts, 1)), grad_query)
+    result = output_for(2, ()) + moved.astype(f32)
+    second = result
+    moved = lax.ppermute(result.astype(bf16), "dp", shift(parts, 1))
+    result = output_for(3, ()) + moved.astype(f32)
+    both_rows = after(both_rows, result)
+    grad_branch_all = after(grad_branch_all, both_rows)
+    grad_expand_all = grad_expand(after(grad_pre_all, second))
+    grad_expand = after(grad_expand_all, grad_branch_all)
+    grad_expand = lax.psum_scatter(grad_expand, "seq", scatter_dimension=0, tiled=True)
+    both = both.reshape(all_rows, -1)
+    grad_query_rows = both_rows[:, :, :head_cols].transpose(1, 0, 2).reshape(rows, width)
+    grad_keyval_rows = jnp.sum(both_rows[:, :, head_cols:].astype(f32), axis=0).astype(bf16)
+    grad_in = dot(grad_query_rows, query_weight_all)
+    grad_in = grad_in + dot_general(grad_keyval_rows, keyval_weight, (1,), (1,))
+    grad_in_weight = after(dot_general(normed_in_all, both, (0,), (0,)))
+    grad_in_weight = grad_in_weight.reshape(parts, ranks * strip, both.shape[1])
     grad_out = dot_general(mixed.reshape(all_rows, head_cols), grad_branch_all, (0,), (0,))
-    grad_out = ring_scatter(grad_out.reshape(parts, head_cols // parts, width), parts)
+    grad_out = grad_out.reshape(parts, head_cols // parts, width)
+    sums_out = []
+    grad_out = ring_scatter(grad_out, behind, [lambda: [grad_in]], sums_out)
+    grad_expand = grad_expand.reshape(parts, strip, hidden_cols)
+    grad_expand = exchange_parts(grad_expand, ahead, behind, (grad_in,))
+    gates = [lambda: [grad_in], lambda: [sums_out[0]]]
+    gates += [lambda: []] * (parts - 4) + [lambda: [grad_expand]]
+    grad_in_weight = ring_scatter(grad_in_weight, behind, gates).astype(bf16)
+    grad_in_weight = lax.all_to_all(
+        grad_in_weight.reshape(ranks, strip, both.shape[1]), "seq", 0, 0
+    )
+    grad_query_weight = (
+        grad_in_weight[:, :, :head_cols].transpose(1, 0, 2).reshape(strip, width).astype(f32)
+    )
+    grad_keyval_weight = jnp.sum(grad_in_weight[:, :, head_cols:].astype(f32), axis=0)
+
     back = [(d * ranks + s, s * parts + d) for d in range(parts) for s in range(ranks)]
     grad_out = lax.ppermute(grad_out.astype(bf16), BOTH, back).astype(f32)
 
-    both = jnp.concatenate([grad_query, grad_keyval], axis=3).reshape(all_rows, -1)
-    grad_in_weight = dot_general(normed_in_all, both, (0,), (0,))
-    grad_in_weight = ring_scatter(
-        grad_in_weight.reshape(parts, ranks * strip, both.shape[1]), parts
-    ).astype(bf16)
-    grad_in_weight = lax.all_to_all(
-        grad_in_weight.reshape(ranks, strip, both.shape[1]), "seq", 0, 0
-    )
-    grad_query_weight = (
-        grad_in_weight[:, :, :head_cols].transpose(1, 0, 2).reshape(strip, width).astype(f32)
-    )
-    grad_keyval_weight = jnp.sum(grad_in_weight[:, :, head_cols:].astype(f32), axis=0)
-
-    query_weight_all = lax.all_gather(query_weight, "seq", axis=0, tiled=False)
-    both = lax.all_to_all(both.reshape(ranks, rows, -1), "seq", 0, 0)
-    grad_query_rows = both[:, :, :head_cols]
-    grad_keyval_rows = jnp.sum(both[:, :, head_cols:].astype(f32), axis=0).astype(bf16)
-    grad_in = dot_general(grad_query_rows, query_weight_all, (0, 2), (0, 2))
-    grad_in = grad_in + dot_general(grad_keyval_rows, keyval_weight, (1,), (1,))
+    for step in range(4, parts + 1):
+        moved = after(lax.ppermute(result.astype(bf16), "dp", shift(parts, 1)), grad_in)
+        result = output_for(step % parts, ()) + moved.astype(f32)
+        if step == 4:
+            third = result
+    held_valid = (place[None, :] < wanted_lengths[:, None])[:, :, None]
+    result = jnp.where(held_valid, result + contract_bias, 0.0).astype(bf16)
     normed, inv_std = norm_rows(hidden)
     grad_tokens = grad_resid + norm_back(grad_in * gain_one, normed, inv_std)
 
@@ -366,24 +519,24 @@
     def column_sum(values):
         return jnp.sum(values.astype(f32), axis=0)
 
-    expand_sum = column_sum(grad_pre).reshape(parts, 1, hidden_strip)
-    here = jnp.arange(ranks, dtype=jnp.int32)[None, :, None] == rank
+    expand_sum = column_sum(grad_pre_all).reshape(1, ranks, hidden_strip)
+    here = jnp.arange(parts, dtype=jnp.uint32)[:, None, None] == owner
     expand_sum = jnp.where(here, expand_sum, 0.0).reshape(every, hidden_strip)
     sums = jnp.concatenate(
         [
             spread(column_sum(grad_in * normed)),
             spread(column_sum(grad_in)),
-            spread(column_sum(grad_query_rows.transpose(1, 0, 2).reshape(rows, width))),
+            spread(column_sum(grad_query_rows)),
             spread(column_sum(grad_branch)),
             spread(column_sum(grad_c * normed2)),
             spread(column_sum(grad_c)),
-            spread(column_sum(grad_m)),
+            spread(column_sum(grad_y)),
             expand_sum,
             spread(column_sum(grad_keyval_rows)[head_size:]),
         ],
         axis=1,
     )
-    sums = lax.psum_scatter(sums, BOTH, scatter_dimension=0, tiled=True).reshape(-1)
+    sums = jnp.sum(after(lax.all_to_all(sums, BOTH, 0, 0), grad_in_weight, third), axis=0)
     small_grads = []
     at = 0
     for count in lengths_of:
@@ -402,9 +555,9 @@
         small_grads[3],
         small_grads[4],
         small_grads[5],
-        grad_expand,
+        grad_expand.astype(f32),
         small_grads[7],
-        grad_contract,
+        after(grad_contract, grad_in).astype(f32),
         small_grads[6],
     )
 

time: 1050 us -> 769 us (0.73)
  waiting for transfers between devices: 596 us -> 249 us
  starting transfers between devices: 53.1 us -> 139 us
  blocking collectives: 43.8 us -> 0 us
  local copies, waits for them, and re-layouts: 102 us -> 66.5 us
  other arithmetic: 62.4 us -> 90.1 us
  matrix products: 137 us -> 162 us
    ppermute x31 -> x35, waiting for transfers between devices: 320 us -> 167 us  [the longest x6 57.1 us: ring_pieces(): pieces.append(lax.ppermute(pieces[-1], 'dp', shift(count, 1)))]
    unnamed x11 -> x8, waiting for transfers between devices: 115 us -> 0.8 us
    reduce_scatter x2, waiting for transfers between devices: 110 us -> 0.01 us  [the longest x1 0.01 us: shards(): lax.psum_scatter(grad_contract, 'seq', scatter_dimension=0, tiled=True)]
    ppermute x31 -> x35, starting transfers between devices: 15.5 us -> 69.8 us  [the longest x8 35.5 us: deal_strips(): moved.append(after(lax.ppermute(piece_for(by), BOTH, routes), *gates))]
    all_gather x6 -> x5, waiting for transfers between devices: 8.37 us -> 61.5 us  [the longest x1 36.6 us: shards(): lax.all_gather(after(w_contract, expand_weight), 'seq', axis=0, tiled=True)]
    all_to_all x1 -> x0, blocking collectives: 43.8 us -> none  [shards(): lax.all_to_all(sent, 'seq', 0, 0)]
    dot_general x5 -> x12, matrix products: 43.2 us -> 70 us  [dot(): return jnp.dot(left, right, preferred_element_type=f32)]
    all_to_all x3 -> x5, starting transfers between devices: 15.4 us -> 36 us  [the longest x1 11.8 us: shards(): lax.all_to_all(sums, BOTH, 0, 0)]
  transfers between devices with their start and end apart: 47 -> 51, of which waited for: 32 -> 26; matrix products, arithmetic and copies ran while one was open for 23% -> 39% of each run, Pallas kernels for 3% -> 4%
where the time goes in v3:
time: 769 us; the launch traced here: 761 us
  waiting for transfers between devices  249 us (32%)
  matrix products  162 us (21%)
  starting transfers between devices  139 us (18%)
  other arithmetic  90.1 us (12%)
  local copies, waits for them, and re-layouts  66.5 us (9%)
  Pallas kernels  28.5 us (4%)
  between operations  26.2 us (3%)
    dot_general x14, matrix products, dot_general(): lax.dot_general(left, right, ((left_dims, right_dims), ((), ())), preferr...  91.6 us
    dot_general x12, matrix products, dot(): return jnp.dot(left, right, preferred_element_type=f32)  70 us
    ppermute x6, waiting for transfers between devices, ring_pieces(): pieces.append(lax.ppermute(pieces[-1], 'dp', shift(count, 1)))  57.1 us
    ppermute x9, waiting for transfers between devices, ring_sum(): moving = lax.ppermute(sent[0], 'dp', shift(count, 1))  51.8 us
    all_gather x1, waiting for transfers between devices, shards(): lax.all_gather(after(w_contract, expand_weight), 'seq', axis=0, tiled=True)  36.6 us
    ppermute x8, starting transfers between devices, deal_strips(): moved.append(after(lax.ppermute(piece_for(by), BOTH, routes), *gates))  35.5 us
    all_gather x1, waiting for transfers between devices, shards(): lax.all_gather(after(expand_rows, mixed_rows), 'seq', axis=0, tiled=True)  24.9 us
    ppermute x3, waiting for transfers between devices, exchange_parts(): lax.ppermute(pick(pieces, ahead[by]), 'dp', shift(count, by))  24.6 us
  transfers between devices with their start and end apart: 51, of which 26 were waited for; matrix products, arithmetic and copies ran while one was open for 39% of the time, Pallas kernels for 4%

profile of v3, /device:TPU:1, one launch (start us, length us, event | category | flops | bytes accessed | tf_op | source)
XLA Modules:
  0.0 760.8 jit_solution(9731497000005290592)
XLA Ops:
  52.3 10.0 %collective-permute-done.1 = bf16[512,256]{1,0:T(8,128)(2,1)S(1)} collective-permute-done((bf16[512,256]{1,0:T(8,128)(2,1)S(1)}, bf16[512,256]{1,0:T(8,128)(2,1)S(1)}, u32[]{:S(2)}, u32[]{:S(2)}) %collective-permute-start.1) | collective-permute-done | bytes 262176 | tf_op jit(solution)/shard_map/ppermute | solution.py:65
  103.9 19.1 %collective-permute-done.10 = bf16[2,128,2048]{2,1,0:T(8,128)(2,1)S(1)} collective-permute-done((bf16[2,128,2048]{2,1,0:T(8,128)(2,1)}, bf16[2,128,2048]{2,1,0:T(8,128)(2,1)S(1)}, u32[]{:S(2)}, u32[]{:S(2)}) %collective-permute-start.10) | collective-permute-done | bytes 1048608 | tf_op jit(solution)/shard_map/ppermute | solution.py:79
  148.8 11.0 %collective-permute-start.13 = (bf16[64,2048]{1,0:T(8,128)(2,1)S(1)}, bf16[64,2048]{1,0:T(8,128)(2,1)}, u32[]{:S(2)}, u32[]{:S(2)}) collective-permute-start(bf16[64,2048]{1,0:T(8,128)(2,1)S(1)} %get-tuple-element.164), channel_id=1, source_target_pairs={{0,0},{1,8},{2,16},{3,24},{4,1},{5,9},{6,17},{7,25},{8,2},{9,10},{... | collective-permute-start | bytes 786440 | tf_op jit(solution)/shard_map/ppermute | solution.py:92
  167.4 11.7 %attend.1 = bf16[8,2,128,256]{3,2,1,0:T(8,128)(2,1)} custom-call(s32[2]{0:T(128)} %dynamic_slice.136.lengths_ref, bf16[8,2,128,256]{3,2,1,0:T(8,128)(2,1)} %bitcast.356, bf16[8,2,128,256]{3,2,1,0:T(8,128)(2,1)} %bitcast.358), custom_call_target="tpu_custom_call" | custom-call | flops 2147483648 | bytes 4194304 | tf_op jit(solution)/shard_map/attend/pallas_call | solution.py:365
  214.1 25.6 %collective-permute-done.17 = bf16[256,2048]{1,0:T(8,128)(2,1)} collective-permute-done((bf16[256,2048]{1,0:T(8,128)(2,1)S(1)}, bf16[256,2048]{1,0:T(8,128)(2,1)}, u32[]{:S(2)}, u32[]{:S(2)}) %collective-permute-start.17) | collective-permute-done | bytes 1048608 | tf_op jit(solution)/shard_map/ppermute | solution.py:79
  239.7 24.9 %all-gather.11.cloned.1.call-done = bf16[2048,2048]{1,0:T(8,128)(2,1)} async-done(((bf16[256,2048]{1,0:T(8,128)(2,1)}), bf16[2048,2048]{1,0:T(8,128)(2,1)}) %all-gather.11.cloned.1.call-update) | async-done | bytes 8388624 | tf_op jit(solution)/shard_map/all_gather | solution.py:377
  284.0 36.6 %all-gather.13.cloned.1.call-done = bf16[2048,2048]{1,0:T(8,128)(2,1)} async-done(((bf16[256,2048]{1,0:T(8,128)(2,1)}), bf16[2048,2048]{1,0:T(8,128)(2,1)}) %all-gather.13.cloned.1.call-update) | async-done | bytes 8388624 | tf_op jit(solution)/shard_map/all_gather | solution.py:405
  320.6 8.5 %fusion.30 = bf16[256,2048]{1,0:T(8,128)(2,1)} fusion(bf16[2048,2048]{1,0:T(8,128)(2,1)} %all-gather.13.cloned.1.call-done, f32[256,2048]{1,0:T(8,128)} %get-tuple-element.237, bf16[128,2048]{1,0:T(8,128)(2,1)} %get-tuple-element.138, bf16[128,2048]{1,0:T(8,128)(2,1)} %get-tuple-element.140), kind=kOutput, calls=%fused_computation.58 | convolution fusion | flops 2159017984 | bytes 12582912 | tf_op jit(solution)/shard_map/dot_general | solution.py:35
  356.0 11.8 %collective-permute-done.19 = bf16[256,2048]{1,0:T(8,128)(2,1)S(1)} collective-permute-done((bf16[256,2048]{1,0:T(8,128)(2,1)}, bf16[256,2048]{1,0:T(8,128)(2,1)S(1)}, u32[]{:S(2)}, u32[]{:S(2)}) %collective-permute-start.19) | collective-permute-done | bytes 1048608 | tf_op jit(solution)/shard_map/ppermute | solution.py:79
  375.8 11.3 %convolution_convert_fusion.1 = bf16[2048,2048]{1,0:T(8,128)(2,1)} fusion(bf16[1024,2048]{1,0:T(8,128)(2,1)S(1)} %copy-done.43, bf16[256,2048]{1,0:T(8,128)(2,1)S(1)} %get-tuple-element.232, bf16[256,2048]{1,0:T(8,128)(2,1)S(1)} %get-tuple-element.234, bf16[256,2048]{1,0:T(8,128)(2,1)S(1)} %copy-done.64, bf16[256,2048]{1,0:T(8,128)(2,1)S(1)} %get-tuple-element.238), kind=kOutput, calls=%fused_computation.12 | convolution fusion | flops 8610906112 | bytes 16777216 | tf_op jit(solution)/shard_map/dot_general | solution.py:35
  419.7 12.9 %collective-permute-done.22 = bf16[256,2048]{1,0:T(8,128)(2,1)} collective-permute-done((bf16[256,2048]{1,0:T(8,128)(2,1)S(1)}, bf16[256,2048]{1,0:T(8,128)(2,1)}, u32[]{:S(2)}, u32[]{:S(2)}) %collective-permute-start.22) | collective-permute-done | bytes 1048608 | tf_op jit(solution)/shard_map/ppermute | solution.py:121
  442.5 8.1 %convolution_convert_fusion.5 = bf16[256,2048]{1,0:T(8,128)(2,1)} fusion(bf16[256,2048]{1,0:T(8,128)(2,1)} %copy-done.63, bf16[2048,2048]{1,0:T(8,128)(2,1)} %all-gather.13.cloned.1.call-done), kind=kOutput, calls=%fused_computation.62 | convolution fusion | flops 2148007936 | bytes 10485760 | tf_op jit(solution)/shard_map/dot_general | solution.py:31
  450.6 7.7 %fusion.31 = bf16[1,256,2048]{2,1,0:T(8,128)(2,1)} fusion(bf16[256,2048]{1,0:T(8,128)(2,1)S(1)} %copy-done.60, bf16[2048,2048]{1,0:T(8,128)(2,1)} %all-gather.13.cloned.1.call-done), kind=kOutput, calls=%fused_computation.65 | convolution fusion | flops 2148007936 | bytes 10485760 | tf_op jit(solution)/shard_map/dot_general | solution.py:31
  469.3 13.0 %collective-permute-done.23 = bf16[256,2048]{1,0:T(8,128)(2,1)S(1)} collective-permute-done((bf16[256,2048]{1,0:T(8,128)(2,1)S(1)}, bf16[256,2048]{1,0:T(8,128)(2,1)S(1)}, u32[]{:S(2)}, u32[]{:S(2)}) %collective-permute-start.23) | collective-permute-done | bytes 1048608 | tf_op jit(solution)/shard_map/ppermute | solution.py:121
  495.4 8.6 %all-to-all-start.3 = ((bf16[8,256,256]{2,1,0:T(8,128)(2,1)}), bf16[8,256,256]{2,1,0:T(8,128)(2,1)}, u32[]{:S(2)}, u32[]{:S(2)}) async-start(bf16[8,256,256]{2,1,0:T(8,128)(2,1)} %bitcast.280), calls=%async_computation.3 | async-start | bytes 2097152 | tf_op jit(solution)/shard_map/all_to_all | solution.py:460
  506.4 8.6 %select_add_fusion.5 = (f32[1,128,2048]{2,1,0:T(8,128)}, bf16[1,128,2048]{2,1,0:T(8,128)(2,1)S(1)}, bf16[1,128,2048]{2,1,0:T(8,128)(2,1)S(1)}, f32[1,128,2048]{2,1,0:T(8,128)}, f32[1,128,2048]{2,1,0:T(8,128)}) fusion(f32[2,128,2048]{2,1,0:T(8,128)S(1)} %bitcast.284, u32[]{:T(128)} %bitcast.58, bf16[8,128,2048]{2,1,0:T(8,128)(2,1)S(1)} %bitcast.289, ...), kind=kLoop, calls=%fused_computation.126 | loop fusion | flops 4456448 | bytes 12058669 | tf_op jit(solution)/shard_map/add | solution.py:444
  530.8 16.8 %attend_back.1 = (bf16[8,2,128,256]{3,2,1,0:T(8,128)(2,1)}, bf16[8,2,128,256]{3,2,1,0:T(8,128)(2,1)}) custom-call(s32[2]{0:T(128)} %dynamic_slice.136.lengths_ref, bf16[8,2,128,256]{3,2,1,0:T(8,128)(2,1)} %bitcast.357, bf16[8,2,128,256]{3,2,1,0:T(8,128)(2,1)} %bitcast.359, bf16[8,2,128,256]{3,2,1,0:T(8,128)(2,1)} %bitcast.103.grad_ref), custom_call_target="tpu_custom_call" | custom-call | flops 5368709120 | bytes 8388608 | tf_op jit(solution)/shard_map/attend_back/pallas_call | solution.py:463
  562.5 13.4 %convolution_convert_fusion = bf16[2048,2048]{1,0:T(8,128)(2,1)} fusion(bf16[1024,2048]{1,0:T(8,128)(2,1)S(1)} %copy-done.10, bf16[256,2048]{1,0:T(8,128)(2,1)} %copy-done.53, bf16[256,2048]{1,0:T(8,128)(2,1)} %collective-permute-done.18, bf16[256,2048]{1,0:T(8,128)(2,1)} %collective-permute-done.17, bf16[256,2048]{1,0:T(8,128)(2,1)} %copy-done.33), kind=kOutput, calls=%fused_computation.11 | convolution fusion | flops 8610906112 | bytes 16777216 | tf_op jit(solution)/shard_map/dot_general | solution.py:35
  576.0 8.4 %copy.74 = bf16[4,8,64,2048]{3,2,0,1:T(8,128)(2,1)} copy(bf16[4,8,64,2048]{3,2,1,0:T(8,128)(2,1)} %bitcast.299) | data formatting | bytes 16777216 | tf_op jit(solution)/shard_map/reshape | solution.py:453
  628.0 11.8 %all-to-all-start.5 = ((f32[32,1,708]{2,1,0:T(1,128)}), f32[32,1,708]{2,1,0:T(1,128)S(1)}, u32[]{:S(2)}, u32[]{:S(2)}) async-start(f32[32,1,708]{2,1,0:T(1,128)} %all_to_all.31), calls=%async_computation.5 | async-start | bytes 196608 | tf_op jit(solution)/shard_map/all_to_all | solution.py:539
  648.5 14.4 %collective-permute-done.32 = bf16[64,2048]{1,0:T(8,128)(2,1)S(1)} collective-permute-done((bf16[64,2048]{1,0:T(8,128)(2,1)S(1)}, bf16[64,2048]{1,0:T(8,128)(2,1)S(1)}, u32[]{:S(2)}, u32[]{:S(2)}) %collective-permute-start.32) | collective-permute-done | bytes 262176 | tf_op jit(solution)/shard_map/ppermute | solution.py:121
  680.9 12.3 %collective-permute-start.35 = (bf16[64,2048]{1,0:T(8,128)(2,1)}, bf16[64,2048]{1,0:T(8,128)(2,1)S(1)}, u32[]{:S(2)}, u32[]{:S(2)}) collective-permute-start(bf16[64,2048]{1,0:T(8,128)(2,1)} %fusion.59), channel_id=1, source_target_pairs={{0,0},{1,4},{2,8},{3,12},{4,16},{5,20},{6,24},{7,28},{8,1},{9,5},{... | collective-permute-start | bytes 786440 | tf_op jit(solution)/shard_map/ppermute | solution.py:504
  702.3 18.9 %collective-permute-done.31 = bf16[64,2048]{1,0:T(8,128)(2,1)S(1)} collective-permute-done((bf16[64,2048]{1,0:T(8,128)(2,1)S(1)}, bf16[64,2048]{1,0:T(8,128)(2,1)S(1)}, u32[]{:S(2)}, u32[]{:S(2)}) %collective-permute-start.31) | collective-permute-done | bytes 262176 | tf_op jit(solution)/shard_map/ppermute | solution.py:102
  730.0 11.6 %all-to-all-start.6 = ((bf16[8,64,512]{2,1,0:T(8,128)(2,1)}), bf16[8,64,512]{2,1,0:T(8,128)(2,1)}, u32[]{:S(2)}, u32[]{:S(2)}) async-start(bf16[8,64,512]{2,1,0:T(8,128)(2,1)} %bitcast.315), calls=%async_computation.8 | async-start | bytes 1048576 | tf_op jit(solution)/shard_map/all_to_all | solution.py:495
  (424 shorter events, 397.6 us)
Async XLA Ops:
  7.2 86.6 %all-gather.7.cloned.1.call-start = ((), (), s32[]{:S(2)}) async-start(), calls=%async_computation.9 | async-start | bytes 9437184 | tf_op jit(solution)/shard_map/all_gather | solution.py:313
  35.3 32.8 %all-to-all-start.1 = ((bf16[8,4,72,256]{3,2,1,0:T(8,128)(2,1)}), bf16[8,4,72,256]{3,2,1,0:T(8,128)(2,1)S(1)}, u32[]{:S(2)}, u32[]{:S(2)}) async-start(bf16[8,4,72,256]{3,2,1,0:T(8,128)(2,1)} %broadcast_in_dim.256), calls=%async_computation.1 | async-start | bytes 2359296 | tf_op jit(solution)/shard_map/all_to_all | solution.py:331
  42.0 163.5 %all-gather.9.cloned.1.call-start = ((), (), s32[]{:S(2)}) async-start(), calls=%async_computation.10 | async-start | bytes 9437184 | tf_op jit(solution)/shard_map/all_gather | solution.py:355
  94.7 28.2 %collective-permute-start.10 = (bf16[2,128,2048]{2,1,0:T(8,128)(2,1)}, bf16[2,128,2048]{2,1,0:T(8,128)(2,1)S(1)}, u32[]{:S(2)}, u32[]{:S(2)}) collective-permute-start(bf16[2,128,2048]{2,1,0:T(8,128)(2,1)} %param.22), channel_id=1, source_target_pairs={{0,8},{8,16},{16,24},{24,0},{1,9},{9,17},{17,25},{25,1},{2,10},{10... | collective-permute-start | bytes 3145736 | tf_op jit(solution)/shard_map/ppermute | solution.py:79
  123.0 37.4 %collective-permute-start.11 = (bf16[2,128,2048]{2,1,0:T(8,128)(2,1)S(1)}, bf16[2,128,2048]{2,1,0:T(8,128)(2,1)}, u32[]{:S(2)}, u32[]{:S(2)}) collective-permute-start(bf16[2,128,2048]{2,1,0:T(8,128)(2,1)S(1)} %collective-permute-done.10), channel_id=1, source_target_pairs={{0,8},{8,16},{16,24},{24,0},{1,9},{9,17},{17,25},{25,1},{2,10},{10... | collective-permute-start | bytes 3145736 | tf_op jit(solution)/shard_map/ppermute | solution.py:79
  143.2 41.5 %collective-permute-start.14 = (bf16[64,2048]{1,0:T(8,128)(2,1)S(1)}, bf16[64,2048]{1,0:T(8,128)(2,1)S(1)}, u32[]{:S(2)}, u32[]{:S(2)}) collective-permute-start(bf16[64,2048]{1,0:T(8,128)(2,1)S(1)} %get-tuple-element.163), channel_id=1, source_target_pairs={{0,8},{1,16},{2,24},{3,0},{4,9},{5,17},{6,25},{7,1},{8,10},{9,18},... | collective-permute-start | bytes 786440 | tf_op jit(solution)/shard_map/ppermute | solution.py:92
  148.8 35.9 %collective-permute-start.13 = (bf16[64,2048]{1,0:T(8,128)(2,1)S(1)}, bf16[64,2048]{1,0:T(8,128)(2,1)}, u32[]{:S(2)}, u32[]{:S(2)}) collective-permute-start(bf16[64,2048]{1,0:T(8,128)(2,1)S(1)} %get-tuple-element.164), channel_id=1, source_target_pairs={{0,0},{1,8},{2,16},{3,24},{4,1},{5,9},{6,17},{7,25},{8,2},{9,10},{... | collective-permute-start | bytes 786440 | tf_op jit(solution)/shard_map/ppermute | solution.py:92
  160.4 35.5 %collective-permute-start.12 = (bf16[2,128,2048]{2,1,0:T(8,128)(2,1)}, bf16[2,128,2048]{2,1,0:T(8,128)(2,1)}, u32[]{:S(2)}, u32[]{:S(2)}) collective-permute-start(bf16[2,128,2048]{2,1,0:T(8,128)(2,1)} %collective-permute-done.11), channel_id=1, source_target_pairs={{0,8},{8,16},{16,24},{24,0},{1,9},{9,17},{17,25},{25,1},{2,10},{10... | collective-permute-start | bytes 3145736 | tf_op jit(solution)/shard_map/ppermute | solution.py:79
  163.1 29.5 %collective-permute-start.15 = (bf16[64,2048]{1,0:T(8,128)(2,1)S(1)}, bf16[64,2048]{1,0:T(8,128)(2,1)}, u32[]{:S(2)}, u32[]{:S(2)}) collective-permute-start(bf16[64,2048]{1,0:T(8,128)(2,1)S(1)} %get-tuple-element.162), channel_id=1, source_target_pairs={{0,16},{1,24},{2,0},{3,8},{4,17},{5,25},{6,1},{7,9},{8,18},{9,26},... | collective-permute-start | bytes 786440 | tf_op jit(solution)/shard_map/ppermute | solution.py:92
  184.4 80.2 %all-gather.11.cloned.1.call-start = ((), (), s32[]{:S(2)}) async-start(), calls=%async_computation.11 | async-start | bytes 9437184 | tf_op jit(solution)/shard_map/all_gather | solution.py:377
  203.8 116.8 %all-gather.13.cloned.1.call-start = ((), (), s32[]{:S(2)}) async-start(), calls=%async_computation.12 | async-start | bytes 9437184 | tf_op jit(solution)/shard_map/all_gather | solution.py:405
  265.2 171.9 %all-gather.15.cloned.1.call-start = ((), (), s32[]{:S(2)}) async-start(), calls=%async_computation.13 | async-start | bytes 9437184 | tf_op jit(solution)/shard_map/all_gather | solution.py:431
  329.2 187.1 %reduce-scatter.3.cloned.1.call-start = ((), (), s32[]{:S(2)}) async-start(), calls=%async_computation.14 | async-start | bytes 9437184 | tf_op jit(solution)/shard_map/reduce_scatter | solution.py:433
  504.0 89.8 %all-gather.17.cloned.1.call-start = ((), (), s32[]{:S(2)}) async-start(), calls=%async_computation.15 | async-start | bytes 9437184 | tf_op jit(solution)/shard_map/all_gather | solution.py:465
  518.1 40.5 %collective-permute-start.20 = (bf16[2,128,2048]{2,1,0:T(8,128)(2,1)}, bf16[2,128,2048]{2,1,0:T(8,128)(2,1)}, u32[]{:S(2)}, u32[]{:S(2)}) collective-permute-start(bf16[2,128,2048]{2,1,0:T(8,128)(2,1)} %pad_maximum_fusion.3), channel_id=1, source_target_pairs={{0,8},{8,16},{16,24},{24,0},{1,9},{9,17},{17,25},{25,1},{2,10},{10... | collective-permute-start | bytes 3145736 | tf_op jit(solution)/shard_map/ppermute | solution.py:469
  551.9 41.9 %all-to-all-start.4 = ((bf16[8,256,512]{1,2,0:T(8,128)(2,1)}), bf16[8,256,512]{1,2,0:T(8,128)(2,1)S(1)}, u32[]{:S(2)}, u32[]{:S(2)}) async-start(bf16[8,256,512]{1,2,0:T(8,128)(2,1)} %copy.72), calls=%async_computation.4 | async-start | bytes 4194304 | tf_op jit(solution)/shard_map/all_to_all | solution.py:468
  558.6 116.0 %reduce-scatter.5.cloned.1.call-start = ((), (), s32[]{:S(2)}) async-start(), calls=%async_computation.16 | async-start | bytes 9437184 | tf_op jit(solution)/shard_map/reduce_scatter | solution.py:478
  611.1 54.6 %collective-permute-start.25 = (bf16[2,128,2048]{2,1,0:T(8,128)(2,1)}, bf16[2,128,2048]{2,1,0:T(8,128)(2,1)}, u32[]{:S(2)}, u32[]{:S(2)}) collective-permute-start(bf16[2,128,2048]{2,1,0:T(8,128)(2,1)} %maximum_add_fusion.1), channel_id=1, source_target_pairs={{0,8},{8,16},{16,24},{24,0},{1,9},{9,17},{17,25},{25,1},{2,10},{10... | collective-permute-start | bytes 3145736 | tf_op jit(solution)/shard_map/ppermute | solution.py:507
  625.8 40.0 %collective-permute-start.27 = (bf16[512,512]{1,0:T(8,128)(2,1)}, bf16[512,512]{1,0:T(8,128)(2,1)}, u32[]{:S(2)}, u32[]{:S(2)}) collective-permute-start(bf16[512,512]{1,0:T(8,128)(2,1)} %fusion.53), channel_id=1, source_target_pairs={{0,8},{8,16},{16,24},{24,0},{1,9},{9,17},{17,25},{25,1},{2,10},{10... | collective-permute-start | bytes 1572872 | tf_op jit(solution)/shard_map/ppermute | solution.py:121
  628.0 101.9 %all-to-all-start.5 = ((f32[32,1,708]{2,1,0:T(1,128)}), f32[32,1,708]{2,1,0:T(1,128)S(1)}, u32[]{:S(2)}, u32[]{:S(2)}) async-start(f32[32,1,708]{2,1,0:T(1,128)} %all_to_all.31), calls=%async_computation.5 | async-start | bytes 196608 | tf_op jit(solution)/shard_map/all_to_all | solution.py:539
  674.5 52.5 %collective-permute-start.28 = (bf16[512,512]{1,0:T(8,128)(2,1)}, bf16[512,512]{1,0:T(8,128)(2,1)}, u32[]{:S(2)}, u32[]{:S(2)}) collective-permute-start(bf16[512,512]{1,0:T(8,128)(2,1)} %fusion.54), channel_id=1, source_target_pairs={{0,8},{8,16},{16,24},{24,0},{1,9},{9,17},{17,25},{25,1},{2,10},{10... | collective-permute-start | bytes 1572872 | tf_op jit(solution)/shard_map/ppermute | solution.py:121
  680.9 64.9 %collective-permute-start.35 = (bf16[64,2048]{1,0:T(8,128)(2,1)}, bf16[64,2048]{1,0:T(8,128)(2,1)S(1)}, u32[]{:S(2)}, u32[]{:S(2)}) collective-permute-start(bf16[64,2048]{1,0:T(8,128)(2,1)} %fusion.59), channel_id=1, source_target_pairs={{0,0},{1,4},{2,8},{3,12},{4,16},{5,20},{6,24},{7,28},{8,1},{9,5},{... | collective-permute-start | bytes 786440 | tf_op jit(solution)/shard_map/ppermute | solution.py:504
  693.2 28.0 %collective-permute-start.31 = (bf16[64,2048]{1,0:T(8,128)(2,1)S(1)}, bf16[64,2048]{1,0:T(8,128)(2,1)S(1)}, u32[]{:S(2)}, u32[]{:S(2)}) collective-permute-start(bf16[64,2048]{1,0:T(8,128)(2,1)S(1)} %get-tuple-element.157), channel_id=1, source_target_pairs={{0,24},{8,0},{16,8},{24,16},{1,25},{9,1},{17,9},{25,17},{2,26},{10... | collective-permute-start | bytes 786440 | tf_op jit(solution)/shard_map/ppermute | solution.py:102
  696.2 30.7 %collective-permute-start.30 = (bf16[64,2048]{1,0:T(8,128)(2,1)S(1)}, bf16[64,2048]{1,0:T(8,128)(2,1)S(1)}, u32[]{:S(2)}, u32[]{:S(2)}) collective-permute-start(bf16[64,2048]{1,0:T(8,128)(2,1)S(1)} %get-tuple-element.158), channel_id=1, source_target_pairs={{0,16},{8,24},{16,0},{24,8},{1,17},{9,25},{17,1},{25,9},{2,18},{10... | collective-permute-start | bytes 786440 | tf_op jit(solution)/shard_map/ppermute | solution.py:102
  (103 other events, 1967.4 us)
Sparse Core Ops, SparseCore 0:
  9.9 74.6 all-gather.6
  94.9 68.7 all-gather.8
  203.9 60.6 all-gather.10
  266.3 54.2 all-gather.12
  329.3 55.8 all-gather.14
  437.3 70.8 reduce-scatter.2
  516.4 75.8 all-gather.16
  595.7 77.4 reduce-scatter.4

commit v4 on v3

--- a/solution.py
+++ b/solution.py
@@ -398,18 +398,28 @@
     slopes = [None] * parts
     grad_pres = [None] * parts
 
-    for by in range(parts):
-        preact = dot(normed2_ins[by], expand_weight) + expand_bias
+    sums_c = []
+
+    def forward(by, *gates):
+        preact = dot(after(normed2_ins[by], *gates), expand_weight) + expand_bias
         active, slopes[by] = gelu_parts(preact)
         actives[by] = active.astype(bf16)
+
+    for by in range(3):
+        forward(by)
     contract_weight = lax.all_gather(after(w_contract, expand_weight), "seq", axis=0, tiled=True)
-    active_all = jnp.concatenate(actives, axis=0)
     grad_m_all = jnp.concatenate(grad_ms, axis=0)
-    grad_contract = dot_general(active_all, grad_m_all, (0,), (0,)).astype(bf16)
-    grad_contract_all = grad_contract
+    grad_contracts = []
+
+    def contract_gate():
+        active_all = jnp.concatenate(actives, axis=0)
+        grad_contracts.append(dot_general(active_all, grad_m_all, (0,), (0,)).astype(bf16))
+        return grad_contracts
 
     def grad_c_for(by, sent):
         sums_c.extend(sent)
+        if actives[by] is None:
+            forward(by, *sums_c[:1])
         grad_active = dot_general(grad_ms[by], contract_weight, (1,), (1,))
         grad_pres[by] = (grad_active * slopes[by]).astype(bf16)
         return dot_general(grad_pres[by], expand_weight, (1,), (1,))
@@ -421,15 +431,15 @@
         return outputs[by]
 
     gates = (
-        lambda: [grad_contract_all],
         lambda: [output_of(1)],
+        *[lambda: []] * (parts - 4),
+        contract_gate,
         lambda: [output_of(2)],
     )
-    sums_c = []
     grad_c = ring_sum(grad_c_for, parts, gates)
     query_weight_all = after(query_weight.T, grad_pres[1])
     query_weight_all = lax.all_gather(query_weight_all, "seq", axis=0, tiled=True)
-    grad_contract = after(grad_contract_all, sums_c[-1], query_weight_all)
+    grad_contract = after(grad_contracts[0], query_weight_all)
     grad_contract = lax.psum_scatter(grad_contract, "seq", scatter_dimension=0, tiled=True)
     for by in range(parts):
         if outputs[by] is None:

time: 769 us -> 750 us (0.975)
  waiting for transfers between devices: 249 us -> 241 us
    unnamed x14 -> x12, other arithmetic: 16.4 us -> 16.5 us
where the time goes in v4:
time: 750 us; the launch traced here: 742 us
  waiting for transfers between devices  241 us (32%)
  matrix products  156 us (21%)
  starting transfers between devices  132 us (18%)
  other arithmetic  89.5 us (12%)
  local copies, waits for them, and re-layouts  68 us (9%)
  Pallas kernels  28.6 us (4%)
  between operations  26 us (3%)
    dot_general x14, matrix products, dot_general(): lax.dot_general(left, right, ((left_dims, right_dims), ((), ())), preferr...  86.9 us
    dot_general x12, matrix products, dot(): return jnp.dot(left, right, preferred_element_type=f32)  69.6 us
    ppermute x6, waiting for transfers between devices, ring_pieces(): pieces.append(lax.ppermute(pieces[-1], 'dp', shift(count, 1)))  53.7 us
    ppermute x9, waiting for transfers between devices, ring_sum(): moving = lax.ppermute(sent[0], 'dp', shift(count, 1))  48 us
    all_gather x1, waiting for transfers between devices, shards(): lax.all_gather(after(w_contract, expand_weight), 'seq', axis=0, tiled=True)  36.5 us
    ppermute x8, starting transfers between devices, deal_strips(): moved.append(after(lax.ppermute(piece_for(by), BOTH, routes), *gates))  35.3 us
    ppermute x3, waiting for transfers between devices, exchange_parts(): lax.ppermute(pick(pieces, ahead[by]), 'dp', shift(count, by))  26.6 us
    all_gather x1, waiting for transfers between devices, shards(): lax.all_gather(after(expand_rows, mixed_rows), 'seq', axis=0, tiled=True)  24.8 us
  transfers between devices with their start and end apart: 51, of which 26 were waited for; matrix products, arithmetic and copies ran while one was open for 39% of the time, Pallas kernels for 4%

profile of v4, /device:TPU:1, one launch (start us, length us, event | category | flops | bytes accessed | tf_op | source)
XLA Modules:
  0.0 741.8 jit_solution(15618714199710980291)
XLA Ops:
  52.3 10.0 %collective-permute-done.1 = bf16[512,256]{1,0:T(8,128)(2,1)S(1)} collective-permute-done((bf16[512,256]{1,0:T(8,128)(2,1)S(1)}, bf16[512,256]{1,0:T(8,128)(2,1)S(1)}, u32[]{:S(2)}, u32[]{:S(2)}) %collective-permute-start.1) | collective-permute-done | bytes 262176 | tf_op jit(solution)/shard_map/ppermute | solution.py:65
  103.9 19.1 %collective-permute-done.10 = bf16[2,128,2048]{2,1,0:T(8,128)(2,1)S(1)} collective-permute-done((bf16[2,128,2048]{2,1,0:T(8,128)(2,1)}, bf16[2,128,2048]{2,1,0:T(8,128)(2,1)S(1)}, u32[]{:S(2)}, u32[]{:S(2)}) %collective-permute-start.10) | collective-permute-done | bytes 1048608 | tf_op jit(solution)/shard_map/ppermute | solution.py:79
  148.9 11.0 %collective-permute-start.13 = (bf16[64,2048]{1,0:T(8,128)(2,1)S(1)}, bf16[64,2048]{1,0:T(8,128)(2,1)}, u32[]{:S(2)}, u32[]{:S(2)}) collective-permute-start(bf16[64,2048]{1,0:T(8,128)(2,1)S(1)} %get-tuple-element.166), channel_id=1, source_target_pairs={{0,0},{1,8},{2,16},{3,24},{4,1},{5,9},{6,17},{7,25},{8,2},{9,10},{... | collective-permute-start | bytes 786440 | tf_op jit(solution)/shard_map/ppermute | solution.py:92
  167.1 11.8 %attend.1 = bf16[8,2,128,256]{3,2,1,0:T(8,128)(2,1)} custom-call(s32[2]{0:T(128)} %dynamic_slice.136.lengths_ref, bf16[8,2,128,256]{3,2,1,0:T(8,128)(2,1)} %bitcast.352, bf16[8,2,128,256]{3,2,1,0:T(8,128)(2,1)} %bitcast.354), custom_call_target="tpu_custom_call" | custom-call | flops 2147483648 | bytes 4194304 | tf_op jit(solution)/shard_map/attend/pallas_call | solution.py:365
  214.3 25.5 %collective-permute-done.17 = bf16[256,2048]{1,0:T(8,128)(2,1)} collective-permute-done((bf16[256,2048]{1,0:T(8,128)(2,1)S(1)}, bf16[256,2048]{1,0:T(8,128)(2,1)}, u32[]{:S(2)}, u32[]{:S(2)}) %collective-permute-start.17) | collective-permute-done | bytes 1048608 | tf_op jit(solution)/shard_map/ppermute | solution.py:79
  239.8 24.8 %all-gather.11.cloned.1.call-done = bf16[2048,2048]{1,0:T(8,128)(2,1)} async-done(((bf16[256,2048]{1,0:T(8,128)(2,1)}), bf16[2048,2048]{1,0:T(8,128)(2,1)}) %all-gather.11.cloned.1.call-update) | async-done | bytes 8388624 | tf_op jit(solution)/shard_map/all_gather | solution.py:377
  284.0 36.5 %all-gather.13.cloned.1.call-done = bf16[2048,2048]{1,0:T(8,128)(2,1)} async-done(((bf16[256,2048]{1,0:T(8,128)(2,1)}), bf16[2048,2048]{1,0:T(8,128)(2,1)}) %all-gather.13.cloned.1.call-update) | async-done | bytes 8388624 | tf_op jit(solution)/shard_map/all_gather | solution.py:410
  320.6 8.5 %fusion.27 = bf16[256,2048]{1,0:T(8,128)(2,1)} fusion(bf16[2048,2048]{1,0:T(8,128)(2,1)} %all-gather.13.cloned.1.call-done, f32[256,2048]{1,0:T(8,128)} %get-tuple-element.239, bf16[128,2048]{1,0:T(8,128)(2,1)} %get-tuple-element.140, bf16[128,2048]{1,0:T(8,128)(2,1)} %get-tuple-element.142), kind=kOutput, calls=%fused_computation.55 | convolution fusion | flops 2159017984 | bytes 12582912 | tf_op jit(solution)/shard_map/dot_general | solution.py:35
  342.5 7.5 %multiply_convert_fusion.3 = (bf16[256,2048]{1,0:T(8,128)(2,1)S(1)}, f32[256,2048]{1,0:T(8,128)}) fusion(f32[2048]{0:T(1024)S(1)} %bitcast.341, bf16[256,2048]{1,0:T(8,128)(2,1)S(1)} %copy-done.34, bf16[2048,2048]{1,0:T(8,128)(2,1)} %all-gather.11.cloned.1.call-done), kind=kOutput, calls=%fused_computation.92 | convolution fusion | flops 2152726528 | bytes 12591104 | tf_op jit(solution)/shard_map/dot_general | solution.py:31
  359.4 8.4 %collective-permute-done.19 = bf16[256,2048]{1,0:T(8,128)(2,1)S(1)} collective-permute-done((bf16[256,2048]{1,0:T(8,128)(2,1)}, bf16[256,2048]{1,0:T(8,128)(2,1)S(1)}, u32[]{:S(2)}, u32[]{:S(2)}) %collective-permute-start.19) | collective-permute-done | bytes 1048608 | tf_op jit(solution)/shard_map/ppermute | solution.py:79
  373.0 11.3 %convolution_convert_fusion.1 = bf16[2048,2048]{1,0:T(8,128)(2,1)} fusion(bf16[1024,2048]{1,0:T(8,128)(2,1)S(1)} %copy-done.45, bf16[256,2048]{1,0:T(8,128)(2,1)S(1)} %get-tuple-element.234, bf16[256,2048]{1,0:T(8,128)(2,1)S(1)} %get-tuple-element.236, bf16[256,2048]{1,0:T(8,128)(2,1)S(1)} %copy-done.62, bf16[256,2048]{1,0:T(8,128)(2,1)S(1)} %get-tuple-element.240), kind=kOutput, calls=%fused_computation.12 | convolution fusion | flops 8610906112 | bytes 16777216 | tf_op jit(solution)/shard_map/dot_general | solution.py:35
  391.9 8.6 %convolution_convert_fusion.6 = bf16[256,2048]{1,0:T(8,128)(2,1)} fusion(bf16[256,2048]{1,0:T(8,128)(2,1)} %get-tuple-element.238, bf16[2048,2048]{1,0:T(8,128)(2,1)} %all-gather.13.cloned.1.call-done), kind=kOutput, calls=%fused_computation.63 | convolution fusion | flops 2148007936 | bytes 10485760 | tf_op jit(solution)/shard_map/dot_general | solution.py:31
  434.2 11.2 %collective-permute-done.22 = bf16[256,2048]{1,0:T(8,128)(2,1)S(1)} collective-permute-done((bf16[256,2048]{1,0:T(8,128)(2,1)S(1)}, bf16[256,2048]{1,0:T(8,128)(2,1)S(1)}, u32[]{:S(2)}, u32[]{:S(2)}) %collective-permute-start.22) | collective-permute-done | bytes 1048608 | tf_op jit(solution)/shard_map/ppermute | solution.py:121
  461.7 10.8 %collective-permute-done.23 = bf16[256,2048]{1,0:T(8,128)(2,1)S(1)} collective-permute-done((bf16[256,2048]{1,0:T(8,128)(2,1)S(1)}, bf16[256,2048]{1,0:T(8,128)(2,1)S(1)}, u32[]{:S(2)}, u32[]{:S(2)}) %collective-permute-start.23) | collective-permute-done | bytes 1048608 | tf_op jit(solution)/shard_map/ppermute | solution.py:121
  494.9 8.5 %select_add_fusion.5 = (f32[1,128,2048]{2,1,0:T(8,128)}, bf16[1,128,2048]{2,1,0:T(8,128)(2,1)S(1)}, bf16[1,128,2048]{2,1,0:T(8,128)(2,1)S(1)}, f32[1,128,2048]{2,1,0:T(8,128)}, f32[1,128,2048]{2,1,0:T(8,128)}) fusion(f32[2,128,2048]{2,1,0:T(8,128)S(1)} %bitcast.284, u32[]{:T(128)} %bitcast.69, bf16[8,128,2048]{2,1,0:T(8,128)(2,1)S(1)} %bitcast.289, ...), kind=kLoop, calls=%fused_computation.126 | loop fusion | flops 4456448 | bytes 12058669 | tf_op jit(solution)/shard_map/add | solution.py:454
  517.3 16.8 %attend_back.1 = (bf16[8,2,128,256]{3,2,1,0:T(8,128)(2,1)}, bf16[8,2,128,256]{3,2,1,0:T(8,128)(2,1)}) custom-call(s32[2]{0:T(128)} %dynamic_slice.136.lengths_ref, bf16[8,2,128,256]{3,2,1,0:T(8,128)(2,1)} %bitcast.353, bf16[8,2,128,256]{3,2,1,0:T(8,128)(2,1)} %bitcast.355, bf16[8,2,128,256]{3,2,1,0:T(8,128)(2,1)} %bitcast.103.grad_ref), custom_call_target="tpu_custom_call" | custom-call | flops 5368709120 | bytes 8388608 | tf_op jit(solution)/shard_map/attend_back/pallas_call | solution.py:473
  548.8 13.5 %convolution_convert_fusion = bf16[2048,2048]{1,0:T(8,128)(2,1)} fusion(bf16[1024,2048]{1,0:T(8,128)(2,1)S(1)} %copy-done.10, bf16[256,2048]{1,0:T(8,128)(2,1)} %copy-done.55, bf16[256,2048]{1,0:T(8,128)(2,1)} %collective-permute-done.18, bf16[256,2048]{1,0:T(8,128)(2,1)} %collective-permute-done.17, bf16[256,2048]{1,0:T(8,128)(2,1)} %copy-done.33), kind=kOutput, calls=%fused_computation.11 | convolution fusion | flops 8610906112 | bytes 16777216 | tf_op jit(solution)/shard_map/dot_general | solution.py:35
  562.3 8.4 %copy.74 = bf16[4,8,64,2048]{3,2,0,1:T(8,128)(2,1)} copy(bf16[4,8,64,2048]{3,2,1,0:T(8,128)(2,1)} %bitcast.299) | data formatting | bytes 16777216 | tf_op jit(solution)/shard_map/reshape | solution.py:463
  583.4 7.6 %fusion.79 = f32[2048,512]{1,0:T(8,128)S(1)} fusion(bf16[2048,2048]{1,0:T(8,128)(2,1)} %copy-done.5, bf16[2048,512]{1,0:T(8,128)(2,1)} %bitcast.304), kind=kOutput, calls=%fused_computation.253 | convolution fusion | flops 4294967296 | bytes 14680064 | tf_op jit(solution)/shard_map/dot_general | solution.py:35
  610.9 11.2 %all-to-all-start.5 = ((f32[32,1,708]{2,1,0:T(1,128)}), f32[32,1,708]{2,1,0:T(1,128)S(1)}, u32[]{:S(2)}, u32[]{:S(2)}) async-start(f32[32,1,708]{2,1,0:T(1,128)} %all_to_all.31), calls=%async_computation.5 | async-start | bytes 196608 | tf_op jit(solution)/shard_map/all_to_all | solution.py:549
  630.6 15.2 %collective-permute-done.32 = bf16[64,2048]{1,0:T(8,128)(2,1)S(1)} collective-permute-done((bf16[64,2048]{1,0:T(8,128)(2,1)S(1)}, bf16[64,2048]{1,0:T(8,128)(2,1)S(1)}, u32[]{:S(2)}, u32[]{:S(2)}) %collective-permute-start.32) | collective-permute-done | bytes 262176 | tf_op jit(solution)/shard_map/ppermute | solution.py:121
  664.4 12.2 %collective-permute-start.35 = (bf16[64,2048]{1,0:T(8,128)(2,1)}, bf16[64,2048]{1,0:T(8,128)(2,1)S(1)}, u32[]{:S(2)}, u32[]{:S(2)}) collective-permute-start(bf16[64,2048]{1,0:T(8,128)(2,1)} %fusion.59), channel_id=1, source_target_pairs={{0,0},{1,4},{2,8},{3,12},{4,16},{5,20},{6,24},{7,28},{8,1},{9,5},{... | collective-permute-start | bytes 786440 | tf_op jit(solution)/shard_map/ppermute | solution.py:514
  683.2 20.9 %collective-permute-done.31 = bf16[64,2048]{1,0:T(8,128)(2,1)S(1)} collective-permute-done((bf16[64,2048]{1,0:T(8,128)(2,1)S(1)}, bf16[64,2048]{1,0:T(8,128)(2,1)S(1)}, u32[]{:S(2)}, u32[]{:S(2)}) %collective-permute-start.31) | collective-permute-done | bytes 262176 | tf_op jit(solution)/shard_map/ppermute | solution.py:102
  712.8 9.8 %all-to-all-start.6 = ((bf16[8,64,512]{2,1,0:T(8,128)(2,1)}), bf16[8,64,512]{2,1,0:T(8,128)(2,1)}, u32[]{:S(2)}, u32[]{:S(2)}) async-start(bf16[8,64,512]{2,1,0:T(8,128)(2,1)} %bitcast.315), calls=%async_computation.8 | async-start | bytes 1048576 | tf_op jit(solution)/shard_map/all_to_all | solution.py:505
  (420 shorter events, 386.8 us)
Async XLA Ops:
  7.2 86.6 %all-gather.7.cloned.1.call-start = ((), (), s32[]{:S(2)}) async-start(), calls=%async_computation.9 | async-start | bytes 9437184 | tf_op jit(solution)/shard_map/all_gather | solution.py:313
  35.3 32.8 %all-to-all-start.1 = ((bf16[8,4,72,256]{3,2,1,0:T(8,128)(2,1)}), bf16[8,4,72,256]{3,2,1,0:T(8,128)(2,1)S(1)}, u32[]{:S(2)}, u32[]{:S(2)}) async-start(bf16[8,4,72,256]{3,2,1,0:T(8,128)(2,1)} %broadcast_in_dim.256), calls=%async_computation.1 | async-start | bytes 2359296 | tf_op jit(solution)/shard_map/all_to_all | solution.py:331
  42.0 163.5 %all-gather.9.cloned.1.call-start = ((), (), s32[]{:S(2)}) async-start(), calls=%async_computation.10 | async-start | bytes 9437184 | tf_op jit(solution)/shard_map/all_gather | solution.py:355
  94.7 28.3 %collective-permute-start.10 = (bf16[2,128,2048]{2,1,0:T(8,128)(2,1)}, bf16[2,128,2048]{2,1,0:T(8,128)(2,1)S(1)}, u32[]{:S(2)}, u32[]{:S(2)}) collective-permute-start(bf16[2,128,2048]{2,1,0:T(8,128)(2,1)} %param.22), channel_id=1, source_target_pairs={{0,8},{8,16},{16,24},{24,0},{1,9},{9,17},{17,25},{25,1},{2,10},{10... | collective-permute-start | bytes 3145736 | tf_op jit(solution)/shard_map/ppermute | solution.py:79
  123.0 37.5 %collective-permute-start.11 = (bf16[2,128,2048]{2,1,0:T(8,128)(2,1)S(1)}, bf16[2,128,2048]{2,1,0:T(8,128)(2,1)}, u32[]{:S(2)}, u32[]{:S(2)}) collective-permute-start(bf16[2,128,2048]{2,1,0:T(8,128)(2,1)S(1)} %collective-permute-done.10), channel_id=1, source_target_pairs={{0,8},{8,16},{16,24},{24,0},{1,9},{9,17},{17,25},{25,1},{2,10},{10... | collective-permute-start | bytes 3145736 | tf_op jit(solution)/shard_map/ppermute | solution.py:79
  143.2 41.8 %collective-permute-start.14 = (bf16[64,2048]{1,0:T(8,128)(2,1)S(1)}, bf16[64,2048]{1,0:T(8,128)(2,1)S(1)}, u32[]{:S(2)}, u32[]{:S(2)}) collective-permute-start(bf16[64,2048]{1,0:T(8,128)(2,1)S(1)} %get-tuple-element.165), channel_id=1, source_target_pairs={{0,8},{1,16},{2,24},{3,0},{4,9},{5,17},{6,25},{7,1},{8,10},{9,18},... | collective-permute-start | bytes 786440 | tf_op jit(solution)/shard_map/ppermute | solution.py:92
  148.9 36.1 %collective-permute-start.13 = (bf16[64,2048]{1,0:T(8,128)(2,1)S(1)}, bf16[64,2048]{1,0:T(8,128)(2,1)}, u32[]{:S(2)}, u32[]{:S(2)}) collective-permute-start(bf16[64,2048]{1,0:T(8,128)(2,1)S(1)} %get-tuple-element.166), channel_id=1, source_target_pairs={{0,0},{1,8},{2,16},{3,24},{4,1},{5,9},{6,17},{7,25},{8,2},{9,10},{... | collective-permute-start | bytes 786440 | tf_op jit(solution)/shard_map/ppermute | solution.py:92
  160.5 35.5 %collective-permute-start.12 = (bf16[2,128,2048]{2,1,0:T(8,128)(2,1)}, bf16[2,128,2048]{2,1,0:T(8,128)(2,1)}, u32[]{:S(2)}, u32[]{:S(2)}) collective-permute-start(bf16[2,128,2048]{2,1,0:T(8,128)(2,1)} %collective-permute-done.11), channel_id=1, source_target_pairs={{0,8},{8,16},{16,24},{24,0},{1,9},{9,17},{17,25},{25,1},{2,10},{10... | collective-permute-start | bytes 3145736 | tf_op jit(solution)/shard_map/ppermute | solution.py:79
  163.2 29.5 %collective-permute-start.15 = (bf16[64,2048]{1,0:T(8,128)(2,1)S(1)}, bf16[64,2048]{1,0:T(8,128)(2,1)}, u32[]{:S(2)}, u32[]{:S(2)}) collective-permute-start(bf16[64,2048]{1,0:T(8,128)(2,1)S(1)} %get-tuple-element.164), channel_id=1, source_target_pairs={{0,16},{1,24},{2,0},{3,8},{4,17},{5,25},{6,1},{7,9},{8,18},{9,26},... | collective-permute-start | bytes 786440 | tf_op jit(solution)/shard_map/ppermute | solution.py:92
  184.5 80.1 %all-gather.11.cloned.1.call-start = ((), (), s32[]{:S(2)}) async-start(), calls=%async_computation.11 | async-start | bytes 9437184 | tf_op jit(solution)/shard_map/all_gather | solution.py:377
  203.8 116.7 %all-gather.13.cloned.1.call-start = ((), (), s32[]{:S(2)}) async-start(), calls=%async_computation.12 | async-start | bytes 9437184 | tf_op jit(solution)/shard_map/all_gather | solution.py:410
  265.3 119.9 %all-gather.15.cloned.1.call-start = ((), (), s32[]{:S(2)}) async-start(), calls=%async_computation.13 | async-start | bytes 9437184 | tf_op jit(solution)/shard_map/all_gather | solution.py:441
  329.1 175.4 %reduce-scatter.3.cloned.1.call-start = ((), (), s32[]{:S(2)}) async-start(), calls=%async_computation.14 | async-start | bytes 9437184 | tf_op jit(solution)/shard_map/reduce_scatter | solution.py:443
  492.6 84.4 %all-gather.17.cloned.1.call-start = ((), (), s32[]{:S(2)}) async-start(), calls=%async_computation.15 | async-start | bytes 9437184 | tf_op jit(solution)/shard_map/all_gather | solution.py:475
  506.4 39.3 %collective-permute-start.20 = (bf16[2,128,2048]{2,1,0:T(8,128)(2,1)}, bf16[2,128,2048]{2,1,0:T(8,128)(2,1)}, u32[]{:S(2)}, u32[]{:S(2)}) collective-permute-start(bf16[2,128,2048]{2,1,0:T(8,128)(2,1)} %pad_maximum_fusion.3), channel_id=1, source_target_pairs={{0,8},{8,16},{16,24},{24,0},{1,9},{9,17},{17,25},{25,1},{2,10},{10... | collective-permute-start | bytes 3145736 | tf_op jit(solution)/shard_map/ppermute | solution.py:479
  538.4 38.6 %all-to-all-start.4 = ((bf16[8,256,512]{1,2,0:T(8,128)(2,1)}), bf16[8,256,512]{1,2,0:T(8,128)(2,1)S(1)}, u32[]{:S(2)}, u32[]{:S(2)}) async-start(bf16[8,256,512]{1,2,0:T(8,128)(2,1)} %copy.72), calls=%async_computation.4 | async-start | bytes 4194304 | tf_op jit(solution)/shard_map/all_to_all | solution.py:478
  545.6 112.4 %reduce-scatter.5.cloned.1.call-start = ((), (), s32[]{:S(2)}) async-start(), calls=%async_computation.16 | async-start | bytes 9437184 | tf_op jit(solution)/shard_map/reduce_scatter | solution.py:488
  594.5 54.1 %collective-permute-start.25 = (bf16[2,128,2048]{2,1,0:T(8,128)(2,1)}, bf16[2,128,2048]{2,1,0:T(8,128)(2,1)}, u32[]{:S(2)}, u32[]{:S(2)}) collective-permute-start(bf16[2,128,2048]{2,1,0:T(8,128)(2,1)} %maximum_add_fusion.1), channel_id=1, source_target_pairs={{0,8},{8,16},{16,24},{24,0},{1,9},{9,17},{17,25},{25,1},{2,10},{10... | collective-permute-start | bytes 3145736 | tf_op jit(solution)/shard_map/ppermute | solution.py:517
  608.6 40.0 %collective-permute-start.27 = (bf16[512,512]{1,0:T(8,128)(2,1)}, bf16[512,512]{1,0:T(8,128)(2,1)}, u32[]{:S(2)}, u32[]{:S(2)}) collective-permute-start(bf16[512,512]{1,0:T(8,128)(2,1)} %fusion.53), channel_id=1, source_target_pairs={{0,8},{8,16},{16,24},{24,0},{1,9},{9,17},{17,25},{25,1},{2,10},{10... | collective-permute-start | bytes 1572872 | tf_op jit(solution)/shard_map/ppermute | solution.py:121
  610.9 101.9 %all-to-all-start.5 = ((f32[32,1,708]{2,1,0:T(1,128)}), f32[32,1,708]{2,1,0:T(1,128)S(1)}, u32[]{:S(2)}, u32[]{:S(2)}) async-start(f32[32,1,708]{2,1,0:T(1,128)} %all_to_all.31), calls=%async_computation.5 | async-start | bytes 196608 | tf_op jit(solution)/shard_map/all_to_all | solution.py:549
  657.3 52.5 %collective-permute-start.28 = (bf16[512,512]{1,0:T(8,128)(2,1)}, bf16[512,512]{1,0:T(8,128)(2,1)}, u32[]{:S(2)}, u32[]{:S(2)}) collective-permute-start(bf16[512,512]{1,0:T(8,128)(2,1)} %fusion.54), channel_id=1, source_target_pairs={{0,8},{8,16},{16,24},{24,0},{1,9},{9,17},{17,25},{25,1},{2,10},{10... | collective-permute-start | bytes 1572872 | tf_op jit(solution)/shard_map/ppermute | solution.py:121
  664.4 62.4 %collective-permute-start.35 = (bf16[64,2048]{1,0:T(8,128)(2,1)}, bf16[64,2048]{1,0:T(8,128)(2,1)S(1)}, u32[]{:S(2)}, u32[]{:S(2)}) collective-permute-start(bf16[64,2048]{1,0:T(8,128)(2,1)} %fusion.59), channel_id=1, source_target_pairs={{0,0},{1,4},{2,8},{3,12},{4,16},{5,20},{6,24},{7,28},{8,1},{9,5},{... | collective-permute-start | bytes 786440 | tf_op jit(solution)/shard_map/ppermute | solution.py:514
  676.6 27.4 %collective-permute-start.31 = (bf16[64,2048]{1,0:T(8,128)(2,1)S(1)}, bf16[64,2048]{1,0:T(8,128)(2,1)S(1)}, u32[]{:S(2)}, u32[]{:S(2)}) collective-permute-start(bf16[64,2048]{1,0:T(8,128)(2,1)S(1)} %get-tuple-element.159), channel_id=1, source_target_pairs={{0,24},{8,0},{16,8},{24,16},{1,25},{9,1},{17,9},{25,17},{2,26},{10... | collective-permute-start | bytes 786440 | tf_op jit(solution)/shard_map/ppermute | solution.py:102
  677.9 31.9 %collective-permute-start.30 = (bf16[64,2048]{1,0:T(8,128)(2,1)S(1)}, bf16[64,2048]{1,0:T(8,128)(2,1)S(1)}, u32[]{:S(2)}, u32[]{:S(2)}) collective-permute-start(bf16[64,2048]{1,0:T(8,128)(2,1)S(1)} %get-tuple-element.160), channel_id=1, source_target_pairs={{0,16},{8,24},{16,0},{24,8},{1,17},{9,25},{17,1},{25,9},{2,18},{10... | collective-permute-start | bytes 786440 | tf_op jit(solution)/shard_map/ppermute | solution.py:102
  (102 other events, 1862.6 us)
Sparse Core Ops, SparseCore 0:
  9.9 74.5 all-gather.6
  94.9 68.7 all-gather.8
  204.0 60.5 all-gather.10
  266.3 54.2 all-gather.12
  329.2 55.8 all-gather.14
  388.4 70.8 reduce-scatter.2
  504.7 67.6 all-gather.16
  577.1 77.9 reduce-scatter.4
